TPU v7x, 32 devices: a whole 2x2x4 slice. The times are simulated.
32 devices in a mesh: dp: 8 (over z, x), row: 2 (over y), col: 2 (over core).
Axes of the slice: x: 2, y: 2, z: 4, core: 2. Of those that a mesh axis runs over, the one named last changes fastest.
Arguments:
- block_input: float32 [4096, 640], P(('dp', 'col'), 'row'), may hold values from -200 to 200
- segment_ids: int32 [16, 256], P(('dp', 'row')), may hold values from 0 to 3, never falling along the last dimension, each value on 1 to 128 neighbouring positions
- w_query: bfloat16 [640, 1024], P('row', 'col'), may hold values from -0.25 to 0.25
- w_key: bfloat16 [640, 256], P('row'), may hold values from -0.25 to 0.25
- w_value: bfloat16 [640, 256], P('row'), may hold values from -0.25 to 0.25
- w_out: bfloat16 [1024, 640], P('col', 'row'), may hold values from -0.1875 to 0.1875
- w_gate: bfloat16 [640, 2048], P('row', 'col'), may hold values from -0.25 to 0.25
- w_up: bfloat16 [640, 2048], P('row', 'col'), may hold values from -0.25 to 0.25
- w_down: bfloat16 [2048, 640], P('col', 'row'), may hold values from -0.125 to 0.125
- gain_input: float32 [640], P('row'), may hold values from 0.25 to 1.75
- gain_attn: float32 [640], P('row'), may hold values from 0.25 to 1.75
- gain_ffn_pre: float32 [640], P('row'), may hold values from 0.25 to 1.75
- gain_ffn_post: float32 [640], P('row'), may hold values from 0.25 to 1.75
- gain_query: float32 [256], replicated, may hold values from 0.25 to 1.75
- gain_key: float32 [256], replicated, may hold values from 0.25 to 1.75
- out_cotangent: float32 [4096, 640], P(('dp', 'col'), 'row'), may hold values from -6 to 6
Outputs:
- block_output: float32 [4096, 640], P(('dp', 'col'), 'row')
- input_grad: float32 [4096, 640], P(('dp', 'col'), 'row')
- query_grad: float32 [640, 1024], P('row', 'col')
- key_grad: float32 [640, 256], P('row')
- value_grad: float32 [640, 256], P('row')
- out_grad: float32 [1024, 640], P('col', 'row')
- gate_grad: float32 [640, 2048], P('row', 'col')
- up_grad: float32 [640, 2048], P('row', 'col')
- down_grad: float32 [2048, 640], P('col', 'row')
- gain_input_grad: float32 [640], P('row')
- gain_attn_grad: float32 [640], P('row')
- gain_ffn_pre_grad: float32 [640], P('row')
- gain_ffn_post_grad: float32 [640], P('row')
- gain_query_grad: float32 [256], replicated
- gain_key_grad: float32 [256], replicated
Inputs may be any that keep to these rules, and one draw needn't show every extreme that they name: `segment_ids`: one packed sequence a row; document numbers never fall, start at 0 and take every value up to 3; each document has 1 to 128 tokens and one has exactly 128.
All inputs are finite; a program needn't handle non-finite values.
Results may differ from a plain program's by a relative error of at most 0.014.
Values may be sent and summed in bfloat16 or wider, within the bound.
No kernel may reach another device: no remote copies, remote signals or barrier semaphores. Data moves between devices by JAX's collectives and lax.ppermute only.
A program may use at most 64 MiB of HBM per device.

v0:
```python
import jax
import jax.numpy as jnp
from jax import lax
from jax.experimental import pallas as pl
from jax.experimental.pallas import tpu as pltpu
from jax.sharding import PartitionSpec as P

eps_norm = 1e-06
rope_base = 1000000.0
bf16 = jnp.bfloat16
f32 = jnp.float32
gelu_c = (2.0 / 3.141592653589793) ** 0.5
gelu_a = 0.044715


PLAN = {
    "down": ("y", 1, 2, 4),
    "gate": (2, "y", 1, 4),
    "up": (1, "y", 2, 4),
    "attn": (2, "y", 1, 4),
}
GATHER = {"down": (4, 2, 1), "gate": (4, 2, 1), "up": (4, 2, 1), "attn": (4, 1, 2)}
TOP_BITS = (1, 2, 4)


def dot(left, right, contract=((1,), (0,))):
    return lax.dot_general(left, right, (contract, ((), ())), preferred_element_type=f32)


def rms_scale(values):
    return lax.rsqrt(jnp.mean(values * values, axis=-1, keepdims=True) + eps_norm)


def norm_back(upstream, values, inv_rms, gain_vector):
    weighted = upstream * gain_vector
    width_sum = jnp.sum(weighted * values, axis=1, keepdims=True)
    through = inv_rms * weighted - values * (inv_rms**3 * width_sum / values.shape[1])
    return through, jnp.sum(upstream * values * inv_rms, axis=0, keepdims=True)


def rotate(values, cosine_table, sine_table):
    half = values.shape[1] // 2
    a, b = values[:, :half], values[:, half:]
    return jnp.concatenate(
        [a * cosine_table - b * sine_table, b * cosine_table + a * sine_table], axis=1
    )


def rotate_back(values, cosine_table, sine_table):
    return rotate(values, cosine_table, -sine_table)


def gelu_parts(v):
    t = jnp.tanh(gelu_c * (v + gelu_a * v * v * v))
    return t, 0.5 * v * (1.0 + t)


def call(body, outs, *args, scalars=None, scratch=(), out_hbm=False, limit=24):
    in_specs = [pl.BlockSpec(memory_space=pltpu.VMEM) for _ in args]
    args = tuple(pltpu.with_memory_space_constraint(v, pltpu.VMEM) for v in args)
    if scalars is not None:
        in_specs = [pl.BlockSpec(memory_space=pltpu.SMEM)] + in_specs
        args = (scalars,) + args
    place = jax.ShapeDtypeStruct if out_hbm else pltpu.VMEM
    return pl.pallas_call(
        body,
        in_specs=in_specs,
        out_specs=[pl.BlockSpec(memory_space=pltpu.VMEM) for _ in outs],
        out_shape=[place(s, d) for s, d in outs],
        scratch_shapes=list(scratch),
        compiler_params=pltpu.CompilerParams(vmem_limit_bytes=limit << 20),
    )(*args)


def join_rows(scr, own, other):
    half = own.shape[0]
    scr[:half, :] = own[...]
    scr[half:, :] = other[...]


def place_rows(scr, sc, pieces, first_bit):
    own, near, first, second = pieces
    half, q = own.shape[0], near.shape[0]
    scr[:half, :] = own[...]
    b1, b2 = sc[1], sc[2]

    def at(r1, r2):
        p1 = 1 - b1 if r1 else b1
        p2 = 1 - b2 if r2 else b2
        return pl.ds(pl.multiple_of(half + q * (2 * p2 + p1), 16), q)

    scr[at(0, 0), :] = near[...]
    scr[at(1, 0) if first_bit == 1 else at(0, 1), :] = first[...]
    scr[at(0, 1) if first_bit == 1 else at(1, 0), :] = second[:q, :]
    scr[at(1, 1), :] = second[q:, :]


def sequence_t(sc, local, own_recv, diag_recv, other_recv):
    diag = sc[3] == 1
    own = jnp.where(diag, local[...], own_recv[...].astype(f32))
    other = jnp.where(diag, diag_recv[...].astype(f32), other_recv[...].astype(f32))
    return jnp.concatenate([own, other], axis=0).T


def proj_body(sc, x_local, x_own, x_diag, x_other, g, w_own, w_other, x, normed, raw_q, kv, w):
    join_rows(w, w_own, w_other)
    v = sequence_t(sc, x_local, x_own, x_diag, x_other)
    x[...] = v
    n = (v * rms_scale(v) * g[0:1, :]).astype(bf16)
    normed[...] = n
    p = dot(n, w[...])
    qw = raw_q.shape[1]
    raw_q[...] = p[:, :qw]
    kv[...] = p[:, qw:]


def cot_body(sc, c_local, c_own, c_diag, c_other, cot):
    cot[...] = sequence_t(sc, c_local, c_own, c_diag, c_other)


def attn_body(sc, raw_q, kv_mine, kv_theirs, mask, cos, sin, gq, gk, w_own, w_other, q, k, v,
              probs, heads, part, send, w):
    join_rows(w, w_own, w_other)
    first = sc[0] == 1
    c, s = cos[...], sin[...]
    hd = k.shape[1]
    raw_k = jnp.where(first, kv_mine[...], kv_theirs[...])
    raw_v = jnp.where(first, kv_theirs[...], kv_mine[...])
    key = rotate(raw_k * rms_scale(raw_k) * gk[...], c, s).astype(bf16)
    value = raw_v.astype(bf16)
    k[...] = key
    v[...] = value
    allowed = mask[...] > 0.0
    for h in range(q.shape[1] // hd):
        raw = raw_q[:, h * hd : (h + 1) * hd]
        query = rotate(raw * rms_scale(raw) * gq[...], c, s).astype(bf16)
        q[:, h * hd : (h + 1) * hd] = query
        logits = dot(query, key, ((1,), (1,))) * (hd**-0.5)
        weights = jnp.where(allowed, jnp.exp(logits), 0.0)
        p = weights / jnp.sum(weights, axis=1, keepdims=True)
        probs[h] = p
        heads[:, h * hd : (h + 1) * hd] = dot(p.astype(bf16), value).astype(bf16)
    out = dot(heads[...], w[...], ((1,), (1,)))
    part[...] = out
    send[...] = out.astype(bf16)


def mix_body(sc, x, own, recv, g, *refs):
    wg_p, wu_p = refs[0:4], refs[4:8]
    proj, mid, ffn_in, gate, up, hidden, wg, wu = refs[8:]
    place_rows(wg, sc, wg_p, 1)
    place_rows(wu, sc, wu_p, 2)
    y = own[...] + recv[...].astype(f32)
    proj[...] = y
    m = x[...] + y * rms_scale(y) * g[1:2, :]
    mid[...] = m
    n = (m * rms_scale(m) * g[2:3, :]).astype(bf16)
    ffn_in[...] = n
    ga = dot(n, wg[...])
    gate[...] = ga
    u = dot(n, wu[...])
    up[...] = u
    hidden[...] = (gelu_parts(ga)[1] * u).astype(bf16)


def down_body(sc, hidden, *refs):
    wd_p = refs[0:4]
    part, send, wd = refs[4:]
    place_rows(wd, sc, wd_p, 1)
    out = dot(hidden[...], wd[...], ((1,), (1,)))
    part[...] = out
    send[...] = out.astype(bf16)


def split_axis(sc, src, blocks, rows, left, d, emit):
    if d == "y":
        emit(0, 0, src(0, 0, rows), src(1, 0, rows))
        return
    groups = 1 << left.index(d)
    size = rows // groups
    half = size // 2
    b = sc[{1: 1, 2: 2, 4: 4}[d]]
    for block in range(blocks):
        for i in range(groups):
            mine = pl.multiple_of(i * size + b * half, 8)
            theirs = pl.multiple_of(i * size + (1 - b) * half, 8)
            emit(block, i * half, src(block, mine, half), src(block, theirs, half))


def split_grad(sc, left_t, right, send, keep, acc, d, col=0):
    g = dot(left_t, right)
    n = g.shape[1]
    cols = slice(col, col + n)
    half = g.shape[0] // 2
    if d == "y":
        send[0, :, cols] = g[half:].astype(bf16)
        keep[0, :, cols] = g[:half]
        return
    acc[0, :, cols] = g[:half]
    acc[1, :, cols] = g[half:]

    def emit(block, at, mine, theirs):
        rows = slice(at, at + mine.shape[0])
        send[block, rows, cols] = theirs.astype(bf16)
        keep[block, rows, cols] = mine

    split_axis(
        sc, lambda block, start, size: acc[block, pl.ds(start, size), cols], 2, half, TOP_BITS,
        d, emit,
    )


def stage_shapes(blocks, rows, n, d):
    if d == "y":
        return (1, rows, n)
    return (blocks, rows // 2, n)


def stage_body(d, left):
    def body(sc, keep_in, recv, send, keep, acc):
        blocks, rows, _ = keep_in.shape
        for block in range(blocks):
            acc[block] = keep_in[block] + recv[block].astype(f32)

        def emit(block, at, mine, theirs):
            span = slice(at, at + mine.shape[0])
            send[block, span, :] = theirs.astype(bf16)
            keep[block, span, :] = mine

        split_axis(
            sc, lambda block, start, size: acc[block, pl.ds(start, size), :], blocks, rows, left,
            d, emit,
        )

    return body


def last_sum_body(keep_in, recv, send):
    send[...] = (keep_in[...] + recv[...].astype(f32)).astype(bf16)


def assemble_body(order, widths):
    def body(sc, near, far, *outs):
        rows = near.shape[1]
        for part, ref in ((0, near), (1, far)):
            for j in range(4):
                rel = {order[0]: j & 1, order[1]: j >> 1, order[2]: part}
                pos = 0
                for bit in TOP_BITS:
                    b = sc[bit]
                    pos = 2 * pos + (1 - b if rel[bit] else b)
                at = pl.ds(pl.multiple_of(pos * rows, 8), rows)
                val = ref[j].astype(f32)
                col = 0
                for out, w in zip(outs, widths):
                    out[at, :] = val[:, col : col + w].astype(out.dtype)
                    col += w

    return body


def down_grad_body(sc, mid, own, recv, cot, g, hidden, out, out_send, grad_ffn, gain_part, send,
                   keep):
    f = own[...] + recv[...].astype(f32)
    s = rms_scale(f)
    full = (mid[...] + f * s * g[3:4, :]).T
    half = full.shape[0] // 2
    out[...] = full[:half]
    out_send[...] = full[half:].astype(bf16)
    through, part = norm_back(cot[...], f, s, g[3:4, :])
    gain_part[...] = part
    gf = through.astype(bf16)
    grad_ffn[...] = gf
    split_grad(sc, gf.T, hidden[...], send, keep, None, PLAN["down"][0])


def mix_grad_body(sc, grad_ffn, gate, up, ffn_in, *refs):
    wg_p, wu_p, wd_p = refs[0:4], refs[4:8], refs[8:12]
    s_gate, k_gate, s_up, k_up, part, send, wg, wu, wd, acc = refs[12:]
    place_rows(wd, sc, wd_p, 1)
    place_rows(wg, sc, wg_p, 1)
    place_rows(wu, sc, wu_p, 2)
    gh = dot(grad_ffn[...], wd[...])
    v = gate[...]
    t, gelu = gelu_parts(v)
    slope = 0.5 * (1.0 + t) + 0.5 * v * (1.0 - t * t) * (gelu_c * (1.0 + 3.0 * gelu_a * v * v))
    gg = (gh * up[...] * slope).astype(bf16)
    gu = (gh * gelu).astype(bf16)
    n_t = ffn_in[...].T
    split_grad(sc, n_t, gg, s_gate, k_gate, acc, PLAN["gate"][0])
    split_grad(sc, n_t, gu, s_up, k_up, acc, PLAN["up"][0])
    out = dot(gg, wg[...], ((1,), (1,))) + dot(gu, wu[...], ((1,), (1,)))
    part[...] = out
    send[...] = out.astype(bf16)


def attn_grad_body(sc, own, recv, mid, proj, cot, g, w_own, w_other, q, k, v, probs, raw_q, cos,
                   sin, gq, grad_mid, grad_attn, pre_part, attn_part, kv_own, kv_send, grad_q,
                   q_part, w):
    join_rows(w, w_own, w_other)
    up = own[...] + recv[...].astype(f32)
    m = mid[...]
    through, part = norm_back(up, m, rms_scale(m), g[2:3, :])
    pre_part[...] = part
    gm = cot[...] + through
    grad_mid[...] = gm
    y = proj[...]
    through, part = norm_back(gm, y, rms_scale(y), g[1:2, :])
    attn_part[...] = part
    ga = through.astype(bf16)
    grad_attn[...] = ga
    grad_heads = dot(ga, w[...]).astype(bf16)
    hd = k.shape[1]
    c, s = cos[...], sin[...]
    key, value = k[...], v[...]
    value_part, key_part, gain_part = 0.0, 0.0, 0.0
    scale = hd**-0.5
    for h in range(q.shape[1] // hd):
        cols = slice(h * hd, (h + 1) * hd)
        gh = grad_heads[:, cols]
        p = probs[h]
        value_part = value_part + dot(p.astype(bf16).T, gh)
        gp = dot(gh, value, ((1,), (1,)))
        delta = jnp.sum(p * gp, axis=1, keepdims=True)
        gs = (p * (gp - delta)).astype(bf16)
        gq_rot = dot(gs, key) * scale
        key_part = key_part + dot(gs.T, q[:, cols]) * scale
        raw = raw_q[:, cols]
        through, part = norm_back(rotate_back(gq_rot, c, s), raw, rms_scale(raw), gq[...])
        grad_q[:, cols] = through.astype(bf16)
        gain_part = gain_part + part
    q_part[...] = gain_part
    first = sc[0] == 1
    kv_own[...] = jnp.where(first, key_part, value_part)
    kv_send[...] = jnp.where(first, value_part, key_part)


def joint_body(sc, kv_own, kv_recv, kv_raw, cos, sin, gk, grad_q, normed, grad_attn, heads,
               w_own, w_other, k_part, send, keep, part, part_send, w, acc):
    join_rows(w, w_own, w_other)
    total = kv_own[...] + kv_recv[...]
    raw = kv_raw[...]
    through, gain_part = norm_back(
        rotate_back(total, cos[...], sin[...]), raw, rms_scale(raw), gk[...]
    )
    first = sc[0] == 1
    k_part[...] = jnp.where(first, gain_part, 0.0)
    kvg = jnp.where(first, through, total).astype(bf16)
    gq = grad_q[...]
    qw, kw = gq.shape[1], kvg.shape[1]
    n_t = normed[...].T
    d = PLAN["attn"][0]
    split_grad(sc, n_t, gq, send, keep, acc, d, 0)
    split_grad(sc, n_t, kvg, send, keep, acc, d, qw)
    split_grad(sc, grad_attn[...].T, heads[...], send, keep, acc, d, qw + kw)
    out = dot(gq, w[:, :qw], ((1,), (1,))) + dot(kvg, w[:, qw:], ((1,), (1,)))
    part[...] = out
    part_send[...] = out.astype(bf16)


def input_body(own, recv, x, grad_mid, g, out, out_send, gain_part):
    up = own[...] + recv[...].astype(f32)
    v = x[...]
    through, part = norm_back(up, v, rms_scale(v), g[0:1, :])
    full = (grad_mid[...] + through).T
    half = full.shape[0] // 2
    out[...] = full[:half]
    out_send[...] = full[half:].astype(bf16)
    gain_part[...] = part


def make_step(mesh):
    n_dp, n_row, n_col = mesh.shape["dp"], mesh.shape["row"], mesh.shape["col"]
    assert n_row == 2 and n_col == 2 and n_dp >= 8
    bits = []
    while (1 << len(bits)) < n_dp:
        bits.append(1 << len(bits))
    assert (1 << len(bits)) == n_dp
    extra = tuple(b for b in bits if b > 4)

    def swap_row(v):
        return lax.ppermute(v, "row", [(0, 1), (1, 0)])

    def swap_col(v):
        return lax.ppermute(v, "col", [(0, 1), (1, 0)])

    def swap_dp(v, bit):
        return lax.ppermute(v, "dp", [(i, i ^ bit) for i in range(n_dp)])

    def step(
        block_input, segment_ids, w_query, w_key, w_value, w_out, w_gate, w_up, w_down,
        gain_input, gain_attn, gain_ffn_pre, gain_ffn_post, gain_query, gain_key, out_cotangent,
    ):
        rows, half_width = block_input.shape
        width = 2 * half_width
        hd = w_key.shape[1]
        qw = w_query.shape[1]
        n_head = qw // hd
        ff = w_gate.shape[1]
        row = lax.axis_index("row")
        col = lax.axis_index("col")
        dp = lax.axis_index("dp")
        diag = row == col
        first_col = col == 0

        def bit_of(bit):
            return (dp // bit) % 2

        code = (1 - col) + 2 * bit_of(1) + 4 * bit_of(2) + 8 * (row == col) + 16 * bit_of(4)
        sc = (code >> jnp.arange(8, dtype=jnp.int32)) & 1

        def off_to_diag(v):
            return lax.ppermute(v, ("row", "col"), [(1, 3), (2, 0)])

        def diag_to_off_col(v):
            return lax.ppermute(v, ("row", "col"), [(0, 1), (3, 2)])

        def diag_to_off_row(v):
            return lax.ppermute(v, ("row", "col"), [(0, 2), (3, 1)])

        def chip_sequence(local, kind):
            local_t = local.T
            narrow = local_t.astype(kind)
            from_row = off_to_diag(narrow)
            return local_t, diag_to_off_col(narrow), from_row, diag_to_off_col(from_row)

        def with_other_rows(own, first_bit, second_bit):
            q = own.shape[0] // 4
            at = (2 * bit_of(2) + bit_of(1)) * q
            near = swap_row(lax.dynamic_slice_in_dim(own, at, q, 0))
            first = swap_dp(near, first_bit)
            second = swap_dp(jnp.concatenate([near, first], axis=0), second_bit)
            return own, near, first, second

        x_pieces = chip_sequence(block_input, f32)
        joint_own = jnp.concatenate([w_query, jnp.where(first_col, w_key, w_value)], axis=1)
        w_joint = (joint_own, swap_row(joint_own))
        which = lax.broadcasted_iota(jnp.int32, (4, half_width), 0)
        gains_own = jnp.where(
            which == 0, gain_input,
            jnp.where(which == 1, gain_attn, jnp.where(which == 2, gain_ffn_pre, gain_ffn_post)),
        )
        gains = jnp.concatenate([gains_own, swap_row(gains_own)], axis=1)
        wg = with_other_rows(w_gate, 1, 2)
        wu = with_other_rows(w_up, 2, 1)
        out_own = w_out.T
        wo = (out_own, swap_row(out_own))
        wd = with_other_rows(w_down.T, 1, 2)
        cot_pieces = chip_sequence(out_cotangent, bf16)

        segments = segment_ids[0]
        places = jnp.arange(rows, dtype=jnp.int32)
        allowed = (segments[:, None] == segments[None, :]) & (places[:, None] >= places[None, :])
        mask = allowed.astype(f32)
        offsets = jnp.sum(mask, axis=1) - 1.0
        frequency = rope_base ** (-(jnp.arange(hd // 2, dtype=f32) * 2.0 / hd))
        angles = offsets[:, None] * frequency
        cos, sin = jnp.cos(angles), jnp.sin(angles)
        gq, gk = gain_query[None], gain_key[None]

        t = rows
        joint_width = qw + hd
        wide_f, wide_b = ((t, width), f32), ((t, width), bf16)
        ffn_scratch = [pltpu.VMEM((width, ff), bf16) for _ in range(3)]
        x, normed, raw_q, kv_mine = call(
            proj_body, [wide_f, wide_b, ((t, qw), f32), ((t, hd), f32)],
            *x_pieces, gains, *w_joint, scalars=sc,
            scratch=[pltpu.VMEM((width, joint_width), bf16)],
        )
        kv_theirs = swap_col(kv_mine)
        q, k, v, probs, heads, part, send = call(
            attn_body,
            [((t, qw), bf16), ((t, hd), bf16), ((t, hd), bf16), ((n_head, t, t), f32),
             ((t, qw), bf16), wide_f, wide_b],
            raw_q, kv_mine, kv_theirs, mask, cos, sin, gq, gk, *wo, scalars=sc,
            scratch=[pltpu.VMEM((width, qw), bf16)],
        )
        (cotangent,) = call(cot_body, [wide_f], *cot_pieces, scalars=sc)
        proj, mid, ffn_in, gate, up, hidden = call(
            mix_body,
            [wide_f, wide_f, wide_b, ((t, ff), f32), ((t, ff), f32), ((t, ff), bf16)],
            x, part, swap_col(send), gains, *wg, *wu, scalars=sc,
            scratch=ffn_scratch[:2],
        )
        part, send = call(
            down_body, [wide_f, wide_b], hidden, *wd, scalars=sc,
            scratch=ffn_scratch[:1],
        )

        def first_shapes(name, n):
            s = stage_shapes(2, half_width, n, PLAN[name][0])
            return [(s, bf16), (s, f32)]

        def swap(v, d):
            return swap_row(v) if d == "y" else swap_dp(v, d)

        def more_bits(cur):
            n = cur.shape[-1]
            for bit in extra:
                size = cur.shape[1] // 2
                halves = cur.reshape(2, size, n).astype(f32)
                b = bit_of(bit)
                sent = lax.dynamic_index_in_dim(halves, 1 - b, 0).astype(bf16)
                got = swap_dp(sent, bit).astype(f32)
                cur = lax.dynamic_index_in_dim(halves, b, 0) + got
            cur = cur.astype(bf16)
            for bit in reversed(extra):
                theirs = swap_dp(cur, bit)
                b = bit_of(bit)
                cur = jnp.concatenate(
                    [jnp.where(b == 0, cur, theirs), jnp.where(b == 0, theirs, cur)], axis=1
                )
            return cur

        def grad_sum(name, send, keep, outs):
            n = keep.shape[-1]
            order = PLAN[name]
            left = list(TOP_BITS)
            if order[0] != "y":
                left.remove(order[0])
            for stage, d in enumerate(order):
                recv = swap(send, d)
                if stage + 1 == len(order):
                    break
                nxt = order[stage + 1]
                blocks, r, _ = keep.shape
                shape = stage_shapes(blocks, r, n, nxt)
                send, keep = call(
                    stage_body(nxt, tuple(left)),
                    [(shape, bf16), (shape, f32)], keep, recv, scalars=sc,
                    scratch=[pltpu.VMEM((blocks, r, n), f32)],
                )
                if nxt != "y":
                    left.remove(nxt)
            (cur,) = call(last_sum_body, [(keep.shape, bf16)], keep, recv)
            if extra:
                cur = more_bits(cur)
            stage = len(order) - 1
            for d in GATHER[name]:
                stage += 1
                theirs = swap_dp(cur, d)
                if d != GATHER[name][-1]:
                    cur = jnp.concatenate([cur, theirs], axis=0)
            return call(
                assemble_body(GATHER[name], [w for w, _ in outs]),
                [((half_width, w), dt) for w, dt in outs], cur, theirs, scalars=sc, out_hbm=True,
            )

        def place_out(own_t, send):
            return jnp.where(diag, own_t, diag_to_off_row(send).astype(f32)).T

        out_pair = [((half_width, t), f32), ((half_width, t), bf16)]
        own_t, out_send, grad_ffn, post_part, s_down, k_down = call(
            down_grad_body,
            out_pair + [wide_b, ((1, width), f32)] + first_shapes("down", ff),
            mid, part, swap_col(send), cotangent, gains, hidden, scalars=sc,
        )
        block_output = place_out(own_t, out_send)
        (down_sum,) = grad_sum("down", s_down, k_down, [(ff, f32)])
        s_gate, k_gate, s_up, k_up, part, send = call(
            mix_grad_body,
            first_shapes("gate", ff) + first_shapes("up", ff) + [wide_f, wide_b],
            grad_ffn, gate, up, ffn_in, *wg, *wu, *wd, scalars=sc,
            scratch=ffn_scratch + [pltpu.VMEM((2, half_width, ff), f32)],
        )
        (gate_sum,) = grad_sum("gate", s_gate, k_gate, [(ff, f32)])
        (up_sum,) = grad_sum("up", s_up, k_up, [(ff, f32)])
        grad_mid, grad_attn, pre_part, attn_part, kv_own, kv_send, grad_q, q_part = call(
            attn_grad_body,
            [wide_f, wide_b, ((1, width), f32), ((1, width), f32),
             ((t, hd), f32), ((t, hd), f32), ((t, qw), bf16), ((1, hd), f32)],
            part, swap_col(send), mid, proj, cotangent, gains, *wo, q, k, v, probs,
            raw_q, cos, sin, gq, scalars=sc, scratch=[pltpu.VMEM((width, qw), bf16)],
        )
        n_attn = joint_width + qw
        k_part, s_attn, k_attn, part, send = call(
            joint_body,
            [((1, hd), f32)] + first_shapes("attn", n_attn) + [wide_f, wide_b],
            kv_own, swap_col(kv_send), kv_mine, cos, sin, gk, grad_q, normed,
            grad_attn, heads, *w_joint, scalars=sc,
            scratch=[pltpu.VMEM((width, joint_width), bf16),
                     pltpu.VMEM((2, half_width, n_attn), f32)],
        )
        query_sum, kv_sum, out_sum = grad_sum(
            "attn", s_attn, k_attn, [(qw, f32), (hd, bf16), (qw, f32)]
        )
        own_t, out_send, in_part = call(
            input_body, out_pair + [((1, width), f32)],
            part, swap_col(send), x, grad_mid, gains,
        )
        input_grad = place_out(own_t, out_send)
        kv_sum_theirs = swap_col(kv_sum)
        key_sum = jnp.where(first_col, kv_sum, kv_sum_theirs).astype(f32)
        value_sum = jnp.where(first_col, kv_sum_theirs, kv_sum).astype(f32)

        width_parts = jnp.concatenate([in_part, attn_part, pre_part, post_part], axis=0)
        width_parts = jnp.where(diag, width_parts, 0.0)
        ends = [q_part[0], k_part[0]]
        own = jnp.concatenate([width_parts[:, :half_width].reshape(-1)] + ends)
        away = jnp.concatenate([width_parts[:, half_width:].reshape(-1)] + ends)
        small = own + swap_row(away)
        small = small + swap_col(small)
        for bit in bits:
            small = small + swap_dp(small, bit)
        width_sums = small[: 4 * half_width].reshape(4, half_width)
        return (
            block_output, input_grad, query_sum, key_sum, value_sum, out_sum.T,
            gate_sum, up_sum, down_sum.T,
            width_sums[0], width_sums[1], width_sums[2], width_sums[3],
            small[4 * half_width : 4 * half_width + hd], small[4 * half_width + hd :],
        )

    return step


def solution(mesh):
    rows_by_width = P(("dp", "col"), "row")
    in_specs = (
        rows_by_width, P(("dp", "row"), None), P("row", "col"), P("row", None), P("row", None),
        P("col", "row"), P("row", "col"), P("row", "col"), P("col", "row"),
        P("row"), P("row"), P("row"), P("row"), P(), P(), rows_by_width,
    )
    out_specs = (
        rows_by_width, rows_by_width, P("row", "col"), P("row", None), P("row", None),
        P("col", "row"), P("row", "col"), P("row", "col"), P("col", "row"),
        P("row"), P("row"), P("row"), P("row"), P(), P(),
    )
    return jax.shard_map(
        make_step(mesh), mesh=mesh, in_specs=in_specs, out_specs=out_specs, check_vma=False
    )
```

profile of v0, /device:TPU:0, one launch (start us, length us, event | category | flops | bytes accessed | tf_op | source)
XLA Modules:
  0.0 191.1 jit_solution(275773879367819628)
XLA Ops:
  0.7 1.4 collective-permute-start.1
  2.1 6.5 %collective-permute-start = (f32[320,256]{1,0:T(8,128)}, f32[320,256]{1,0:T(8,128)}, u32[]{:S(2)}, u32[]{:S(2)}) collective-permute-start(f32[320,256]{1,0:T(8,128)} %bitcast.25), channel_id=1, source_target_pairs={{0,1},{3,2},{4,5},{7,6},{8,9},{11,10},{12,13},{15,14},{16,17},{19,... | collective-permute-start | bytes 983048 | tf_op jit(solution)/shard_map/ppermute | solution.py:416
  9.5 1.6 constant_dynamic-slice_fusion
  11.1 2.0 %collective-permute-start.11 = (bf16[80,1024]{1,0:T(8,128)(2,1)}, bf16[80,1024]{1,0:T(8,128)(2,1)S(1)}, u32[]{:S(2)}, u32[]{:S(2)}) collective-permute-start(bf16[80,1024]{1,0:T(8,128)(2,1)} %constant_dynamic-slice_fusion), channel_id=1, source_target_pairs={{0,2},{2,0},{1,3},{3,1},{4,6},{6,4},{5,7},{7,5},{8,10},{10,8},{9,1... | collective-permute-start | bytes 491528 | tf_op jit(solution)/shard_map/ppermute | solution.py:382
  16.2 2.0 %collective-permute-start.2 = (f32[320,256]{1,0:T(8,128)}, f32[320,256]{1,0:T(8,128)}, u32[]{:S(2)}, u32[]{:S(2)}) collective-permute-start(f32[320,256]{1,0:T(8,128)} %collective-permute-done.1.x_diag), channel_id=1, source_target_pairs={{0,1},{3,2},{4,5},{7,6},{8,9},{11,10},{12,13},{15,14},{16,17},{19,... | collective-permute-start | bytes 983048 | tf_op jit(solution)/shard_map/ppermute | solution.py:416
  21.6 11.1 %collective-permute-done.8.refs_1_ = bf16[80,1024]{1,0:T(8,128)(2,1)S(1)} collective-permute-done((bf16[80,1024]{1,0:T(8,128)(2,1)}, bf16[80,1024]{1,0:T(8,128)(2,1)S(1)}, u32[]{:S(2)}, u32[]{:S(2)}) %collective-permute-start.8) | collective-permute-done | bytes 163872 | tf_op jit(solution)/shard_map/ppermute | solution.py:382
  34.8 1.5 collective-permute-start.9
  36.3 2.0 %shard_map.271 = (f32[256,640]{1,0:T(8,128)S(1)}, bf16[256,640]{1,0:T(8,128)(2,1)S(1)}, f32[256,512]{1,0:T(8,128)S(1)}, f32[256,256]{1,0:T(8,128)S(1)}) custom-call(s32[8]{0:T(128)S(1)} %shift-right-arithmetic_and_fusion.sc, f32[320,256]{1,0:T(8,128)S(1)} %bitcast.26, f32[320,256]{1,0:T(8,128)} %collective-permute-done.x_own, ...), custom_call_target="tpu_custom_call" | custom-call | tf_op jit(solution)/shard_map/pallas_call | solution.py:65
  39.6 1.6 collective-permute-start.13
  42.0 1.6 shard_map.272
  43.7 2.4 %collective-permute-done.15.refs_2_.refs_10_ = bf16[80,1024]{1,0:T(8,128)(2,1)S(1)} collective-permute-done((bf16[80,1024]{1,0:T(8,128)(2,1)S(1)}, bf16[80,1024]{1,0:T(8,128)(2,1)S(1)}, u32[]{:S(2)}, u32[]{:S(2)}) %collective-permute-start.15) | collective-permute-done | bytes 163872 | tf_op jit(solution)/shard_map/ppermute | solution.py:388
  47.9 4.7 %collective-permute-done.13.refs_7_ = bf16[160,1024]{1,0:T(8,128)(2,1)S(1)} collective-permute-done((bf16[160,1024]{1,0:T(8,128)(2,1)S(1)}, bf16[160,1024]{1,0:T(8,128)(2,1)S(1)}, u32[]{:S(2)}, u32[]{:S(2)}) %collective-permute-start.13) | collective-permute-done | bytes 327712 | tf_op jit(solution)/shard_map/ppermute | solution.py:388
  52.6 2.0 %shard_map.273 = (f32[256,640]{1,0:T(8,128)S(1)}, f32[256,640]{1,0:T(8,128)S(1)}, bf16[256,640]{1,0:T(8,128)(2,1)S(1)}, f32[256,1024]{1,0:T(8,128)S(1)}, f32[256...) custom-call(s32[8]{0:T(128)S(1)} %shift-right-arithmetic_and_fusion.sc, f32[256,640]{1,0:T(8,128)S(1)} %get-tuple-element.89.x, ...), custom_call_target="tpu_custom_call" | custom-call | tf_op jit(solution)/shard_map/pallas_call | solution.py:65
  54.6 3.2 %collective-permute-done.16.refs_3_.refs_11_ = bf16[160,1024]{1,0:T(8,128)(2,1)S(1)} collective-permute-done((bf16[160,1024]{1,0:T(8,128)(2,1)S(1)}, bf16[160,1024]{1,0:T(8,128)(2,1)S(1)}, u32[]{:S(2)}, u32[]{:S(2)}) %collective-permute-start.16) | collective-permute-done | bytes 327712 | tf_op jit(solution)/shard_map/ppermute | solution.py:388
  59.1 2.4 %collective-permute-start.18 = (bf16[320,256]{1,0:T(8,128)(2,1)S(1)}, bf16[320,256]{1,0:T(8,128)(2,1)S(1)}, u32[]{:S(2)}, u32[]{:S(2)}) collective-permute-start(bf16[320,256]{1,0:T(8,128)(2,1)S(1)} %bitcast_convert_fusion), channel_id=1, source_target_pairs={{0,1},{3,2},{4,5},{7,6},{8,9},{11,10},{12,13},{15,14},{16,17},{19,... | collective-permute-start | bytes 491528 | tf_op jit(solution)/shard_map/ppermute | solution.py:416
  61.5 1.5 collective-permute-start.20
  64.6 2.3 %shard_map.276 = (f32[320,256]{1,0:T(8,128)S(1)}, bf16[320,256]{1,0:T(8,128)(2,1)S(1)}, bf16[256,640]{1,0:T(8,128)(2,1)S(1)}, f32[1,640]{1,0:T(1,128)S(1)}, bf16...) custom-call(s32[8]{0:T(128)S(1)} %shift-right-arithmetic_and_fusion.sc, f32[256,640]{1,0:T(8,128)S(1)} %get-tuple-element.94.mid, ...), custom_call_target="tpu_custom_call" | custom-call | tf_op jit(solution)/shard_map/pallas_call | solution.py:65
  68.7 4.4 %shard_map.277 = (bf16[2,160,1024]{2,1,0:T(8,128)(2,1)S(1)}, f32[2,160,1024]{2,1,0:T(8,128)S(1)}, bf16[2,160,1024]{2,1,0:T(8,128)(2,1)}, f32[2,160,1024]{2,1,0:T...) custom-call(s32[8]{0:T(128)S(1)} %shift-right-arithmetic_and_fusion.sc, ...), custom_call_target="tpu_custom_call" | custom-call | tf_op jit(solution)/shard_map/pallas_call | solution.py:65
  74.7 2.6 %shard_map.278 = (f32[256,640]{1,0:T(8,128)S(1)}, bf16[256,640]{1,0:T(8,128)(2,1)S(1)}, f32[1,640]{1,0:T(1,128)S(1)}, f32[1,640]{1,0:T(1,128)S(1)}, f32[256,256]...) custom-call(s32[8]{0:T(128)S(1)} %shift-right-arithmetic_and_fusion.sc, ...), custom_call_target="tpu_custom_call" | custom-call | tf_op jit(solution)/shard_map/pallas_call | solution.py:65
  78.9 2.6 %shard_map.279 = (f32[1,256]{1,0:T(1,128)S(1)}, bf16[2,160,1280]{2,1,0:T(8,128)(2,1)}, f32[2,160,1280]{2,1,0:T(8,128)S(1)}, f32[256,640]{1,0:T(8,128)S(1)}, bf16[256,640]{1,0:T(8,128)(2,1)S(1)}) custom-call(s32[8]{0:T(128)S(1)} %shift-right-arithmetic_and_fusion.sc, f32[256,256]{1,0:T(8,128)S(1)} %get-tuple-element.111.kv_own, ...), custom_call_target="tpu_custom_call" | custom-call | tf_op jit(solution)/shard_map/pallas_call | solution.py:65
  84.1 6.9 %collective-permute-done.34.recv = bf16[2,160,1024]{2,1,0:T(8,128)(2,1)S(1)} collective-permute-done((bf16[2,160,1024]{2,1,0:T(8,128)(2,1)S(1)}, bf16[2,160,1024]{2,1,0:T(8,128)(2,1)S(1)}, u32[]{:S(2)}, u32[]{:S(2)}) %collective-permute-start.34) | collective-permute-done | bytes 655392 | tf_op jit(solution)/shard_map/ppermute | solution.py:388
  96.7 2.3 %collective-permute-done.41.recv = bf16[2,160,1024]{2,1,0:T(8,128)(2,1)} collective-permute-done((bf16[2,160,1024]{2,1,0:T(8,128)(2,1)}, bf16[2,160,1024]{2,1,0:T(8,128)(2,1)}, u32[]{:S(2)}, u32[]{:S(2)}) %collective-permute-start.41) | collective-permute-done | bytes 655392 | tf_op jit(solution)/shard_map/ppermute | solution.py:388
  99.0 1.9 shard_map.291
  103.1 2.2 %shard_map.296 = (bf16[1,160,1024]{2,1,0:T(8,128)(2,1)}, f32[1,160,1024]{2,1,0:T(8,128)S(1)}) custom-call(s32[8]{0:T(128)S(1)} %shift-right-arithmetic_and_fusion.sc, f32[1,320,1024]{2,1,0:T(8,128)S(1)} %copy-done.7, bf16[1,320,1024]{2,1,0:T(8,128)(2,1)} %collective-permute-done.48.recv), custom_call_target="tpu_custom_call" | custom-call | tf_op jit(solution)/shard_map/pallas_call | solution.py:65
  108.7 1.5 collective-permute-start.57
  110.2 5.2 %collective-permute-done.57 = f32[1792]{0:T(1024)S(1)} collective-permute-done((f32[1792]{0:T(1024)S(1)}, f32[1792]{0:T(1024)S(1)}, u32[]{:S(2)}, u32[]{:S(2)}) %collective-permute-start.57) | collective-permute-done | bytes 7200 | tf_op jit(solution)/shard_map/ppermute | solution.py:388
  118.3 2.8 %collective-permute-start.21 = (bf16[320,256]{1,0:T(8,128)(2,1)}, bf16[320,256]{1,0:T(8,128)(2,1)S(1)}, u32[]{:S(2)}, u32[]{:S(2)}) collective-permute-start(bf16[320,256]{1,0:T(8,128)(2,1)} %copy-done.24), channel_id=1, source_target_pairs={{0,2},{3,1},{4,6},{7,5},{8,10},{11,9},{12,14},{15,13},{16,18},{19,... | collective-permute-start | bytes 491528 | tf_op jit(solution)/shard_map/ppermute | solution.py:419
  122.6 2.7 %collective-permute-start.59 = (f32[1792]{0:T(1024)S(1)}, f32[1792]{0:T(1024)S(1)}, u32[]{:S(2)}, u32[]{:S(2)}) collective-permute-start(f32[1792]{0:T(1024)S(1)} %add.73), channel_id=1, source_target_pairs={{0,16},{4,20},{8,24},{12,28},{16,0},{20,4},{24,8},{28,12},{1,17},{... | collective-permute-start | bytes 21512 | tf_op jit(solution)/shard_map/ppermute | solution.py:388
  131.0 4.1 %collective-permute-start.25 = (bf16[320,256]{1,0:T(8,128)(2,1)S(1)}, bf16[320,256]{1,0:T(8,128)(2,1)S(1)}, u32[]{:S(2)}, u32[]{:S(2)}) collective-permute-start(bf16[320,256]{1,0:T(8,128)(2,1)S(1)} %get-tuple-element.121), channel_id=1, source_target_pairs={{0,2},{3,1},{4,6},{7,5},{8,10},{11,9},{12,14},{15,13},{16,18},{19,... | collective-permute-start | bytes 491528 | tf_op jit(solution)/shard_map/ppermute | solution.py:419
  135.7 2.7 %collective-permute-start.44 = (bf16[1,40,1024]{2,1,0:T(8,128)(2,1)S(1)}, bf16[1,40,1024]{2,1,0:T(8,128)(2,1)S(1)}, u32[]{:S(2)}, u32[]{:S(2)}) collective-permute-start(bf16[1,40,1024]{2,1,0:T(8,128)(2,1)S(1)} %get-tuple-element.148), channel_id=1, source_target_pairs={{0,16},{4,20},{8,24},{12,28},{16,0},{20,4},{24,8},{28,12},{1,17},{... | collective-permute-start | bytes 245768 | tf_op jit(solution)/shard_map/ppermute | solution.py:388
  139.4 2.7 %collective-permute-start.38 = (bf16[1,40,1024]{2,1,0:T(8,128)(2,1)S(1)}, bf16[1,40,1024]{2,1,0:T(8,128)(2,1)S(1)}, u32[]{:S(2)}, u32[]{:S(2)}) collective-permute-start(bf16[1,40,1024]{2,1,0:T(8,128)(2,1)S(1)} %shard_map.289), channel_id=1, source_target_pairs={{0,16},{4,20},{8,24},{12,28},{16,0},{20,4},{24,8},{28,12},{1,17},{... | collective-permute-start | bytes 245768 | tf_op jit(solution)/shard_map/ppermute | solution.py:388
  142.7 1.6 collective-permute-start.28
  145.3 4.0 %collective-permute-done.51.recv = bf16[1,40,1024]{2,1,0:T(8,128)(2,1)S(1)} collective-permute-done((bf16[1,40,1024]{2,1,0:T(8,128)(2,1)S(1)}, bf16[1,40,1024]{2,1,0:T(8,128)(2,1)S(1)}, u32[]{:S(2)}, u32[]{:S(2)}) %collective-permute-start.51) | collective-permute-done | bytes 81952 | tf_op jit(solution)/shard_map/ppermute | solution.py:388
  150.1 3.0 %collective-permute-start.29 = (bf16[1,40,1280]{2,1,0:T(8,128)(2,1)S(1)}, bf16[1,40,1280]{2,1,0:T(8,128)(2,1)S(1)}, u32[]{:S(2)}, u32[]{:S(2)}) collective-permute-start(bf16[1,40,1280]{2,1,0:T(8,128)(2,1)S(1)} %get-tuple-element.129), channel_id=1, source_target_pairs={{0,16},{4,20},{8,24},{12,28},{16,0},{20,4},{24,8},{28,12},{1,17},{... | collective-permute-start | bytes 307208 | tf_op jit(solution)/shard_map/ppermute | solution.py:388
  153.1 1.8 collective-permute-start.39
  154.9 1.9 collective-permute-done.29.recv
  156.8 3.0 %collective-permute-start.30 = (bf16[1,40,1280]{2,1,0:T(8,128)(2,1)S(1)}, bf16[1,40,1280]{2,1,0:T(8,128)(2,1)S(1)}, u32[]{:S(2)}, u32[]{:S(2)}) collective-permute-start(bf16[1,40,1280]{2,1,0:T(8,128)(2,1)S(1)} %shard_map.284), channel_id=1, source_target_pairs={{0,16},{4,20},{8,24},{12,28},{16,0},{20,4},{24,8},{28,12},{1,17},{... | collective-permute-start | bytes 307208 | tf_op jit(solution)/shard_map/ppermute | solution.py:388
  159.9 4.0 %collective-permute-start.46 = (bf16[2,40,1024]{2,1,0:T(8,128)(2,1)S(1)}, bf16[2,40,1024]{2,1,0:T(8,128)(2,1)S(1)}, u32[]{:S(2)}, u32[]{:S(2)}) collective-permute-start(bf16[2,40,1024]{2,1,0:T(8,128)(2,1)S(1)} %pad_maximum_fusion.10), channel_id=1, source_target_pairs={{0,8},{4,12},{8,0},{12,4},{16,24},{20,28},{24,16},{28,20},{1,9},{5... | collective-permute-start | bytes 491528 | tf_op jit(solution)/shard_map/ppermute | solution.py:388
  164.5 3.8 %collective-permute-start.53 = (bf16[2,40,1024]{2,1,0:T(8,128)(2,1)S(1)}, bf16[2,40,1024]{2,1,0:T(8,128)(2,1)S(1)}, u32[]{:S(2)}, u32[]{:S(2)}) collective-permute-start(bf16[2,40,1024]{2,1,0:T(8,128)(2,1)S(1)} %pad_maximum_fusion.11), channel_id=1, source_target_pairs={{0,8},{4,12},{8,0},{12,4},{16,24},{20,28},{24,16},{28,20},{1,9},{5... | collective-permute-start | bytes 491528 | tf_op jit(solution)/shard_map/ppermute | solution.py:388
  168.3 2.1 %collective-permute-start.40 = (bf16[4,40,1024]{2,1,0:T(8,128)(2,1)S(1)}, bf16[4,40,1024]{2,1,0:T(8,128)(2,1)S(1)}, u32[]{:S(2)}, u32[]{:S(2)}) collective-permute-start(bf16[4,40,1024]{2,1,0:T(8,128)(2,1)S(1)} %pad_maximum_fusion.5.near), channel_id=1, source_target_pairs={{0,4},{4,0},{8,12},{12,8},{16,20},{20,16},{24,28},{28,24},{1,5},{5... | collective-permute-start | bytes 983048 | tf_op jit(solution)/shard_map/ppermute | solution.py:388
  170.3 1.6 collective-permute-done.31
  172.0 4.2 %collective-permute-start.32 = (bf16[4,40,1280]{2,1,0:T(8,128)(2,1)S(1)}, bf16[4,40,1280]{2,1,0:T(8,128)(2,1)S(1)}, u32[]{:S(2)}, u32[]{:S(2)}) collective-permute-start(bf16[4,40,1280]{2,1,0:T(8,128)(2,1)S(1)} %pad_maximum_fusion.1.near), channel_id=1, source_target_pairs={{0,8},{4,12},{8,0},{12,4},{16,24},{20,28},{24,16},{28,20},{1,9},{5... | collective-permute-start | bytes 1228808 | tf_op jit(solution)/shard_map/ppermute | solution.py:388
  176.3 2.1 %collective-permute-start.54 = (bf16[4,40,1024]{2,1,0:T(8,128)(2,1)S(1)}, bf16[4,40,1024]{2,1,0:T(8,128)(2,1)S(1)}, u32[]{:S(2)}, u32[]{:S(2)}) collective-permute-start(bf16[4,40,1024]{2,1,0:T(8,128)(2,1)S(1)} %pad_maximum_fusion.7.near), channel_id=1, source_target_pairs={{0,4},{4,0},{8,12},{12,8},{16,20},{20,16},{24,28},{28,24},{1,5},{5... | collective-permute-start | bytes 983048 | tf_op jit(solution)/shard_map/ppermute | solution.py:388
  179.0 3.1 %collective-permute-done.32.far = bf16[4,40,1280]{2,1,0:T(8,128)(2,1)S(1)} collective-permute-done((bf16[4,40,1280]{2,1,0:T(8,128)(2,1)S(1)}, bf16[4,40,1280]{2,1,0:T(8,128)(2,1)S(1)}, u32[]{:S(2)}, u32[]{:S(2)}) %collective-permute-start.32) | collective-permute-done | bytes 409632 | tf_op jit(solution)/shard_map/ppermute | solution.py:388
  182.1 1.7 shard_map.285
  184.6 1.7 shard_map.290
  186.2 1.7 shard_map.295
  188.6 1.7 shard_map.300
  (198 shorter events, 53.0 us)
Async XLA Ops:
  0.7 15.6 %collective-permute-start.1 = (f32[320,256]{1,0:T(8,128)}, f32[320,256]{1,0:T(8,128)}, u32[]{:S(2)}, u32[]{:S(2)}) collective-permute-start(f32[320,256]{1,0:T(8,128)} %bitcast.24), channel_id=1, source_target_pairs={{1,3},{2,0},{5,7},{6,4},{9,11},{10,8},{13,15},{14,12},{17,19},{18,... | collective-permute-start | bytes 983048 | tf_op jit(solution)/shard_map/ppermute | solution.py:413
  2.1 31.7 %collective-permute-start = (f32[320,256]{1,0:T(8,128)}, f32[320,256]{1,0:T(8,128)}, u32[]{:S(2)}, u32[]{:S(2)}) collective-permute-start(f32[320,256]{1,0:T(8,128)} %bitcast.25), channel_id=1, source_target_pairs={{0,1},{3,2},{4,5},{7,6},{8,9},{11,10},{12,13},{15,14},{16,17},{19,... | collective-permute-start | bytes 983048 | tf_op jit(solution)/shard_map/ppermute | solution.py:416
  9.4 9.3 %collective-permute-start.3 = (f32[4,320]{1,0:T(4,128)S(1)}, f32[4,320]{1,0:T(4,128)}, u32[]{:S(2)}, u32[]{:S(2)}) collective-permute-start(f32[4,320]{1,0:T(4,128)S(1)} %select_select_fusion), channel_id=1, source_target_pairs={{0,2},{2,0},{1,3},{3,1},{4,6},{6,4},{5,7},{7,5},{8,10},{10,8},{9,1... | collective-permute-start | bytes 15368 | tf_op jit(solution)/shard_map/ppermute | solution.py:382
  11.1 9.6 %collective-permute-start.11 = (bf16[80,1024]{1,0:T(8,128)(2,1)}, bf16[80,1024]{1,0:T(8,128)(2,1)S(1)}, u32[]{:S(2)}, u32[]{:S(2)}) collective-permute-start(bf16[80,1024]{1,0:T(8,128)(2,1)} %constant_dynamic-slice_fusion), channel_id=1, source_target_pairs={{0,2},{2,0},{1,3},{3,1},{4,6},{6,4},{5,7},{7,5},{8,10},{10,8},{9,1... | collective-permute-start | bytes 491528 | tf_op jit(solution)/shard_map/ppermute | solution.py:382
  15.0 19.8 %collective-permute-start.4 = (bf16[320,768]{1,0:T(8,128)(2,1)S(1)}, bf16[320,768]{1,0:T(8,128)(2,1)S(1)}, u32[]{:S(2)}, u32[]{:S(2)}) collective-permute-start(bf16[320,768]{1,0:T(8,128)(2,1)S(1)} %pad_maximum_fusion.w_own), channel_id=1, source_target_pairs={{0,2},{2,0},{1,3},{3,1},{4,6},{6,4},{5,7},{7,5},{8,10},{10,8},{9,1... | collective-permute-start | bytes 1474568 | tf_op jit(solution)/shard_map/ppermute | solution.py:382
  16.2 20.1 %collective-permute-start.2 = (f32[320,256]{1,0:T(8,128)}, f32[320,256]{1,0:T(8,128)}, u32[]{:S(2)}, u32[]{:S(2)}) collective-permute-start(f32[320,256]{1,0:T(8,128)} %collective-permute-done.1.x_diag), channel_id=1, source_target_pairs={{0,1},{3,2},{4,5},{7,6},{8,9},{11,10},{12,13},{15,14},{16,17},{19,... | collective-permute-start | bytes 983048 | tf_op jit(solution)/shard_map/ppermute | solution.py:416
  18.8 13.9 %collective-permute-start.8 = (bf16[80,1024]{1,0:T(8,128)(2,1)}, bf16[80,1024]{1,0:T(8,128)(2,1)S(1)}, u32[]{:S(2)}, u32[]{:S(2)}) collective-permute-start(bf16[80,1024]{1,0:T(8,128)(2,1)} %constant_dynamic-slice_fusion.1), channel_id=1, source_target_pairs={{0,2},{2,0},{1,3},{3,1},{4,6},{6,4},{5,7},{7,5},{8,10},{10,8},{9,1... | collective-permute-start | bytes 491528 | tf_op jit(solution)/shard_map/ppermute | solution.py:382
  20.7 18.2 %collective-permute-start.14 = (bf16[80,1024]{1,0:T(8,128)(2,1)S(1)}, bf16[80,1024]{1,0:T(8,128)(2,1)S(1)}, u32[]{:S(2)}, u32[]{:S(2)}) collective-permute-start(bf16[80,1024]{1,0:T(8,128)(2,1)S(1)} %dynamic-slice_bitcast_fusion), channel_id=1, source_target_pairs={{0,2},{2,0},{1,3},{3,1},{4,6},{6,4},{5,7},{7,5},{8,10},{10,8},{9,1... | collective-permute-start | bytes 491528 | tf_op jit(solution)/shard_map/ppermute | solution.py:382
  32.7 9.3 %collective-permute-start.6 = (bf16[320,512]{1,0:T(8,128)(2,1)S(1)}, bf16[320,512]{1,0:T(8,128)(2,1)S(1)}, u32[]{:S(2)}, u32[]{:S(2)}) collective-permute-start(bf16[320,512]{1,0:T(8,128)(2,1)S(1)} %bitcast.20), channel_id=1, source_target_pairs={{0,2},{2,0},{1,3},{3,1},{4,6},{6,4},{5,7},{7,5},{8,10},{10,8},{9,1... | collective-permute-start | bytes 983048 | tf_op jit(solution)/shard_map/ppermute | solution.py:382
  38.9 7.1 %collective-permute-start.15 = (bf16[80,1024]{1,0:T(8,128)(2,1)S(1)}, bf16[80,1024]{1,0:T(8,128)(2,1)S(1)}, u32[]{:S(2)}, u32[]{:S(2)}) collective-permute-start(bf16[80,1024]{1,0:T(8,128)(2,1)S(1)} %collective-permute-done.14.refs_1_.refs_9_), channel_id=1, source_target_pairs={{0,4},{4,0},{8,12},{12,8},{16,20},{20,16},{24,28},{28,24},{1,5},{5... | collective-permute-start | bytes 491528 | tf_op jit(solution)/shard_map/ppermute | solution.py:388
  39.6 13.1 %collective-permute-start.13 = (bf16[160,1024]{1,0:T(8,128)(2,1)S(1)}, bf16[160,1024]{1,0:T(8,128)(2,1)S(1)}, u32[]{:S(2)}, u32[]{:S(2)}) collective-permute-start(bf16[160,1024]{1,0:T(8,128)(2,1)S(1)} %pad_maximum_fusion.3), channel_id=1, source_target_pairs={{0,4},{4,0},{8,12},{12,8},{16,20},{20,16},{24,28},{28,24},{1,5},{5... | collective-permute-start | bytes 983048 | tf_op jit(solution)/shard_map/ppermute | solution.py:388
  41.2 11.5 %collective-permute-start.10 = (bf16[160,1024]{1,0:T(8,128)(2,1)S(1)}, bf16[160,1024]{1,0:T(8,128)(2,1)S(1)}, u32[]{:S(2)}, u32[]{:S(2)}) collective-permute-start(bf16[160,1024]{1,0:T(8,128)(2,1)S(1)} %pad_maximum_fusion.2), channel_id=1, source_target_pairs={{0,8},{4,12},{8,0},{12,4},{16,24},{20,28},{24,16},{28,20},{1,9},{5... | collective-permute-start | bytes 983048 | tf_op jit(solution)/shard_map/ppermute | solution.py:388
  43.6 9.0 %collective-permute-start.7 = (bf16[256,640]{1,0:T(8,128)(2,1)S(1)}, bf16[256,640]{1,0:T(8,128)(2,1)S(1)}, u32[]{:S(2)}, u32[]{:S(2)}) collective-permute-start(bf16[256,640]{1,0:T(8,128)(2,1)S(1)} %get-tuple-element.93), channel_id=1, source_target_pairs={{0,1},{1,0},{2,3},{3,2},{4,5},{5,4},{6,7},{7,6},{8,9},{9,8},{10,11... | collective-permute-start | bytes 983048 | tf_op jit(solution)/shard_map/ppermute | solution.py:385
  46.1 11.7 %collective-permute-start.16 = (bf16[160,1024]{1,0:T(8,128)(2,1)S(1)}, bf16[160,1024]{1,0:T(8,128)(2,1)S(1)}, u32[]{:S(2)}, u32[]{:S(2)}) collective-permute-start(bf16[160,1024]{1,0:T(8,128)(2,1)S(1)} %pad_maximum_fusion.4), channel_id=1, source_target_pairs={{0,8},{4,12},{8,0},{12,4},{16,24},{20,28},{24,16},{28,20},{1,9},{5... | collective-permute-start | bytes 983048 | tf_op jit(solution)/shard_map/ppermute | solution.py:388
  46.6 14.9 %collective-permute-start.19 = (bf16[320,256]{1,0:T(8,128)(2,1)S(1)}, bf16[320,256]{1,0:T(8,128)(2,1)S(1)}, u32[]{:S(2)}, u32[]{:S(2)}) collective-permute-start(bf16[320,256]{1,0:T(8,128)(2,1)S(1)} %bitcast_convert_fusion), channel_id=1, source_target_pairs={{1,3},{2,0},{5,7},{6,4},{9,11},{10,8},{13,15},{14,12},{17,19},{18,... | collective-permute-start | bytes 491528 | tf_op jit(solution)/shard_map/ppermute | solution.py:413
  73.4 17.6 %collective-permute-start.34 = (bf16[2,160,1024]{2,1,0:T(8,128)(2,1)S(1)}, bf16[2,160,1024]{2,1,0:T(8,128)(2,1)S(1)}, u32[]{:S(2)}, u32[]{:S(2)}) collective-permute-start(bf16[2,160,1024]{2,1,0:T(8,128)(2,1)S(1)} %get-tuple-element.134), channel_id=1, source_target_pairs={{0,8},{4,12},{8,0},{12,4},{16,24},{20,28},{24,16},{28,20},{1,9},{5... | collective-permute-start | bytes 1966088 | tf_op jit(solution)/shard_map/ppermute | solution.py:388
  81.6 12.8 %collective-permute-start.24 = (bf16[256,640]{1,0:T(8,128)(2,1)S(1)}, bf16[256,640]{1,0:T(8,128)(2,1)S(1)}, u32[]{:S(2)}, u32[]{:S(2)}) collective-permute-start(bf16[256,640]{1,0:T(8,128)(2,1)S(1)} %get-tuple-element.118), channel_id=1, source_target_pairs={{0,1},{1,0},{2,3},{3,2},{4,5},{5,4},{6,7},{7,6},{8,9},{9,8},{10,11... | collective-permute-start | bytes 983048 | tf_op jit(solution)/shard_map/ppermute | solution.py:385
  81.9 17.1 %collective-permute-start.41 = (bf16[2,160,1024]{2,1,0:T(8,128)(2,1)}, bf16[2,160,1024]{2,1,0:T(8,128)(2,1)}, u32[]{:S(2)}, u32[]{:S(2)}) collective-permute-start(bf16[2,160,1024]{2,1,0:T(8,128)(2,1)} %get-tuple-element.142), channel_id=1, source_target_pairs={{0,4},{4,0},{8,12},{12,8},{16,20},{20,16},{24,28},{28,24},{1,5},{5... | collective-permute-start | bytes 1966088 | tf_op jit(solution)/shard_map/ppermute | solution.py:388
  82.5 20.7 %collective-permute-start.48 = (bf16[1,320,1024]{2,1,0:T(8,128)(2,1)}, bf16[1,320,1024]{2,1,0:T(8,128)(2,1)}, u32[]{:S(2)}, u32[]{:S(2)}) collective-permute-start(bf16[1,320,1024]{2,1,0:T(8,128)(2,1)} %get-tuple-element.150), channel_id=1, source_target_pairs={{0,2},{2,0},{1,3},{3,1},{4,6},{6,4},{5,7},{7,5},{8,10},{10,8},{9,1... | collective-permute-start | bytes 1966088 | tf_op jit(solution)/shard_map/ppermute | solution.py:382
  83.6 34.7 %collective-permute-start.26 = (bf16[2,160,1280]{2,1,0:T(8,128)(2,1)}, bf16[2,160,1280]{2,1,0:T(8,128)(2,1)}, u32[]{:S(2)}, u32[]{:S(2)}) collective-permute-start(bf16[2,160,1280]{2,1,0:T(8,128)(2,1)} %get-tuple-element.123), channel_id=1, source_target_pairs={{0,8},{4,12},{8,0},{12,4},{16,24},{20,28},{24,16},{28,20},{1,9},{5... | collective-permute-start | bytes 2457608 | tf_op jit(solution)/shard_map/ppermute | solution.py:388
  93.2 22.7 %collective-permute-start.35 = (bf16[1,160,1024]{2,1,0:T(8,128)(2,1)}, bf16[1,160,1024]{2,1,0:T(8,128)(2,1)S(1)}, u32[]{:S(2)}, u32[]{:S(2)}) collective-permute-start(bf16[1,160,1024]{2,1,0:T(8,128)(2,1)} %get-tuple-element.136), channel_id=1, source_target_pairs={{0,2},{2,0},{1,3},{3,1},{4,6},{6,4},{5,7},{7,5},{8,10},{10,8},{9,1... | collective-permute-start | bytes 983048 | tf_op jit(solution)/shard_map/ppermute | solution.py:382
  95.8 11.7 %collective-permute-start.55 = (f32[1792]{0:T(1024)S(1)}, f32[1792]{0:T(1024)S(1)}, u32[]{:S(2)}, u32[]{:S(2)}) collective-permute-start(f32[1792]{0:T(1024)S(1)} %pad_maximum_fusion.12), channel_id=1, source_target_pairs={{0,2},{2,0},{1,3},{3,1},{4,6},{6,4},{5,7},{7,5},{8,10},{10,8},{9,1... | collective-permute-start | bytes 21512 | tf_op jit(solution)/shard_map/ppermute | solution.py:382
  101.8 20.8 %collective-permute-start.42 = (bf16[1,160,1024]{2,1,0:T(8,128)(2,1)}, bf16[1,160,1024]{2,1,0:T(8,128)(2,1)}, u32[]{:S(2)}, u32[]{:S(2)}) collective-permute-start(bf16[1,160,1024]{2,1,0:T(8,128)(2,1)} %get-tuple-element.144), channel_id=1, source_target_pairs={{0,2},{2,0},{1,3},{3,1},{4,6},{6,4},{5,7},{7,5},{8,10},{10,8},{9,1... | collective-permute-start | bytes 983048 | tf_op jit(solution)/shard_map/ppermute | solution.py:382
  106.1 20.2 %collective-permute-start.49 = (bf16[1,160,1024]{2,1,0:T(8,128)(2,1)}, bf16[1,160,1024]{2,1,0:T(8,128)(2,1)S(1)}, u32[]{:S(2)}, u32[]{:S(2)}) collective-permute-start(bf16[1,160,1024]{2,1,0:T(8,128)(2,1)} %get-tuple-element.152), channel_id=1, source_target_pairs={{0,4},{4,0},{8,12},{12,8},{16,20},{20,16},{24,28},{28,24},{1,5},{5... | collective-permute-start | bytes 983048 | tf_op jit(solution)/shard_map/ppermute | solution.py:388
  115.4 7.1 %collective-permute-start.58 = (f32[1792]{0:T(1024)S(1)}, f32[1792]{0:T(1024)S(1)}, u32[]{:S(2)}, u32[]{:S(2)}) collective-permute-start(f32[1792]{0:T(1024)S(1)} %add.72), channel_id=1, source_target_pairs={{0,8},{4,12},{8,0},{12,4},{16,24},{20,28},{24,16},{28,20},{1,9},{5... | collective-permute-start | bytes 21512 | tf_op jit(solution)/shard_map/ppermute | solution.py:388
  117.7 10.4 %collective-permute-start.36 = (bf16[1,80,1024]{2,1,0:T(8,128)(2,1)S(1)}, bf16[1,80,1024]{2,1,0:T(8,128)(2,1)S(1)}, u32[]{:S(2)}, u32[]{:S(2)}) collective-permute-start(bf16[1,80,1024]{2,1,0:T(8,128)(2,1)S(1)} %get-tuple-element.138), channel_id=1, source_target_pairs={{0,4},{4,0},{8,12},{12,8},{16,20},{20,16},{24,28},{28,24},{1,5},{5... | collective-permute-start | bytes 491528 | tf_op jit(solution)/shard_map/ppermute | solution.py:388
  118.3 11.5 %collective-permute-start.21 = (bf16[320,256]{1,0:T(8,128)(2,1)}, bf16[320,256]{1,0:T(8,128)(2,1)S(1)}, u32[]{:S(2)}, u32[]{:S(2)}) collective-permute-start(bf16[320,256]{1,0:T(8,128)(2,1)} %copy-done.24), channel_id=1, source_target_pairs={{0,2},{3,1},{4,6},{7,5},{8,10},{11,9},{12,14},{15,13},{16,18},{19,... | collective-permute-start | bytes 491528 | tf_op jit(solution)/shard_map/ppermute | solution.py:419
  122.5 19.5 %collective-permute-start.27 = (bf16[1,160,1280]{2,1,0:T(8,128)(2,1)S(1)}, bf16[1,160,1280]{2,1,0:T(8,128)(2,1)S(1)}, u32[]{:S(2)}, u32[]{:S(2)}) collective-permute-start(bf16[1,160,1280]{2,1,0:T(8,128)(2,1)S(1)} %get-tuple-element.125), channel_id=1, source_target_pairs={{0,2},{2,0},{1,3},{3,1},{4,6},{6,4},{5,7},{7,5},{8,10},{10,8},{9,1... | collective-permute-start | bytes 1228808 | tf_op jit(solution)/shard_map/ppermute | solution.py:382
  122.6 8.4 %collective-permute-start.59 = (f32[1792]{0:T(1024)S(1)}, f32[1792]{0:T(1024)S(1)}, u32[]{:S(2)}, u32[]{:S(2)}) collective-permute-start(f32[1792]{0:T(1024)S(1)} %add.73), channel_id=1, source_target_pairs={{0,16},{4,20},{8,24},{12,28},{16,0},{20,4},{24,8},{28,12},{1,17},{... | collective-permute-start | bytes 21512 | tf_op jit(solution)/shard_map/ppermute | solution.py:388
  126.4 8.7 %collective-permute-start.43 = (bf16[1,80,1024]{2,1,0:T(8,128)(2,1)S(1)}, bf16[1,80,1024]{2,1,0:T(8,128)(2,1)S(1)}, u32[]{:S(2)}, u32[]{:S(2)}) collective-permute-start(bf16[1,80,1024]{2,1,0:T(8,128)(2,1)S(1)} %get-tuple-element.146), channel_id=1, source_target_pairs={{0,8},{4,12},{8,0},{12,4},{16,24},{20,28},{24,16},{28,20},{1,9},{5... | collective-permute-start | bytes 491528 | tf_op jit(solution)/shard_map/ppermute | solution.py:388
  128.1 10.2 %collective-permute-start.50 = (bf16[1,80,1024]{2,1,0:T(8,128)(2,1)S(1)}, bf16[1,80,1024]{2,1,0:T(8,128)(2,1)S(1)}, u32[]{:S(2)}, u32[]{:S(2)}) collective-permute-start(bf16[1,80,1024]{2,1,0:T(8,128)(2,1)S(1)} %get-tuple-element.154), channel_id=1, source_target_pairs={{0,8},{4,12},{8,0},{12,4},{16,24},{20,28},{24,16},{28,20},{1,9},{5... | collective-permute-start | bytes 491528 | tf_op jit(solution)/shard_map/ppermute | solution.py:388
  129.8 9.5 %collective-permute-start.37 = (bf16[1,40,1024]{2,1,0:T(8,128)(2,1)S(1)}, bf16[1,40,1024]{2,1,0:T(8,128)(2,1)S(1)}, u32[]{:S(2)}, u32[]{:S(2)}) collective-permute-start(bf16[1,40,1024]{2,1,0:T(8,128)(2,1)S(1)} %get-tuple-element.140), channel_id=1, source_target_pairs={{0,16},{4,20},{8,24},{12,28},{16,0},{20,4},{24,8},{28,12},{1,17},{... | collective-permute-start | bytes 245768 | tf_op jit(solution)/shard_map/ppermute | solution.py:388
  131.0 52.8 %collective-permute-start.25 = (bf16[320,256]{1,0:T(8,128)(2,1)S(1)}, bf16[320,256]{1,0:T(8,128)(2,1)S(1)}, u32[]{:S(2)}, u32[]{:S(2)}) collective-permute-start(bf16[320,256]{1,0:T(8,128)(2,1)S(1)} %get-tuple-element.121), channel_id=1, source_target_pairs={{0,2},{3,1},{4,6},{7,5},{8,10},{11,9},{12,14},{15,13},{16,18},{19,... | collective-permute-start | bytes 491528 | tf_op jit(solution)/shard_map/ppermute | solution.py:419
  135.7 9.3 %collective-permute-start.44 = (bf16[1,40,1024]{2,1,0:T(8,128)(2,1)S(1)}, bf16[1,40,1024]{2,1,0:T(8,128)(2,1)S(1)}, u32[]{:S(2)}, u32[]{:S(2)}) collective-permute-start(bf16[1,40,1024]{2,1,0:T(8,128)(2,1)S(1)} %get-tuple-element.148), channel_id=1, source_target_pairs={{0,16},{4,20},{8,24},{12,28},{16,0},{20,4},{24,8},{28,12},{1,17},{... | collective-permute-start | bytes 245768 | tf_op jit(solution)/shard_map/ppermute | solution.py:388
  138.9 10.5 %collective-permute-start.51 = (bf16[1,40,1024]{2,1,0:T(8,128)(2,1)S(1)}, bf16[1,40,1024]{2,1,0:T(8,128)(2,1)S(1)}, u32[]{:S(2)}, u32[]{:S(2)}) collective-permute-start(bf16[1,40,1024]{2,1,0:T(8,128)(2,1)S(1)} %get-tuple-element.156), channel_id=1, source_target_pairs={{0,16},{4,20},{8,24},{12,28},{16,0},{20,4},{24,8},{28,12},{1,17},{... | collective-permute-start | bytes 245768 | tf_op jit(solution)/shard_map/ppermute | solution.py:388
  139.4 13.7 %collective-permute-start.38 = (bf16[1,40,1024]{2,1,0:T(8,128)(2,1)S(1)}, bf16[1,40,1024]{2,1,0:T(8,128)(2,1)S(1)}, u32[]{:S(2)}, u32[]{:S(2)}) collective-permute-start(bf16[1,40,1024]{2,1,0:T(8,128)(2,1)S(1)} %shard_map.289), channel_id=1, source_target_pairs={{0,16},{4,20},{8,24},{12,28},{16,0},{20,4},{24,8},{28,12},{1,17},{... | collective-permute-start | bytes 245768 | tf_op jit(solution)/shard_map/ppermute | solution.py:388
  142.7 6.8 %collective-permute-start.28 = (bf16[1,80,1280]{2,1,0:T(8,128)(2,1)S(1)}, bf16[1,80,1280]{2,1,0:T(8,128)(2,1)S(1)}, u32[]{:S(2)}, u32[]{:S(2)}) collective-permute-start(bf16[1,80,1280]{2,1,0:T(8,128)(2,1)S(1)} %get-tuple-element.127), channel_id=1, source_target_pairs={{0,4},{4,0},{8,12},{12,8},{16,20},{20,16},{24,28},{28,24},{1,5},{5... | collective-permute-start | bytes 614408 | tf_op jit(solution)/shard_map/ppermute | solution.py:388
  144.9 14.9 %collective-permute-start.45 = (bf16[1,40,1024]{2,1,0:T(8,128)(2,1)S(1)}, bf16[1,40,1024]{2,1,0:T(8,128)(2,1)S(1)}, u32[]{:S(2)}, u32[]{:S(2)}) collective-permute-start(bf16[1,40,1024]{2,1,0:T(8,128)(2,1)S(1)} %shard_map.294), channel_id=1, source_target_pairs={{0,16},{4,20},{8,24},{12,28},{16,0},{20,4},{24,8},{28,12},{1,17},{... | collective-permute-start | bytes 245768 | tf_op jit(solution)/shard_map/ppermute | solution.py:388
  149.4 15.0 %collective-permute-start.52 = (bf16[1,40,1024]{2,1,0:T(8,128)(2,1)S(1)}, bf16[1,40,1024]{2,1,0:T(8,128)(2,1)S(1)}, u32[]{:S(2)}, u32[]{:S(2)}) collective-permute-start(bf16[1,40,1024]{2,1,0:T(8,128)(2,1)S(1)} %shard_map.299), channel_id=1, source_target_pairs={{0,16},{4,20},{8,24},{12,28},{16,0},{20,4},{24,8},{28,12},{1,17},{... | collective-permute-start | bytes 245768 | tf_op jit(solution)/shard_map/ppermute | solution.py:388
  153.1 15.1 %collective-permute-start.39 = (bf16[2,40,1024]{2,1,0:T(8,128)(2,1)S(1)}, bf16[2,40,1024]{2,1,0:T(8,128)(2,1)S(1)}, u32[]{:S(2)}, u32[]{:S(2)}) collective-permute-start(bf16[2,40,1024]{2,1,0:T(8,128)(2,1)S(1)} %pad_maximum_fusion.9), channel_id=1, source_target_pairs={{0,8},{4,12},{8,0},{12,4},{16,24},{20,28},{24,16},{28,20},{1,9},{5... | collective-permute-start | bytes 491528 | tf_op jit(solution)/shard_map/ppermute | solution.py:388
  156.8 7.1 %collective-permute-start.30 = (bf16[1,40,1280]{2,1,0:T(8,128)(2,1)S(1)}, bf16[1,40,1280]{2,1,0:T(8,128)(2,1)S(1)}, u32[]{:S(2)}, u32[]{:S(2)}) collective-permute-start(bf16[1,40,1280]{2,1,0:T(8,128)(2,1)S(1)} %shard_map.284), channel_id=1, source_target_pairs={{0,16},{4,20},{8,24},{12,28},{16,0},{20,4},{24,8},{28,12},{1,17},{... | collective-permute-start | bytes 307208 | tf_op jit(solution)/shard_map/ppermute | solution.py:388
  159.9 16.3 %collective-permute-start.46 = (bf16[2,40,1024]{2,1,0:T(8,128)(2,1)S(1)}, bf16[2,40,1024]{2,1,0:T(8,128)(2,1)S(1)}, u32[]{:S(2)}, u32[]{:S(2)}) collective-permute-start(bf16[2,40,1024]{2,1,0:T(8,128)(2,1)S(1)} %pad_maximum_fusion.10), channel_id=1, source_target_pairs={{0,8},{4,12},{8,0},{12,4},{16,24},{20,28},{24,16},{28,20},{1,9},{5... | collective-permute-start | bytes 491528 | tf_op jit(solution)/shard_map/ppermute | solution.py:388
  163.9 8.0 %collective-permute-start.31 = (bf16[2,40,1280]{2,1,0:T(8,128)(2,1)S(1)}, bf16[2,40,1280]{2,1,0:T(8,128)(2,1)S(1)}, u32[]{:S(2)}, u32[]{:S(2)}) collective-permute-start(bf16[2,40,1280]{2,1,0:T(8,128)(2,1)S(1)} %pad_maximum_fusion.8), channel_id=1, source_target_pairs={{0,4},{4,0},{8,12},{12,8},{16,20},{20,16},{24,28},{28,24},{1,5},{5... | collective-permute-start | bytes 614408 | tf_op jit(solution)/shard_map/ppermute | solution.py:388
  164.5 11.8 %collective-permute-start.53 = (bf16[2,40,1024]{2,1,0:T(8,128)(2,1)S(1)}, bf16[2,40,1024]{2,1,0:T(8,128)(2,1)S(1)}, u32[]{:S(2)}, u32[]{:S(2)}) collective-permute-start(bf16[2,40,1024]{2,1,0:T(8,128)(2,1)S(1)} %pad_maximum_fusion.11), channel_id=1, source_target_pairs={{0,8},{4,12},{8,0},{12,4},{16,24},{20,28},{24,16},{28,20},{1,9},{5... | collective-permute-start | bytes 491528 | tf_op jit(solution)/shard_map/ppermute | solution.py:388
  168.3 16.3 %collective-permute-start.40 = (bf16[4,40,1024]{2,1,0:T(8,128)(2,1)S(1)}, bf16[4,40,1024]{2,1,0:T(8,128)(2,1)S(1)}, u32[]{:S(2)}, u32[]{:S(2)}) collective-permute-start(bf16[4,40,1024]{2,1,0:T(8,128)(2,1)S(1)} %pad_maximum_fusion.5.near), channel_id=1, source_target_pairs={{0,4},{4,0},{8,12},{12,8},{16,20},{20,16},{24,28},{28,24},{1,5},{5... | collective-permute-start | bytes 983048 | tf_op jit(solution)/shard_map/ppermute | solution.py:388
  172.0 10.1 %collective-permute-start.32 = (bf16[4,40,1280]{2,1,0:T(8,128)(2,1)S(1)}, bf16[4,40,1280]{2,1,0:T(8,128)(2,1)S(1)}, u32[]{:S(2)}, u32[]{:S(2)}) collective-permute-start(bf16[4,40,1280]{2,1,0:T(8,128)(2,1)S(1)} %pad_maximum_fusion.1.near), channel_id=1, source_target_pairs={{0,8},{4,12},{8,0},{12,4},{16,24},{20,28},{24,16},{28,20},{1,9},{5... | collective-permute-start | bytes 1228808 | tf_op jit(solution)/shard_map/ppermute | solution.py:388
  176.2 10.1 %collective-permute-start.47 = (bf16[4,40,1024]{2,1,0:T(8,128)(2,1)S(1)}, bf16[4,40,1024]{2,1,0:T(8,128)(2,1)S(1)}, u32[]{:S(2)}, u32[]{:S(2)}) collective-permute-start(bf16[4,40,1024]{2,1,0:T(8,128)(2,1)S(1)} %pad_maximum_fusion.6.near), channel_id=1, source_target_pairs={{0,4},{4,0},{8,12},{12,8},{16,20},{20,16},{24,28},{28,24},{1,5},{5... | collective-permute-start | bytes 983048 | tf_op jit(solution)/shard_map/ppermute | solution.py:388
  176.3 12.2 %collective-permute-start.54 = (bf16[4,40,1024]{2,1,0:T(8,128)(2,1)S(1)}, bf16[4,40,1024]{2,1,0:T(8,128)(2,1)S(1)}, u32[]{:S(2)}, u32[]{:S(2)}) collective-permute-start(bf16[4,40,1024]{2,1,0:T(8,128)(2,1)S(1)} %pad_maximum_fusion.7.near), channel_id=1, source_target_pairs={{0,4},{4,0},{8,12},{12,8},{16,20},{20,16},{24,28},{28,24},{1,5},{5... | collective-permute-start | bytes 983048 | tf_op jit(solution)/shard_map/ppermute | solution.py:388
  (39 other events, 286.0 us)
where the time goes:
time: 194 us; the launch traced here: 191 us
  starting transfers between devices  81.3 us (42%)
  waiting for transfers between devices  51.9 us (27%)
  Pallas kernels  39 us (20%)
  local copies, waits for them, and re-layouts  9.96 us (5%)
  other arithmetic  7.63 us (4%)
    ppermute x33, starting transfers between devices, swap_dp(): return lax.ppermute(v, 'dp', [(i, i ^ bit) for i in range(n_dp)])  48 us
    pallas_call x30, Pallas kernels, call(): pl.pallas_call(body, in_specs=in_specs, out_specs=[pl.BlockSpec(memory_sp...  39 us
    ppermute x33, waiting for transfers between devices, swap_dp(): return lax.ppermute(v, 'dp', [(i, i ^ bit) for i in range(n_dp)])  35.9 us
    ppermute x4, starting transfers between devices, diag_to_off_col(): return lax.ppermute(v, ('row', 'col'), [(0, 1), (3, 2)])  12.4 us
    ppermute x11, waiting for transfers between devices, swap_row(): return lax.ppermute(v, 'row', [(0, 1), (1, 0)])  12 us
    ppermute x11, starting transfers between devices, swap_row(): return lax.ppermute(v, 'row', [(0, 1), (1, 0)])  9.9 us
    ppermute x2, starting transfers between devices, diag_to_off_row(): return lax.ppermute(v, ('row', 'col'), [(0, 2), (3, 1)])  6.84 us
    unnamed x54, local copies, waits for them, and re-layouts  6.2 us
  transfers between devices with their start and end apart: 60, of which 18 were waited for; matrix products, arithmetic and copies ran while one was open for 6% of the time, Pallas kernels for 17%

commit v1 on v0

--- a/solution.py
+++ b/solution.py
@@ -11,15 +11,16 @@
 f32 = jnp.float32
 gelu_c = (2.0 / 3.141592653589793) ** 0.5
 gelu_a = 0.044715
+gain_cols = 128
 
 
 PLAN = {
-    "down": ("y", 1, 2, 4),
-    "gate": (2, "y", 1, 4),
-    "up": (1, "y", 2, 4),
-    "attn": (2, "y", 1, 4),
+    "down": (2, 1, "y", 4),
+    "gate": (1, 2, "y", 4),
+    "up": (2, 1, "y", 4),
+    "attn": ("y", 1, 2, 4),
 }
-GATHER = {"down": (4, 2, 1), "gate": (4, 2, 1), "up": (4, 2, 1), "attn": (4, 1, 2)}
+GATHER = {"down": (2, 1), "gate": (2, 1), "up": (2, 1), "attn": (1, 2)}
 TOP_BITS = (1, 2, 4)
 
 
@@ -78,10 +79,10 @@
     scr[half:, :] = other[...]
 
 
-def place_rows(scr, sc, pieces, first_bit):
-    own, near, first, second = pieces
+def place_rows(scr, sc, own, group, first_bit, source, target):
+    near, first, second = group
     half, q = own.shape[0], near.shape[0]
-    scr[:half, :] = own[...]
+    scr[:half, target] = own[:, target]
     b1, b2 = sc[1], sc[2]
 
     def at(r1, r2):
@@ -89,10 +90,23 @@
         p2 = 1 - b2 if r2 else b2
         return pl.ds(pl.multiple_of(half + q * (2 * p2 + p1), 16), q)
 
-    scr[at(0, 0), :] = near[...]
-    scr[at(1, 0) if first_bit == 1 else at(0, 1), :] = first[...]
-    scr[at(0, 1) if first_bit == 1 else at(1, 0), :] = second[:q, :]
-    scr[at(1, 1), :] = second[q:, :]
+    scr[at(0, 0), target] = near[:, source]
+    scr[at(1, 0) if first_bit == 1 else at(0, 1), target] = first[:, source]
+    scr[at(0, 1) if first_bit == 1 else at(1, 0), target] = second[:q, source]
+    scr[at(1, 1), target] = second[q:, source]
+
+
+def place_mix(wg, wu, sc, own_g, own_u, e1, e2):
+    ff = wg.shape[1]
+    place_rows(wg, sc, own_g, e1, 1, slice(0, ff), slice(0, ff))
+    place_rows(wu, sc, own_u, e2, 2, slice(0, ff), slice(0, ff))
+
+
+def place_down(wd, sc, own, e1, e2):
+    ff = wd.shape[1]
+    tail = slice(ff, ff + ff // 2)
+    place_rows(wd, sc, own, e1, 1, tail, slice(0, ff // 2))
+    place_rows(wd, sc, own, e2, 2, tail, slice(ff // 2, ff))
 
 
 def sequence_t(sc, local, own_recv, diag_recv, other_recv):
@@ -114,8 +128,9 @@
     kv[...] = p[:, qw:]
 
 
-def cot_body(sc, c_local, c_own, c_diag, c_other, cot):
-    cot[...] = sequence_t(sc, c_local, c_own, c_diag, c_other)
+def cot_body(sc, c_local, c_diag, c_off, cot):
+    here = jnp.concatenate([c_local[...], c_diag[...].astype(f32)], axis=0)
+    cot[...] = jnp.where(sc[3] == 1, here, c_off[...].astype(f32)).T
 
 
 def attn_body(sc, raw_q, kv_mine, kv_theirs, mask, cos, sin, gq, gk, w_own, w_other, q, k, v,
@@ -146,10 +161,8 @@
 
 
 def mix_body(sc, x, own, recv, g, *refs):
-    wg_p, wu_p = refs[0:4], refs[4:8]
     proj, mid, ffn_in, gate, up, hidden, wg, wu = refs[8:]
-    place_rows(wg, sc, wg_p, 1)
-    place_rows(wu, sc, wu_p, 2)
+    place_mix(wg, wu, sc, refs[0], refs[1], refs[2:5], refs[5:8])
     y = own[...] + recv[...].astype(f32)
     proj[...] = y
     m = x[...] + y * rms_scale(y) * g[1:2, :]
@@ -164,9 +177,8 @@
 
 
 def down_body(sc, hidden, *refs):
-    wd_p = refs[0:4]
-    part, send, wd = refs[4:]
-    place_rows(wd, sc, wd_p, 1)
+    part, send, wd = refs[7:]
+    place_down(wd, sc, refs[0], refs[1:4], refs[4:7])
     out = dot(hidden[...], wd[...], ((1,), (1,)))
     part[...] = out
     send[...] = out.astype(bf16)
@@ -188,7 +200,10 @@
 
 
 def split_grad(sc, left_t, right, send, keep, acc, d, col=0):
-    g = dot(left_t, right)
+    split_sum(sc, dot(left_t, right), send, keep, acc, d, col)
+
+
+def split_sum(sc, g, send, keep, acc, d, col=0):
     n = g.shape[1]
     cols = slice(col, col + n)
     half = g.shape[0] // 2
@@ -236,20 +251,18 @@
 
 
 def last_sum_body(keep_in, recv, send):
-    send[...] = (keep_in[...] + recv[...].astype(f32)).astype(bf16)
+    send[...] = (keep_in[...].astype(f32) + recv[...].astype(f32)).astype(bf16)
 
 
 def assemble_body(order, widths):
     def body(sc, near, far, *outs):
         rows = near.shape[1]
         for part, ref in ((0, near), (1, far)):
-            for j in range(4):
-                rel = {order[0]: j & 1, order[1]: j >> 1, order[2]: part}
-                pos = 0
-                for bit in TOP_BITS:
-                    b = sc[bit]
-                    pos = 2 * pos + (1 - b if rel[bit] else b)
-                at = pl.ds(pl.multiple_of(pos * rows, 8), rows)
+            for j in range(2):
+                rel = {order[0]: j, order[1]: part}
+                p1 = 1 - sc[1] if rel[1] else sc[1]
+                p2 = 1 - sc[2] if rel[2] else sc[2]
+                at = pl.ds(pl.multiple_of((2 * p1 + p2) * rows, 8), rows)
                 val = ref[j].astype(f32)
                 col = 0
                 for out, w in zip(outs, widths):
@@ -260,7 +273,7 @@
 
 
 def down_grad_body(sc, mid, own, recv, cot, g, hidden, out, out_send, grad_ffn, gain_part, send,
-                   keep):
+                   keep, acc):
     f = own[...] + recv[...].astype(f32)
     s = rms_scale(f)
     full = (mid[...] + f * s * g[3:4, :]).T
@@ -271,15 +284,13 @@
     gain_part[...] = part
     gf = through.astype(bf16)
     grad_ffn[...] = gf
-    split_grad(sc, gf.T, hidden[...], send, keep, None, PLAN["down"][0])
+    split_grad(sc, gf.T, hidden[...], send, keep, acc, PLAN["down"][0])
 
 
 def mix_grad_body(sc, grad_ffn, gate, up, ffn_in, *refs):
-    wg_p, wu_p, wd_p = refs[0:4], refs[4:8], refs[8:12]
-    s_gate, k_gate, s_up, k_up, part, send, wg, wu, wd, acc = refs[12:]
-    place_rows(wd, sc, wd_p, 1)
-    place_rows(wg, sc, wg_p, 1)
-    place_rows(wu, sc, wu_p, 2)
+    s_gate, k_gate, s_up, k_up, part, send, wg, wu, wd, acc = refs[9:]
+    place_down(wd, sc, refs[2], refs[3:6], refs[6:9])
+    place_mix(wg, wu, sc, refs[0], refs[1], refs[3:6], refs[6:9])
     gh = dot(grad_ffn[...], wd[...])
     v = gate[...]
     t, gelu = gelu_parts(v)
@@ -335,8 +346,9 @@
     kv_send[...] = jnp.where(first, value_part, key_part)
 
 
-def joint_body(sc, kv_own, kv_recv, kv_raw, cos, sin, gk, grad_q, normed, grad_attn, heads,
-               w_own, w_other, k_part, send, keep, part, part_send, w, acc):
+def joint_body(sc, kv_own, kv_recv, kv_raw, cos, sin, gk, grad_q, normed, grad_attn, heads, x,
+               attn_part, pre_part, post_part, q_part, w_own, w_other, send, keep, part,
+               part_send, w, acc):
     join_rows(w, w_own, w_other)
     total = kv_own[...] + kv_recv[...]
     raw = kv_raw[...]
@@ -344,7 +356,7 @@
         rotate_back(total, cos[...], sin[...]), raw, rms_scale(raw), gk[...]
     )
     first = sc[0] == 1
-    k_part[...] = jnp.where(first, gain_part, 0.0)
+    k_part = jnp.where(first, gain_part, 0.0)
     kvg = jnp.where(first, through, total).astype(bf16)
     gq = grad_q[...]
     qw, kw = gq.shape[1], kvg.shape[1]
@@ -352,21 +364,44 @@
     d = PLAN["attn"][0]
     split_grad(sc, n_t, gq, send, keep, acc, d, 0)
     split_grad(sc, n_t, kvg, send, keep, acc, d, qw)
-    split_grad(sc, grad_attn[...].T, heads[...], send, keep, acc, d, qw + kw)
     out = dot(gq, w[:, :qw], ((1,), (1,))) + dot(kvg, w[:, qw:], ((1,), (1,)))
     part[...] = out
     part_send[...] = out.astype(bf16)
-
-
-def input_body(own, recv, x, grad_mid, g, out, out_send, gain_part):
+    v = x[...]
+    in_part = jnp.sum(out * v * rms_scale(v), axis=0, keepdims=True)
+    diag = sc[3] == 1
+    shared = [jnp.where(diag, ref[...], 0.0) for ref in (attn_part, pre_part, post_part)]
+    half = v.shape[1] // 2
+    wide = jnp.concatenate(
+        [in_part] + shared + [jnp.zeros((gain_cols - 4, v.shape[1]), f32)], axis=0
+    ).T
+    ends = jnp.concatenate(
+        [jnp.zeros((4, kw), f32), q_part[...], k_part, jnp.zeros((gain_cols - 6, kw), f32)],
+        axis=0,
+    ).T
+    ends = jnp.concatenate([ends, jnp.zeros((half - kw, gain_cols), f32)], axis=0)
+    gains = wide + jnp.concatenate([ends, ends], axis=0)
+    split_sum(sc, gains, send, keep, acc, d, qw + kw)
+    split_grad(sc, grad_attn[...].T, heads[...], send, keep, acc, d, qw + kw + gain_cols)
+
+
+def finish_body(sc, own, recv, key, value, gains):
+    first = sc[0] == 1
+    kw = key.shape[1]
+    a, b = own[:, :kw].astype(f32), recv[:, :kw].astype(f32)
+    key[...] = jnp.where(first, a, b)
+    value[...] = jnp.where(first, b, a)
+    gains[...] = (own[:, kw:].astype(f32) + recv[:, kw:].astype(f32)).T[: gains.shape[0]]
+
+
+def input_body(own, recv, x, grad_mid, g, out, out_send):
     up = own[...] + recv[...].astype(f32)
     v = x[...]
-    through, part = norm_back(up, v, rms_scale(v), g[0:1, :])
+    through, _ = norm_back(up, v, rms_scale(v), g[0:1, :])
     full = (grad_mid[...] + through).T
     half = full.shape[0] // 2
     out[...] = full[:half]
     out_send[...] = full[half:].astype(bf16)
-    gain_part[...] = part
 
 
 def make_step(mesh):
@@ -424,13 +459,14 @@
             from_row = off_to_diag(narrow)
             return local_t, diag_to_off_col(narrow), from_row, diag_to_off_col(from_row)
 
-        def with_other_rows(own, first_bit, second_bit):
-            q = own.shape[0] // 4
+        def other_rows(own, first_bit, second_bit):
+            q = half_width // 4
             at = (2 * bit_of(2) + bit_of(1)) * q
-            near = swap_row(lax.dynamic_slice_in_dim(own, at, q, 0))
+            part = jnp.concatenate([lax.dynamic_slice_in_dim(w, at, q, 0) for w in own], axis=1)
+            near = swap_row(part)
             first = swap_dp(near, first_bit)
             second = swap_dp(jnp.concatenate([near, first], axis=0), second_bit)
-            return own, near, first, second
+            return near, first, second
 
         x_pieces = chip_sequence(block_input, f32)
         joint_own = jnp.concatenate([w_query, jnp.where(first_col, w_key, w_value)], axis=1)
@@ -441,12 +477,15 @@
             jnp.where(which == 1, gain_attn, jnp.where(which == 2, gain_ffn_pre, gain_ffn_post)),
         )
         gains = jnp.concatenate([gains_own, swap_row(gains_own)], axis=1)
-        wg = with_other_rows(w_gate, 1, 2)
-        wu = with_other_rows(w_up, 2, 1)
         out_own = w_out.T
         wo = (out_own, swap_row(out_own))
-        wd = with_other_rows(w_down.T, 1, 2)
-        cot_pieces = chip_sequence(out_cotangent, bf16)
+        down_own = w_down.T
+        e1 = other_rows((w_gate, down_own[:, : ff // 2]), 1, 2)
+        e2 = other_rows((w_up, down_own[:, ff // 2 :]), 2, 1)
+        cot_t = out_cotangent.T
+        cot_narrow = cot_t.astype(bf16)
+        cot_diag = off_to_diag(cot_narrow)
+        cot_off = diag_to_off_col(jnp.concatenate([cot_narrow, cot_diag], axis=0))
 
         segments = segment_ids[0]
         places = jnp.arange(rows, dtype=jnp.int32)
@@ -475,15 +514,15 @@
             raw_q, kv_mine, kv_theirs, mask, cos, sin, gq, gk, *wo, scalars=sc,
             scratch=[pltpu.VMEM((width, qw), bf16)],
         )
-        (cotangent,) = call(cot_body, [wide_f], *cot_pieces, scalars=sc)
+        (cotangent,) = call(cot_body, [wide_f], cot_t, cot_diag, cot_off, scalars=sc)
         proj, mid, ffn_in, gate, up, hidden = call(
             mix_body,
             [wide_f, wide_f, wide_b, ((t, ff), f32), ((t, ff), f32), ((t, ff), bf16)],
-            x, part, swap_col(send), gains, *wg, *wu, scalars=sc,
+            x, part, swap_col(send), gains, w_gate, w_up, *e1, *e2, scalars=sc,
             scratch=ffn_scratch[:2],
         )
         part, send = call(
-            down_body, [wide_f, wide_b], hidden, *wd, scalars=sc,
+            down_body, [wide_f, wide_b], hidden, down_own, *e1, *e2, scalars=sc,
             scratch=ffn_scratch[:1],
         )
 
@@ -518,9 +557,9 @@
             left = list(TOP_BITS)
             if order[0] != "y":
                 left.remove(order[0])
-            for stage, d in enumerate(order):
+            for stage, d in enumerate(order[:-1]):
                 recv = swap(send, d)
-                if stage + 1 == len(order):
+                if stage == len(order) - 2:
                     break
                 nxt = order[stage + 1]
                 blocks, r, _ = keep.shape
@@ -533,9 +572,11 @@
                 if nxt != "y":
                     left.remove(nxt)
             (cur,) = call(last_sum_body, [(keep.shape, bf16)], keep, recv)
+            stage = len(order) - 1
+            recv = swap_dp(cur, order[-1])
+            (cur,) = call(last_sum_body, [(cur.shape, bf16)], cur, recv)
             if extra:
                 cur = more_bits(cur)
-            stage = len(order) - 1
             for d in GATHER[name]:
                 stage += 1
                 theirs = swap_dp(cur, d)
@@ -546,21 +587,18 @@
                 [((half_width, w), dt) for w, dt in outs], cur, theirs, scalars=sc, out_hbm=True,
             )
 
-        def place_out(own_t, send):
-            return jnp.where(diag, own_t, diag_to_off_row(send).astype(f32)).T
-
         out_pair = [((half_width, t), f32), ((half_width, t), bf16)]
-        own_t, out_send, grad_ffn, post_part, s_down, k_down = call(
+        out_own_t, out_send, grad_ffn, post_part, s_down, k_down = call(
             down_grad_body,
             out_pair + [wide_b, ((1, width), f32)] + first_shapes("down", ff),
             mid, part, swap_col(send), cotangent, gains, hidden, scalars=sc,
-        )
-        block_output = place_out(own_t, out_send)
+            scratch=[pltpu.VMEM((2, half_width, ff), f32)],
+        )
         (down_sum,) = grad_sum("down", s_down, k_down, [(ff, f32)])
         s_gate, k_gate, s_up, k_up, part, send = call(
             mix_grad_body,
             first_shapes("gate", ff) + first_shapes("up", ff) + [wide_f, wide_b],
-            grad_ffn, gate, up, ffn_in, *wg, *wu, *wd, scalars=sc,
+            grad_ffn, gate, up, ffn_in, w_gate, w_up, down_own, *e1, *e2, scalars=sc,
             scratch=ffn_scratch + [pltpu.VMEM((2, half_width, ff), f32)],
         )
         (gate_sum,) = grad_sum("gate", s_gate, k_gate, [(ff, f32)])
@@ -572,42 +610,34 @@
             part, swap_col(send), mid, proj, cotangent, gains, *wo, q, k, v, probs,
             raw_q, cos, sin, gq, scalars=sc, scratch=[pltpu.VMEM((width, qw), bf16)],
         )
-        n_attn = joint_width + qw
-        k_part, s_attn, k_attn, part, send = call(
-            joint_body,
-            [((1, hd), f32)] + first_shapes("attn", n_attn) + [wide_f, wide_b],
+        n_attn = joint_width + gain_cols + qw
+        s_attn, k_attn, part, send = call(
+            joint_body, first_shapes("attn", n_attn) + [wide_f, wide_b],
             kv_own, swap_col(kv_send), kv_mine, cos, sin, gk, grad_q, normed,
-            grad_attn, heads, *w_joint, scalars=sc,
+            grad_attn, heads, x, attn_part, pre_part, post_part, q_part, *w_joint, scalars=sc,
             scratch=[pltpu.VMEM((width, joint_width), bf16),
                      pltpu.VMEM((2, half_width, n_attn), f32)],
         )
         query_sum, kv_sum, out_sum = grad_sum(
-            "attn", s_attn, k_attn, [(qw, f32), (hd, bf16), (qw, f32)]
-        )
-        own_t, out_send, in_part = call(
-            input_body, out_pair + [((1, width), f32)],
+            "attn", s_attn, k_attn, [(qw, f32), (hd + gain_cols, bf16), (qw, f32)]
+        )
+        in_own_t, in_send = call(
+            input_body, out_pair,
             part, swap_col(send), x, grad_mid, gains,
         )
-        input_grad = place_out(own_t, out_send)
-        kv_sum_theirs = swap_col(kv_sum)
-        key_sum = jnp.where(first_col, kv_sum, kv_sum_theirs).astype(f32)
-        value_sum = jnp.where(first_col, kv_sum_theirs, kv_sum).astype(f32)
-
-        width_parts = jnp.concatenate([in_part, attn_part, pre_part, post_part], axis=0)
-        width_parts = jnp.where(diag, width_parts, 0.0)
-        ends = [q_part[0], k_part[0]]
-        own = jnp.concatenate([width_parts[:, :half_width].reshape(-1)] + ends)
-        away = jnp.concatenate([width_parts[:, half_width:].reshape(-1)] + ends)
-        small = own + swap_row(away)
-        small = small + swap_col(small)
-        for bit in bits:
-            small = small + swap_dp(small, bit)
-        width_sums = small[: 4 * half_width].reshape(4, half_width)
+        both = diag_to_off_row(jnp.concatenate([out_send, in_send], axis=0)).astype(f32)
+        block_output = jnp.where(diag, out_own_t, both[:half_width]).T
+        input_grad = jnp.where(diag, in_own_t, both[half_width:]).T
+        key_sum, value_sum, gain_sum = call(
+            finish_body,
+            [((half_width, hd), f32), ((half_width, hd), f32), ((8, half_width), f32)],
+            kv_sum, swap_col(kv_sum), scalars=sc, out_hbm=True,
+        )
         return (
             block_output, input_grad, query_sum, key_sum, value_sum, out_sum.T,
             gate_sum, up_sum, down_sum.T,
-            width_sums[0], width_sums[1], width_sums[2], width_sums[3],
-            small[4 * half_width : 4 * half_width + hd], small[4 * half_width + hd :],
+            gain_sum[0], gain_sum[1], gain_sum[2], gain_sum[3],
+            gain_sum[4, :hd], gain_sum[5, :hd],
         )
 
     return step

time: 194 us -> 189 us (0.974); the launches traced: 191 us -> 189 us
  waiting for transfers between devices: 51.9 us -> 87 us
  starting transfers between devices: 81.3 us -> 57.6 us
  Pallas kernels: 39 us -> 32.5 us
  local copies, waits for them, and re-layouts: 9.96 us -> 3.91 us
    ppermute x11 -> x9, waiting for transfers between devices: 12 us -> 32.1 us  [swap_row(): return lax.ppermute(v, 'row', [(0, 1), (1, 0)])]
    ppermute x33 -> x24, starting transfers between devices: 48 us -> 29.7 us  [swap_dp(): return lax.ppermute(v, 'dp', [(i, i ^ bit) for i in range(n_dp)])]
    ppermute x33 -> x24, waiting for transfers between devices: 35.9 us -> 45.3 us  [swap_dp(): return lax.ppermute(v, 'dp', [(i, i ^ bit) for i in range(n_dp)])]
    pallas_call x30 -> x31, Pallas kernels: 39 us -> 32.5 us  [call(): pl.pallas_call(body, in_specs=in_specs, out_specs=[pl.BlockSpec(memory_sp...]
    ppermute x2, waiting for transfers between devices: 0.01 us -> 5.92 us  [off_to_diag(): return lax.ppermute(v, ('row', 'col'), [(1, 3), (2, 0)])]
    unnamed x54 -> x20, local copies, waits for them, and re-layouts: 6.2 us -> 1.02 us
    ppermute x2 -> x1, starting transfers between devices: 6.84 us -> 3.27 us  [diag_to_off_row(): return lax.ppermute(v, ('row', 'col'), [(0, 2), (3, 1)])]
    ppermute x4 -> x3, starting transfers between devices: 12.4 us -> 10.8 us  [diag_to_off_col(): return lax.ppermute(v, ('row', 'col'), [(0, 1), (3, 2)])]
  transfers between devices with their start and end apart: 60 -> 46, of which waited for: 18 -> 16; matrix products, arithmetic and copies ran while one was open for 6% -> 4% of each run, Pallas kernels for 17% -> 11%
where the time goes in v1:
time: 189 us
  waiting for transfers between devices  87 us (46%)
  starting transfers between devices  57.6 us (30%)
  Pallas kernels  32.5 us (17%)
  other arithmetic  6.41 us (3%)
  local copies, waits for them, and re-layouts  3.91 us (2%)
    ppermute x24, waiting for transfers between devices, swap_dp(): return lax.ppermute(v, 'dp', [(i, i ^ bit) for i in range(n_dp)])  45.3 us
    pallas_call x31, Pallas kernels, call(): pl.pallas_call(body, in_specs=in_specs, out_specs=[pl.BlockSpec(memory_sp...  32.5 us
    ppermute x9, waiting for transfers between devices, swap_row(): return lax.ppermute(v, 'row', [(0, 1), (1, 0)])  32.1 us
    ppermute x24, starting transfers between devices, swap_dp(): return lax.ppermute(v, 'dp', [(i, i ^ bit) for i in range(n_dp)])  29.7 us
    ppermute x3, starting transfers between devices, diag_to_off_col(): return lax.ppermute(v, ('row', 'col'), [(0, 1), (3, 2)])  10.8 us
    ppermute x9, starting transfers between devices, swap_row(): return lax.ppermute(v, 'row', [(0, 1), (1, 0)])  9.49 us
    ppermute x2, waiting for transfers between devices, off_to_diag(): return lax.ppermute(v, ('row', 'col'), [(1, 3), (2, 0)])  5.92 us
  transfers between devices with their start and end apart: 46, of which 16 were waited for; matrix products, arithmetic and copies ran while one was open for 4% of the time, Pallas kernels for 11%

profile of v1, /device:TPU:0, one launch (start us, length us, event | category | flops | bytes accessed | tf_op | source)
XLA Modules:
  0.0 188.7 jit_solution(3786240520026640289)
XLA Ops:
  0.7 1.4 collective-permute-start.1
  2.1 6.5 %collective-permute-start = (f32[320,256]{1,0:T(8,128)}, f32[320,256]{1,0:T(8,128)}, u32[]{:S(2)}, u32[]{:S(2)}) collective-permute-start(f32[320,256]{1,0:T(8,128)} %bitcast.24), channel_id=1, source_target_pairs={{0,1},{3,2},{4,5},{7,6},{8,9},{11,10},{12,13},{15,14},{16,17},{19,... | collective-permute-start | bytes 983048 | tf_op jit(solution)/shard_map/ppermute | solution.py:451
  11.5 2.1 %collective-permute-start.4 = (bf16[320,768]{1,0:T(8,128)(2,1)S(1)}, bf16[320,768]{1,0:T(8,128)(2,1)}, u32[]{:S(2)}, u32[]{:S(2)}) collective-permute-start(bf16[320,768]{1,0:T(8,128)(2,1)S(1)} %pad_maximum_fusion.w_own), channel_id=1, source_target_pairs={{0,2},{2,0},{1,3},{3,1},{4,6},{6,4},{5,7},{7,5},{8,10},{10,8},{9,1... | collective-permute-start | bytes 1474568 | tf_op jit(solution)/shard_map/ppermute | solution.py:417
  17.2 2.0 %collective-permute-start.11 = (bf16[80,1536]{1,0:T(8,128)(2,1)}, bf16[80,1536]{1,0:T(8,128)(2,1)S(1)}, u32[]{:S(2)}, u32[]{:S(2)}) collective-permute-start(bf16[80,1536]{1,0:T(8,128)(2,1)} %pad_maximum_fusion.10), channel_id=1, source_target_pairs={{0,2},{2,0},{1,3},{3,1},{4,6},{6,4},{5,7},{7,5},{8,10},{10,8},{9,1... | collective-permute-start | bytes 737288 | tf_op jit(solution)/shard_map/ppermute | solution.py:417
  19.2 11.7 %collective-permute-done.8.refs_2_.refs_1_.refs_3_ = bf16[80,1536]{1,0:T(8,128)(2,1)S(1)} collective-permute-done((bf16[80,1536]{1,0:T(8,128)(2,1)S(1)}, bf16[80,1536]{1,0:T(8,128)(2,1)S(1)}, u32[]{:S(2)}, u32[]{:S(2)}) %collective-permute-start.8) | collective-permute-done | bytes 245792 | tf_op jit(solution)/shard_map/ppermute | solution.py:417
  30.9 1.3 collective-permute-start.9
  32.2 2.8 %collective-permute-start.2 = (f32[320,256]{1,0:T(8,128)}, f32[320,256]{1,0:T(8,128)}, u32[]{:S(2)}, u32[]{:S(2)}) collective-permute-start(f32[320,256]{1,0:T(8,128)} %collective-permute-done.1.x_diag), channel_id=1, source_target_pairs={{0,1},{3,2},{4,5},{7,6},{8,9},{11,10},{12,13},{15,14},{16,17},{19,... | collective-permute-start | bytes 983048 | tf_op jit(solution)/shard_map/ppermute | solution.py:451
  35.7 1.9 %collective-permute-start.12 = (bf16[80,1536]{1,0:T(8,128)(2,1)S(1)}, bf16[80,1536]{1,0:T(8,128)(2,1)S(1)}, u32[]{:S(2)}, u32[]{:S(2)}) collective-permute-start(bf16[80,1536]{1,0:T(8,128)(2,1)S(1)} %collective-permute-done.11.refs_5_.refs_4_.refs_6_), channel_id=1, source_target_pairs={{0,8},{4,12},{8,0},{12,4},{16,24},{20,28},{24,16},{28,20},{1,9},{5... | collective-permute-start | bytes 737288 | tf_op jit(solution)/shard_map/ppermute | solution.py:423
  39.3 2.1 %shard_map.271 = (f32[256,640]{1,0:T(8,128)S(1)}, bf16[256,640]{1,0:T(8,128)(2,1)S(1)}, f32[256,512]{1,0:T(8,128)S(1)}, f32[256,256]{1,0:T(8,128)S(1)}) custom-call(s32[8]{0:T(128)S(1)} %shift-right-arithmetic_and_fusion.sc, f32[320,256]{1,0:T(8,128)S(1)} %bitcast.25, f32[320,256]{1,0:T(8,128)} %collective-permute-done.x_own, ...), custom_call_target="tpu_custom_call" | custom-call | tf_op jit(solution)/shard_map/pallas_call | solution.py:66
  44.1 1.7 collective-permute-start.13
  45.8 1.9 %collective-permute-done.6.w_other = bf16[320,512]{1,0:T(8,128)(2,1)S(1)} collective-permute-done((bf16[320,512]{1,0:T(8,128)(2,1)}, bf16[320,512]{1,0:T(8,128)(2,1)S(1)}, u32[]{:S(2)}, u32[]{:S(2)}) %collective-permute-start.6) | collective-permute-done | bytes 327712 | tf_op jit(solution)/shard_map/ppermute | solution.py:417
  47.7 1.6 shard_map.272
  49.5 1.3 collective-permute-start.15
  50.8 5.9 %collective-permute-done.15.c_diag = bf16[320,256]{1,0:T(8,128)(2,1)S(1)} collective-permute-done((bf16[320,256]{1,0:T(8,128)(2,1)S(1)}, bf16[320,256]{1,0:T(8,128)(2,1)S(1)}, u32[]{:S(2)}, u32[]{:S(2)}) %collective-permute-start.15) | collective-permute-done | bytes 163872 | tf_op jit(solution)/shard_map/ppermute | solution.py:448
  56.7 1.5 collective-permute-start.16
  58.2 2.0 %shard_map.273 = (f32[256,640]{1,0:T(8,128)S(1)}, f32[256,640]{1,0:T(8,128)S(1)}, bf16[256,640]{1,0:T(8,128)(2,1)S(1)}, f32[256,1024]{1,0:T(8,128)S(1)}, f32[256...) custom-call(s32[8]{0:T(128)S(1)} %shift-right-arithmetic_and_fusion.sc, f32[256,640]{1,0:T(8,128)S(1)} %get-tuple-element.82.x, ...), custom_call_target="tpu_custom_call" | custom-call | tf_op jit(solution)/shard_map/pallas_call | solution.py:66
  60.2 1.2 shard_map.274
  63.2 1.6 shard_map.276
  64.7 3.8 %shard_map.277 = (bf16[2,160,1024]{2,1,0:T(8,128)(2,1)S(1)}, f32[2,160,1024]{2,1,0:T(8,128)S(1)}, bf16[2,160,1024]{2,1,0:T(8,128)(2,1)S(1)}, f32[2,160,1024]{2,1...) custom-call(s32[8]{0:T(128)S(1)} %shift-right-arithmetic_and_fusion.sc, ...), custom_call_target="tpu_custom_call" | custom-call | tf_op jit(solution)/shard_map/pallas_call | solution.py:66
  68.8 1.5 collective-permute-done.17.recv
  70.3 2.6 %shard_map.278 = (f32[256,640]{1,0:T(8,128)S(1)}, bf16[256,640]{1,0:T(8,128)(2,1)S(1)}, f32[1,640]{1,0:T(1,128)S(1)}, f32[1,640]{1,0:T(1,128)S(1)}, f32[256,256]...) custom-call(s32[8]{0:T(128)S(1)} %shift-right-arithmetic_and_fusion.sc, ...), custom_call_target="tpu_custom_call" | custom-call | tf_op jit(solution)/shard_map/pallas_call | solution.py:66
  73.1 1.4 collective-permute-done.18.kv_recv
  74.5 2.2 %shard_map.279 = (bf16[1,320,1408]{2,1,0:T(8,128)(2,1)S(1)}, f32[1,320,1408]{2,1,0:T(8,128)S(1)}, f32[256,640]{1,0:T(8,128)S(1)}, bf16[256,640]{1,0:T(8,128)(2,1)S(1)}) custom-call(s32[8]{0:T(128)S(1)} %shift-right-arithmetic_and_fusion.sc, f32[256,256]{1,0:T(8,128)S(1)} %get-tuple-element.104.kv_own, f32[256,256]{1,0:T(8,128)S(1)} %collective-permute-done.18.kv_recv, ...), custom_call_target="tpu_custom_call" | custom-call | tf_op jit(solution)/shard_map/pallas_call | solution.py:66
  77.1 1.9 %collective-permute-start.40 = (bf16[2,160,1024]{2,1,0:T(8,128)(2,1)S(1)}, bf16[2,160,1024]{2,1,0:T(8,128)(2,1)S(1)}, u32[]{:S(2)}, u32[]{:S(2)}) collective-permute-start(bf16[2,160,1024]{2,1,0:T(8,128)(2,1)S(1)} %get-tuple-element.143), channel_id=1, source_target_pairs={{0,8},{4,12},{8,0},{12,4},{16,24},{20,28},{24,16},{28,20},{1,9},{5... | collective-permute-start | bytes 1966088 | tf_op jit(solution)/shard_map/ppermute | solution.py:423
  80.4 18.4 %collective-permute-done.21.recv = bf16[1,320,1408]{2,1,0:T(8,128)(2,1)S(1)} collective-permute-done((bf16[1,320,1408]{2,1,0:T(8,128)(2,1)S(1)}, bf16[1,320,1408]{2,1,0:T(8,128)(2,1)S(1)}, u32[]{:S(2)}, u32[]{:S(2)}) %collective-permute-start.21) | collective-permute-done | bytes 901152 | tf_op jit(solution)/shard_map/ppermute | solution.py:417
  99.6 1.4 collective-permute-start.22
  101.0 10.2 %collective-permute-done.22.recv = bf16[1,160,1408]{2,1,0:T(8,128)(2,1)S(1)} collective-permute-done((bf16[1,160,1408]{2,1,0:T(8,128)(2,1)S(1)}, bf16[1,160,1408]{2,1,0:T(8,128)(2,1)S(1)}, u32[]{:S(2)}, u32[]{:S(2)}) %collective-permute-start.22) | collective-permute-done | bytes 450592 | tf_op jit(solution)/shard_map/ppermute | solution.py:423
  117.2 1.3 collective-permute-start.29
  118.7 2.7 %collective-permute-start.24 = (bf16[1,80,1408]{2,1,0:T(8,128)(2,1)S(1)}, bf16[1,80,1408]{2,1,0:T(8,128)(2,1)S(1)}, u32[]{:S(2)}, u32[]{:S(2)}) collective-permute-start(bf16[1,80,1408]{2,1,0:T(8,128)(2,1)S(1)} %shard_map.283.keep_in), channel_id=1, source_target_pairs={{0,16},{4,20},{8,24},{12,28},{16,0},{20,4},{24,8},{28,12},{1,17},{... | collective-permute-start | bytes 675848 | tf_op jit(solution)/shard_map/ppermute | solution.py:423
  121.4 2.8 %collective-permute-done.41.recv = bf16[2,80,1024]{2,1,0:T(8,128)(2,1)S(1)} collective-permute-done((bf16[2,80,1024]{2,1,0:T(8,128)(2,1)S(1)}, bf16[2,80,1024]{2,1,0:T(8,128)(2,1)S(1)}, u32[]{:S(2)}, u32[]{:S(2)}) %collective-permute-start.41) | collective-permute-done | bytes 327712 | tf_op jit(solution)/shard_map/ppermute | solution.py:423
  124.8 1.7 collective-permute-start.42
  126.4 2.1 %collective-permute-done.35.recv = bf16[2,80,1024]{2,1,0:T(8,128)(2,1)S(1)} collective-permute-done((bf16[2,80,1024]{2,1,0:T(8,128)(2,1)S(1)}, bf16[2,80,1024]{2,1,0:T(8,128)(2,1)S(1)}, u32[]{:S(2)}, u32[]{:S(2)}) %collective-permute-start.35) | collective-permute-done | bytes 327712 | tf_op jit(solution)/shard_map/ppermute | solution.py:423
  129.1 1.5 collective-permute-start.36
  132.9 2.7 %collective-permute-start.43 = (bf16[1,80,1024]{2,1,0:T(8,128)(2,1)S(1)}, bf16[1,80,1024]{2,1,0:T(8,128)(2,1)S(1)}, u32[]{:S(2)}, u32[]{:S(2)}) collective-permute-start(bf16[1,80,1024]{2,1,0:T(8,128)(2,1)S(1)} %shard_map.299.keep_in), channel_id=1, source_target_pairs={{0,16},{4,20},{8,24},{12,28},{16,0},{20,4},{24,8},{28,12},{1,17},{... | collective-permute-start | bytes 491528 | tf_op jit(solution)/shard_map/ppermute | solution.py:423
  135.6 2.3 %collective-permute-start.37 = (bf16[1,80,1024]{2,1,0:T(8,128)(2,1)S(1)}, bf16[1,80,1024]{2,1,0:T(8,128)(2,1)S(1)}, u32[]{:S(2)}, u32[]{:S(2)}) collective-permute-start(bf16[1,80,1024]{2,1,0:T(8,128)(2,1)S(1)} %shard_map.294.keep_in), channel_id=1, source_target_pairs={{0,16},{4,20},{8,24},{12,28},{16,0},{20,4},{24,8},{28,12},{1,17},{... | collective-permute-start | bytes 491528 | tf_op jit(solution)/shard_map/ppermute | solution.py:423
  138.4 1.7 collective-permute-start.31
  140.1 9.0 %collective-permute-done.43.recv = bf16[1,80,1024]{2,1,0:T(8,128)(2,1)S(1)} collective-permute-done((bf16[1,80,1024]{2,1,0:T(8,128)(2,1)S(1)}, bf16[1,80,1024]{2,1,0:T(8,128)(2,1)S(1)}, u32[]{:S(2)}, u32[]{:S(2)}) %collective-permute-start.43) | collective-permute-done | bytes 163872 | tf_op jit(solution)/shard_map/ppermute | solution.py:423
  149.2 3.4 %collective-permute-done.37.recv = bf16[1,80,1024]{2,1,0:T(8,128)(2,1)S(1)} collective-permute-done((bf16[1,80,1024]{2,1,0:T(8,128)(2,1)S(1)}, bf16[1,80,1024]{2,1,0:T(8,128)(2,1)S(1)}, u32[]{:S(2)}, u32[]{:S(2)}) %collective-permute-start.37) | collective-permute-done | bytes 163872 | tf_op jit(solution)/shard_map/ppermute | solution.py:423
  152.8 2.1 %collective-permute-start.26 = (bf16[2,80,1408]{2,1,0:T(8,128)(2,1)S(1)}, bf16[2,80,1408]{2,1,0:T(8,128)(2,1)S(1)}, u32[]{:S(2)}, u32[]{:S(2)}) collective-permute-start(bf16[2,80,1408]{2,1,0:T(8,128)(2,1)S(1)} %pad_maximum_fusion.3.near), channel_id=1, source_target_pairs={{0,8},{4,12},{8,0},{12,4},{16,24},{20,28},{24,16},{28,20},{1,9},{5... | collective-permute-start | bytes 1351688 | tf_op jit(solution)/shard_map/ppermute | solution.py:423
  154.9 3.3 %collective-permute-start.20 = (bf16[640,256]{1,0:T(8,128)(2,1)S(1)}, bf16[640,256]{1,0:T(8,128)(2,1)S(1)}, u32[]{:S(2)}, u32[]{:S(2)}) collective-permute-start(bf16[640,256]{1,0:T(8,128)(2,1)S(1)} %pad_maximum_fusion.5), channel_id=1, source_target_pairs={{0,2},{3,1},{4,6},{7,5},{8,10},{11,9},{12,14},{15,13},{16,18},{19,... | collective-permute-start | bytes 983048 | tf_op jit(solution)/shard_map/ppermute | solution.py:454
  159.1 2.4 %collective-permute-done.38 = bf16[1,80,1024]{2,1,0:T(8,128)(2,1)S(1)} collective-permute-done((bf16[1,80,1024]{2,1,0:T(8,128)(2,1)S(1)}, bf16[1,80,1024]{2,1,0:T(8,128)(2,1)S(1)}, u32[]{:S(2)}, u32[]{:S(2)}) %collective-permute-start.38) | collective-permute-done | bytes 163872 | tf_op jit(solution)/shard_map/ppermute | solution.py:423
  162.6 12.0 %collective-permute-done.32 = bf16[1,80,1024]{2,1,0:T(8,128)(2,1)S(1)} collective-permute-done((bf16[1,80,1024]{2,1,0:T(8,128)(2,1)S(1)}, bf16[1,80,1024]{2,1,0:T(8,128)(2,1)S(1)}, u32[]{:S(2)}, u32[]{:S(2)}) %collective-permute-start.32) | collective-permute-done | bytes 163872 | tf_op jit(solution)/shard_map/ppermute | solution.py:423
  175.8 1.7 shard_map.285
  178.4 1.7 shard_map.301
  180.1 1.7 shard_map.296
  181.8 2.6 %collective-permute-done.33.far = bf16[2,80,1024]{2,1,0:T(8,128)(2,1)S(1)} collective-permute-done((bf16[2,80,1024]{2,1,0:T(8,128)(2,1)S(1)}, bf16[2,80,1024]{2,1,0:T(8,128)(2,1)S(1)}, u32[]{:S(2)}, u32[]{:S(2)}) %collective-permute-start.33) | collective-permute-done | bytes 327712 | tf_op jit(solution)/shard_map/ppermute | solution.py:423
  184.3 1.7 shard_map.291
  186.0 1.5 shard_map.286
  (127 shorter events, 31.8 us)
Async XLA Ops:
  0.6 12.9 %copy-start = (bf16[1024,320]{0,1:T(8,128)(2,1)S(1)}, bf16[1024,320]{0,1:T(8,128)(2,1)}, u32[]{:S(2)}) copy-start(bf16[1024,320]{0,1:T(8,128)(2,1)} %param.24) | copy-start | bytes 1966084
  0.7 31.6 %collective-permute-start.1 = (f32[320,256]{1,0:T(8,128)}, f32[320,256]{1,0:T(8,128)}, u32[]{:S(2)}, u32[]{:S(2)}) collective-permute-start(f32[320,256]{1,0:T(8,128)} %bitcast.23), channel_id=1, source_target_pairs={{1,3},{2,0},{5,7},{6,4},{9,11},{10,8},{13,15},{14,12},{17,19},{18,... | collective-permute-start | bytes 983048 | tf_op jit(solution)/shard_map/ppermute | solution.py:448
  2.1 35.6 %collective-permute-start = (f32[320,256]{1,0:T(8,128)}, f32[320,256]{1,0:T(8,128)}, u32[]{:S(2)}, u32[]{:S(2)}) collective-permute-start(f32[320,256]{1,0:T(8,128)} %bitcast.24), channel_id=1, source_target_pairs={{0,1},{3,2},{4,5},{7,6},{8,9},{11,10},{12,13},{15,14},{16,17},{19,... | collective-permute-start | bytes 983048 | tf_op jit(solution)/shard_map/ppermute | solution.py:451
  9.4 7.8 %collective-permute-start.3 = (f32[4,320]{1,0:T(4,128)S(1)}, f32[4,320]{1,0:T(4,128)S(1)}, u32[]{:S(2)}, u32[]{:S(2)}) collective-permute-start(f32[4,320]{1,0:T(4,128)S(1)} %select_select_fusion), channel_id=1, source_target_pairs={{0,2},{2,0},{1,3},{3,1},{4,6},{6,4},{5,7},{7,5},{8,10},{10,8},{9,1... | collective-permute-start | bytes 15368 | tf_op jit(solution)/shard_map/ppermute | solution.py:417
  11.5 26.9 %collective-permute-start.4 = (bf16[320,768]{1,0:T(8,128)(2,1)S(1)}, bf16[320,768]{1,0:T(8,128)(2,1)}, u32[]{:S(2)}, u32[]{:S(2)}) collective-permute-start(bf16[320,768]{1,0:T(8,128)(2,1)S(1)} %pad_maximum_fusion.w_own), channel_id=1, source_target_pairs={{0,2},{2,0},{1,3},{3,1},{4,6},{6,4},{5,7},{7,5},{8,10},{10,8},{9,1... | collective-permute-start | bytes 1474568 | tf_op jit(solution)/shard_map/ppermute | solution.py:417
  15.3 15.6 %collective-permute-start.8 = (bf16[80,1536]{1,0:T(8,128)(2,1)S(1)}, bf16[80,1536]{1,0:T(8,128)(2,1)S(1)}, u32[]{:S(2)}, u32[]{:S(2)}) collective-permute-start(bf16[80,1536]{1,0:T(8,128)(2,1)S(1)} %pad_maximum_fusion.9), channel_id=1, source_target_pairs={{0,2},{2,0},{1,3},{3,1},{4,6},{6,4},{5,7},{7,5},{8,10},{10,8},{9,1... | collective-permute-start | bytes 737288 | tf_op jit(solution)/shard_map/ppermute | solution.py:417
  17.2 18.5 %collective-permute-start.11 = (bf16[80,1536]{1,0:T(8,128)(2,1)}, bf16[80,1536]{1,0:T(8,128)(2,1)S(1)}, u32[]{:S(2)}, u32[]{:S(2)}) collective-permute-start(bf16[80,1536]{1,0:T(8,128)(2,1)} %pad_maximum_fusion.10), channel_id=1, source_target_pairs={{0,2},{2,0},{1,3},{3,1},{4,6},{6,4},{5,7},{7,5},{8,10},{10,8},{9,1... | collective-permute-start | bytes 737288 | tf_op jit(solution)/shard_map/ppermute | solution.py:417
  30.9 11.6 %collective-permute-start.9 = (bf16[80,1536]{1,0:T(8,128)(2,1)S(1)}, bf16[80,1536]{1,0:T(8,128)(2,1)S(1)}, u32[]{:S(2)}, u32[]{:S(2)}) collective-permute-start(bf16[80,1536]{1,0:T(8,128)(2,1)S(1)} %collective-permute-done.8.refs_2_.refs_1_.refs_3_), channel_id=1, source_target_pairs={{0,4},{4,0},{8,12},{12,8},{16,20},{20,16},{24,28},{28,24},{1,5},{5... | collective-permute-start | bytes 737288 | tf_op jit(solution)/shard_map/ppermute | solution.py:423
  32.2 6.1 %collective-permute-start.2 = (f32[320,256]{1,0:T(8,128)}, f32[320,256]{1,0:T(8,128)}, u32[]{:S(2)}, u32[]{:S(2)}) collective-permute-start(f32[320,256]{1,0:T(8,128)} %collective-permute-done.1.x_diag), channel_id=1, source_target_pairs={{0,1},{3,2},{4,5},{7,6},{8,9},{11,10},{12,13},{15,14},{16,17},{19,... | collective-permute-start | bytes 983048 | tf_op jit(solution)/shard_map/ppermute | solution.py:451
  35.7 8.3 %collective-permute-start.12 = (bf16[80,1536]{1,0:T(8,128)(2,1)S(1)}, bf16[80,1536]{1,0:T(8,128)(2,1)S(1)}, u32[]{:S(2)}, u32[]{:S(2)}) collective-permute-start(bf16[80,1536]{1,0:T(8,128)(2,1)S(1)} %collective-permute-done.11.refs_5_.refs_4_.refs_6_), channel_id=1, source_target_pairs={{0,8},{4,12},{8,0},{12,4},{16,24},{20,28},{24,16},{28,20},{1,9},{5... | collective-permute-start | bytes 737288 | tf_op jit(solution)/shard_map/ppermute | solution.py:423
  37.7 10.0 %collective-permute-start.6 = (bf16[320,512]{1,0:T(8,128)(2,1)}, bf16[320,512]{1,0:T(8,128)(2,1)S(1)}, u32[]{:S(2)}, u32[]{:S(2)}) collective-permute-start(bf16[320,512]{1,0:T(8,128)(2,1)} %bitcast.19), channel_id=1, source_target_pairs={{0,2},{2,0},{1,3},{3,1},{4,6},{6,4},{5,7},{7,5},{8,10},{10,8},{9,1... | collective-permute-start | bytes 983048 | tf_op jit(solution)/shard_map/ppermute | solution.py:417
  41.5 6.2 %copy-start.3 = (bf16[512,320]{0,1:T(8,128)(2,1)S(1)}, bf16[512,320]{0,1:T(8,128)(2,1)}, u32[]{:S(2)}) copy-start(bf16[512,320]{0,1:T(8,128)(2,1)} %param.21) | copy-start | bytes 983044
  41.5 6.2 %collective-permute-start.5 = (f32[256,256]{1,0:T(8,128)S(1)}, f32[256,256]{1,0:T(8,128)S(1)}, u32[]{:S(2)}, u32[]{:S(2)}) collective-permute-start(f32[256,256]{1,0:T(8,128)S(1)} %get-tuple-element.84.kv_mine.kv_raw), channel_id=1, source_target_pairs={{0,1},{1,0},{2,3},{3,2},{4,5},{5,4},{6,7},{7,6},{8,9},{9,8},{10,11... | collective-permute-start | bytes 786440 | tf_op jit(solution)/shard_map/ppermute | solution.py:420
  42.6 15.6 %collective-permute-start.10 = (bf16[160,1536]{1,0:T(8,128)(2,1)S(1)}, bf16[160,1536]{1,0:T(8,128)(2,1)S(1)}, u32[]{:S(2)}, u32[]{:S(2)}) collective-permute-start(bf16[160,1536]{1,0:T(8,128)(2,1)S(1)} %pad_maximum_fusion.1), channel_id=1, source_target_pairs={{0,8},{4,12},{8,0},{12,4},{16,24},{20,28},{24,16},{28,20},{1,9},{5... | collective-permute-start | bytes 1474568 | tf_op jit(solution)/shard_map/ppermute | solution.py:423
  44.1 14.2 %collective-permute-start.13 = (bf16[160,1536]{1,0:T(8,128)(2,1)S(1)}, bf16[160,1536]{1,0:T(8,128)(2,1)S(1)}, u32[]{:S(2)}, u32[]{:S(2)}) collective-permute-start(bf16[160,1536]{1,0:T(8,128)(2,1)S(1)} %pad_maximum_fusion.2), channel_id=1, source_target_pairs={{0,4},{4,0},{8,12},{12,8},{16,20},{20,16},{24,28},{28,24},{1,5},{5... | collective-permute-start | bytes 1474568 | tf_op jit(solution)/shard_map/ppermute | solution.py:423
  49.3 8.9 %collective-permute-start.7 = (bf16[256,640]{1,0:T(8,128)(2,1)S(1)}, bf16[256,640]{1,0:T(8,128)(2,1)S(1)}, u32[]{:S(2)}, u32[]{:S(2)}) collective-permute-start(bf16[256,640]{1,0:T(8,128)(2,1)S(1)} %get-tuple-element.86), channel_id=1, source_target_pairs={{0,1},{1,0},{2,3},{3,2},{4,5},{5,4},{6,7},{7,6},{8,9},{9,8},{10,11... | collective-permute-start | bytes 983048 | tf_op jit(solution)/shard_map/ppermute | solution.py:420
  49.5 7.2 %collective-permute-start.15 = (bf16[320,256]{1,0:T(8,128)(2,1)S(1)}, bf16[320,256]{1,0:T(8,128)(2,1)S(1)}, u32[]{:S(2)}, u32[]{:S(2)}) collective-permute-start(bf16[320,256]{1,0:T(8,128)(2,1)S(1)} %bitcast_convert_fusion), channel_id=1, source_target_pairs={{1,3},{2,0},{5,7},{6,4},{9,11},{10,8},{13,15},{14,12},{17,19},{18,... | collective-permute-start | bytes 491528 | tf_op jit(solution)/shard_map/ppermute | solution.py:448
  56.7 4.8 %collective-permute-start.16 = (bf16[640,256]{1,0:T(8,128)(2,1)S(1)}, bf16[640,256]{1,0:T(8,128)(2,1)S(1)}, u32[]{:S(2)}, u32[]{:S(2)}) collective-permute-start(bf16[640,256]{1,0:T(8,128)(2,1)S(1)} %pad_maximum_fusion.4), channel_id=1, source_target_pairs={{0,1},{3,2},{4,5},{7,6},{8,9},{11,10},{12,13},{15,14},{16,17},{19,... | collective-permute-start | bytes 983048 | tf_op jit(solution)/shard_map/ppermute | solution.py:451
  61.5 1.7 collective-permute-start.14
  68.6 1.7 collective-permute-start.17
  72.9 1.6 collective-permute-start.18
  76.7 22.1 %collective-permute-start.21 = (bf16[1,320,1408]{2,1,0:T(8,128)(2,1)S(1)}, bf16[1,320,1408]{2,1,0:T(8,128)(2,1)S(1)}, u32[]{:S(2)}, u32[]{:S(2)}) collective-permute-start(bf16[1,320,1408]{2,1,0:T(8,128)(2,1)S(1)} %get-tuple-element.120), channel_id=1, source_target_pairs={{0,2},{2,0},{1,3},{3,1},{4,6},{6,4},{5,7},{7,5},{8,10},{10,8},{9,1... | collective-permute-start | bytes 2703368 | tf_op jit(solution)/shard_map/ppermute | solution.py:417
  77.1 35.6 %collective-permute-start.40 = (bf16[2,160,1024]{2,1,0:T(8,128)(2,1)S(1)}, bf16[2,160,1024]{2,1,0:T(8,128)(2,1)S(1)}, u32[]{:S(2)}, u32[]{:S(2)}) collective-permute-start(bf16[2,160,1024]{2,1,0:T(8,128)(2,1)S(1)} %get-tuple-element.143), channel_id=1, source_target_pairs={{0,8},{4,12},{8,0},{12,4},{16,24},{20,28},{24,16},{28,20},{1,9},{5... | collective-permute-start | bytes 1966088 | tf_op jit(solution)/shard_map/ppermute | solution.py:423
  79.1 35.6 %collective-permute-start.34 = (bf16[2,160,1024]{2,1,0:T(8,128)(2,1)S(1)}, bf16[2,160,1024]{2,1,0:T(8,128)(2,1)S(1)}, u32[]{:S(2)}, u32[]{:S(2)}) collective-permute-start(bf16[2,160,1024]{2,1,0:T(8,128)(2,1)S(1)} %get-tuple-element.137), channel_id=1, source_target_pairs={{0,8},{4,12},{8,0},{12,4},{16,24},{20,28},{24,16},{28,20},{1,9},{5... | collective-permute-start | bytes 1966088 | tf_op jit(solution)/shard_map/ppermute | solution.py:423
  79.2 37.3 %collective-permute-start.28 = (bf16[2,160,1024]{2,1,0:T(8,128)(2,1)S(1)}, bf16[2,160,1024]{2,1,0:T(8,128)(2,1)S(1)}, u32[]{:S(2)}, u32[]{:S(2)}) collective-permute-start(bf16[2,160,1024]{2,1,0:T(8,128)(2,1)S(1)} %get-tuple-element.131), channel_id=1, source_target_pairs={{0,4},{4,0},{8,12},{12,8},{16,20},{20,16},{24,28},{28,24},{1,5},{5... | collective-permute-start | bytes 1966088 | tf_op jit(solution)/shard_map/ppermute | solution.py:423
  99.6 11.6 %collective-permute-start.22 = (bf16[1,160,1408]{2,1,0:T(8,128)(2,1)S(1)}, bf16[1,160,1408]{2,1,0:T(8,128)(2,1)S(1)}, u32[]{:S(2)}, u32[]{:S(2)}) collective-permute-start(bf16[1,160,1408]{2,1,0:T(8,128)(2,1)S(1)} %get-tuple-element.122), channel_id=1, source_target_pairs={{0,4},{4,0},{8,12},{12,8},{16,20},{20,16},{24,28},{28,24},{1,5},{5... | collective-permute-start | bytes 1351688 | tf_op jit(solution)/shard_map/ppermute | solution.py:423
  111.9 6.7 %collective-permute-start.23 = (bf16[1,80,1408]{2,1,0:T(8,128)(2,1)S(1)}, bf16[1,80,1408]{2,1,0:T(8,128)(2,1)S(1)}, u32[]{:S(2)}, u32[]{:S(2)}) collective-permute-start(bf16[1,80,1408]{2,1,0:T(8,128)(2,1)S(1)} %get-tuple-element.124), channel_id=1, source_target_pairs={{0,8},{4,12},{8,0},{12,4},{16,24},{20,28},{24,16},{28,20},{1,9},{5... | collective-permute-start | bytes 675848 | tf_op jit(solution)/shard_map/ppermute | solution.py:423
  113.5 10.6 %collective-permute-start.41 = (bf16[2,80,1024]{2,1,0:T(8,128)(2,1)S(1)}, bf16[2,80,1024]{2,1,0:T(8,128)(2,1)S(1)}, u32[]{:S(2)}, u32[]{:S(2)}) collective-permute-start(bf16[2,80,1024]{2,1,0:T(8,128)(2,1)S(1)} %get-tuple-element.145), channel_id=1, source_target_pairs={{0,4},{4,0},{8,12},{12,8},{16,20},{20,16},{24,28},{28,24},{1,5},{5... | collective-permute-start | bytes 983048 | tf_op jit(solution)/shard_map/ppermute | solution.py:423
  115.4 13.1 %collective-permute-start.35 = (bf16[2,80,1024]{2,1,0:T(8,128)(2,1)S(1)}, bf16[2,80,1024]{2,1,0:T(8,128)(2,1)S(1)}, u32[]{:S(2)}, u32[]{:S(2)}) collective-permute-start(bf16[2,80,1024]{2,1,0:T(8,128)(2,1)S(1)} %get-tuple-element.139), channel_id=1, source_target_pairs={{0,4},{4,0},{8,12},{12,8},{16,20},{20,16},{24,28},{28,24},{1,5},{5... | collective-permute-start | bytes 983048 | tf_op jit(solution)/shard_map/ppermute | solution.py:423
  117.2 14.1 %collective-permute-start.29 = (bf16[2,80,1024]{2,1,0:T(8,128)(2,1)S(1)}, bf16[2,80,1024]{2,1,0:T(8,128)(2,1)S(1)}, u32[]{:S(2)}, u32[]{:S(2)}) collective-permute-start(bf16[2,80,1024]{2,1,0:T(8,128)(2,1)S(1)} %get-tuple-element.133), channel_id=1, source_target_pairs={{0,8},{4,12},{8,0},{12,4},{16,24},{20,28},{24,16},{28,20},{1,9},{5... | collective-permute-start | bytes 983048 | tf_op jit(solution)/shard_map/ppermute | solution.py:423
  118.7 12.0 %collective-permute-start.24 = (bf16[1,80,1408]{2,1,0:T(8,128)(2,1)S(1)}, bf16[1,80,1408]{2,1,0:T(8,128)(2,1)S(1)}, u32[]{:S(2)}, u32[]{:S(2)}) collective-permute-start(bf16[1,80,1408]{2,1,0:T(8,128)(2,1)S(1)} %shard_map.283.keep_in), channel_id=1, source_target_pairs={{0,16},{4,20},{8,24},{12,28},{16,0},{20,4},{24,8},{28,12},{1,17},{... | collective-permute-start | bytes 675848 | tf_op jit(solution)/shard_map/ppermute | solution.py:423
  121.4 16.6 %collective-permute-start.19 = (bf16[256,640]{1,0:T(8,128)(2,1)S(1)}, bf16[256,640]{1,0:T(8,128)(2,1)S(1)}, u32[]{:S(2)}, u32[]{:S(2)}) collective-permute-start(bf16[256,640]{1,0:T(8,128)(2,1)S(1)} %get-tuple-element.115), channel_id=1, source_target_pairs={{0,1},{1,0},{2,3},{3,2},{4,5},{5,4},{6,7},{7,6},{8,9},{9,8},{10,11... | collective-permute-start | bytes 983048 | tf_op jit(solution)/shard_map/ppermute | solution.py:420
  124.8 8.1 %collective-permute-start.42 = (bf16[1,80,1024]{2,1,0:T(8,128)(2,1)S(1)}, bf16[1,80,1024]{2,1,0:T(8,128)(2,1)S(1)}, u32[]{:S(2)}, u32[]{:S(2)}) collective-permute-start(bf16[1,80,1024]{2,1,0:T(8,128)(2,1)S(1)} %get-tuple-element.147), channel_id=1, source_target_pairs={{0,2},{2,0},{1,3},{3,1},{4,6},{6,4},{5,7},{7,5},{8,10},{10,8},{9,1... | collective-permute-start | bytes 491528 | tf_op jit(solution)/shard_map/ppermute | solution.py:417
  129.1 6.5 %collective-permute-start.36 = (bf16[1,80,1024]{2,1,0:T(8,128)(2,1)S(1)}, bf16[1,80,1024]{2,1,0:T(8,128)(2,1)S(1)}, u32[]{:S(2)}, u32[]{:S(2)}) collective-permute-start(bf16[1,80,1024]{2,1,0:T(8,128)(2,1)S(1)} %get-tuple-element.141), channel_id=1, source_target_pairs={{0,2},{2,0},{1,3},{3,1},{4,6},{6,4},{5,7},{7,5},{8,10},{10,8},{9,1... | collective-permute-start | bytes 491528 | tf_op jit(solution)/shard_map/ppermute | solution.py:417
  130.7 22.0 %collective-permute-start.25 = (bf16[1,80,1408]{2,1,0:T(8,128)(2,1)S(1)}, bf16[1,80,1408]{2,1,0:T(8,128)(2,1)S(1)}, u32[]{:S(2)}, u32[]{:S(2)}) collective-permute-start(bf16[1,80,1408]{2,1,0:T(8,128)(2,1)S(1)} %shard_map.284), channel_id=1, source_target_pairs={{0,4},{4,0},{8,12},{12,8},{16,20},{20,16},{24,28},{28,24},{1,5},{5... | collective-permute-start | bytes 675848 | tf_op jit(solution)/shard_map/ppermute | solution.py:423
  132.0 6.4 %collective-permute-start.30 = (bf16[1,80,1024]{2,1,0:T(8,128)(2,1)S(1)}, bf16[1,80,1024]{2,1,0:T(8,128)(2,1)S(1)}, u32[]{:S(2)}, u32[]{:S(2)}) collective-permute-start(bf16[1,80,1024]{2,1,0:T(8,128)(2,1)S(1)} %get-tuple-element.135), channel_id=1, source_target_pairs={{0,2},{2,0},{1,3},{3,1},{4,6},{6,4},{5,7},{7,5},{8,10},{10,8},{9,1... | collective-permute-start | bytes 491528 | tf_op jit(solution)/shard_map/ppermute | solution.py:417
  132.9 16.1 %collective-permute-start.43 = (bf16[1,80,1024]{2,1,0:T(8,128)(2,1)S(1)}, bf16[1,80,1024]{2,1,0:T(8,128)(2,1)S(1)}, u32[]{:S(2)}, u32[]{:S(2)}) collective-permute-start(bf16[1,80,1024]{2,1,0:T(8,128)(2,1)S(1)} %shard_map.299.keep_in), channel_id=1, source_target_pairs={{0,16},{4,20},{8,24},{12,28},{16,0},{20,4},{24,8},{28,12},{1,17},{... | collective-permute-start | bytes 491528 | tf_op jit(solution)/shard_map/ppermute | solution.py:423
  135.6 16.9 %collective-permute-start.37 = (bf16[1,80,1024]{2,1,0:T(8,128)(2,1)S(1)}, bf16[1,80,1024]{2,1,0:T(8,128)(2,1)S(1)}, u32[]{:S(2)}, u32[]{:S(2)}) collective-permute-start(bf16[1,80,1024]{2,1,0:T(8,128)(2,1)S(1)} %shard_map.294.keep_in), channel_id=1, source_target_pairs={{0,16},{4,20},{8,24},{12,28},{16,0},{20,4},{24,8},{28,12},{1,17},{... | collective-permute-start | bytes 491528 | tf_op jit(solution)/shard_map/ppermute | solution.py:423
  138.4 19.8 %collective-permute-start.31 = (bf16[1,80,1024]{2,1,0:T(8,128)(2,1)S(1)}, bf16[1,80,1024]{2,1,0:T(8,128)(2,1)S(1)}, u32[]{:S(2)}, u32[]{:S(2)}) collective-permute-start(bf16[1,80,1024]{2,1,0:T(8,128)(2,1)S(1)} %shard_map.289.keep_in), channel_id=1, source_target_pairs={{0,16},{4,20},{8,24},{12,28},{16,0},{20,4},{24,8},{28,12},{1,17},{... | collective-permute-start | bytes 491528 | tf_op jit(solution)/shard_map/ppermute | solution.py:423
  149.1 9.2 %collective-permute-start.44 = (bf16[1,80,1024]{2,1,0:T(8,128)(2,1)S(1)}, bf16[1,80,1024]{2,1,0:T(8,128)(2,1)S(1)}, u32[]{:S(2)}, u32[]{:S(2)}) collective-permute-start(bf16[1,80,1024]{2,1,0:T(8,128)(2,1)S(1)} %shard_map.300), channel_id=1, source_target_pairs={{0,8},{4,12},{8,0},{12,4},{16,24},{20,28},{24,16},{28,20},{1,9},{5... | collective-permute-start | bytes 491528 | tf_op jit(solution)/shard_map/ppermute | solution.py:423
  152.6 8.9 %collective-permute-start.38 = (bf16[1,80,1024]{2,1,0:T(8,128)(2,1)S(1)}, bf16[1,80,1024]{2,1,0:T(8,128)(2,1)S(1)}, u32[]{:S(2)}, u32[]{:S(2)}) collective-permute-start(bf16[1,80,1024]{2,1,0:T(8,128)(2,1)S(1)} %shard_map.295), channel_id=1, source_target_pairs={{0,8},{4,12},{8,0},{12,4},{16,24},{20,28},{24,16},{28,20},{1,9},{5... | collective-permute-start | bytes 491528 | tf_op jit(solution)/shard_map/ppermute | solution.py:423
  152.8 23.0 %collective-permute-start.26 = (bf16[2,80,1408]{2,1,0:T(8,128)(2,1)S(1)}, bf16[2,80,1408]{2,1,0:T(8,128)(2,1)S(1)}, u32[]{:S(2)}, u32[]{:S(2)}) collective-permute-start(bf16[2,80,1408]{2,1,0:T(8,128)(2,1)S(1)} %pad_maximum_fusion.3.near), channel_id=1, source_target_pairs={{0,8},{4,12},{8,0},{12,4},{16,24},{20,28},{24,16},{28,20},{1,9},{5... | collective-permute-start | bytes 1351688 | tf_op jit(solution)/shard_map/ppermute | solution.py:423
  154.9 20.9 %collective-permute-start.20 = (bf16[640,256]{1,0:T(8,128)(2,1)S(1)}, bf16[640,256]{1,0:T(8,128)(2,1)S(1)}, u32[]{:S(2)}, u32[]{:S(2)}) collective-permute-start(bf16[640,256]{1,0:T(8,128)(2,1)S(1)} %pad_maximum_fusion.5), channel_id=1, source_target_pairs={{0,2},{3,1},{4,6},{7,5},{8,10},{11,9},{12,14},{15,13},{16,18},{19,... | collective-permute-start | bytes 983048 | tf_op jit(solution)/shard_map/ppermute | solution.py:454
  158.2 16.4 %collective-permute-start.32 = (bf16[1,80,1024]{2,1,0:T(8,128)(2,1)S(1)}, bf16[1,80,1024]{2,1,0:T(8,128)(2,1)S(1)}, u32[]{:S(2)}, u32[]{:S(2)}) collective-permute-start(bf16[1,80,1024]{2,1,0:T(8,128)(2,1)S(1)} %shard_map.290), channel_id=1, source_target_pairs={{0,8},{4,12},{8,0},{12,4},{16,24},{20,28},{24,16},{28,20},{1,9},{5... | collective-permute-start | bytes 491528 | tf_op jit(solution)/shard_map/ppermute | solution.py:423
  158.3 20.1 %collective-permute-start.45 = (bf16[2,80,1024]{2,1,0:T(8,128)(2,1)S(1)}, bf16[2,80,1024]{2,1,0:T(8,128)(2,1)S(1)}, u32[]{:S(2)}, u32[]{:S(2)}) collective-permute-start(bf16[2,80,1024]{2,1,0:T(8,128)(2,1)S(1)} %pad_maximum_fusion.8.near), channel_id=1, source_target_pairs={{0,4},{4,0},{8,12},{12,8},{16,20},{20,16},{24,28},{28,24},{1,5},{5... | collective-permute-start | bytes 983048 | tf_op jit(solution)/shard_map/ppermute | solution.py:423
  161.6 18.5 %collective-permute-start.39 = (bf16[2,80,1024]{2,1,0:T(8,128)(2,1)S(1)}, bf16[2,80,1024]{2,1,0:T(8,128)(2,1)S(1)}, u32[]{:S(2)}, u32[]{:S(2)}) collective-permute-start(bf16[2,80,1024]{2,1,0:T(8,128)(2,1)S(1)} %pad_maximum_fusion.7.near), channel_id=1, source_target_pairs={{0,4},{4,0},{8,12},{12,8},{16,20},{20,16},{24,28},{28,24},{1,5},{5... | collective-permute-start | bytes 983048 | tf_op jit(solution)/shard_map/ppermute | solution.py:423
  174.6 9.7 %collective-permute-start.33 = (bf16[2,80,1024]{2,1,0:T(8,128)(2,1)S(1)}, bf16[2,80,1024]{2,1,0:T(8,128)(2,1)S(1)}, u32[]{:S(2)}, u32[]{:S(2)}) collective-permute-start(bf16[2,80,1024]{2,1,0:T(8,128)(2,1)S(1)} %pad_maximum_fusion.6.near), channel_id=1, source_target_pairs={{0,4},{4,0},{8,12},{12,8},{16,20},{20,16},{24,28},{28,24},{1,5},{5... | collective-permute-start | bytes 983048 | tf_op jit(solution)/shard_map/ppermute | solution.py:423
  177.5 8.6 %collective-permute-start.27 = (bf16[320,384]{1,0:T(8,128)(2,1)S(1)}, bf16[320,384]{1,0:T(8,128)(2,1)S(1)}, u32[]{:S(2)}, u32[]{:S(2)}) collective-permute-start(bf16[320,384]{1,0:T(8,128)(2,1)S(1)} %get-tuple-element.126.own), channel_id=1, source_target_pairs={{0,1},{1,0},{2,3},{3,2},{4,5},{5,4},{6,7},{7,6},{8,9},{9,8},{10,11... | collective-permute-start | bytes 737288 | tf_op jit(solution)/shard_map/ppermute | solution.py:420
  (8 other events, 36.6 us)

commit v2 on v1

--- a/solution.py
+++ b/solution.py
@@ -15,12 +15,13 @@
 
 
 PLAN = {
-    "down": (2, 1, "y", 4),
-    "gate": (1, 2, "y", 4),
-    "up": (2, 1, "y", 4),
-    "attn": ("y", 1, 2, 4),
+    "down": ("y", 2, 1, 4),
+    "gate": (2, 1, "y", 4),
+    "up": (1, 2, "y", 4),
+    "out": ("y", 2, 1, 4),
+    "qkv": ("y", 2, 1, 4),
 }
-GATHER = {"down": (2, 1), "gate": (2, 1), "up": (2, 1), "attn": (1, 2)}
+GATHER = {"down": (2, 1), "gate": (1, 2), "up": (2, 1), "out": (2, 1), "qkv": (1, 2)}
 TOP_BITS = (1, 2, 4)
 
 
@@ -131,6 +132,12 @@
 def cot_body(sc, c_local, c_diag, c_off, cot):
     here = jnp.concatenate([c_local[...], c_diag[...].astype(f32)], axis=0)
     cot[...] = jnp.where(sc[3] == 1, here, c_off[...].astype(f32)).T
+
+
+def cot_send_body(own, other, _, send):
+    half = own.shape[0]
+    send[:half, :] = own[...]
+    send[half:, :] = other[...]
 
 
 def attn_body(sc, raw_q, kv_mine, kv_theirs, mask, cos, sin, gq, gk, w_own, w_other, q, k, v,
@@ -306,8 +313,8 @@
 
 
 def attn_grad_body(sc, own, recv, mid, proj, cot, g, w_own, w_other, q, k, v, probs, raw_q, cos,
-                   sin, gq, grad_mid, grad_attn, pre_part, attn_part, kv_own, kv_send, grad_q,
-                   q_part, w):
+                   sin, gq, heads, grad_mid, pre_part, attn_part, kv_own, kv_send, grad_q,
+                   q_part, out_send, out_keep, w, acc):
     join_rows(w, w_own, w_other)
     up = own[...] + recv[...].astype(f32)
     m = mid[...]
@@ -319,7 +326,7 @@
     through, part = norm_back(gm, y, rms_scale(y), g[1:2, :])
     attn_part[...] = part
     ga = through.astype(bf16)
-    grad_attn[...] = ga
+    split_grad(sc, ga.T, heads[...], out_send, out_keep, acc, PLAN["out"][0])
     grad_heads = dot(ga, w[...]).astype(bf16)
     hd = k.shape[1]
     c, s = cos[...], sin[...]
@@ -346,7 +353,7 @@
     kv_send[...] = jnp.where(first, value_part, key_part)
 
 
-def joint_body(sc, kv_own, kv_recv, kv_raw, cos, sin, gk, grad_q, normed, grad_attn, heads, x,
+def joint_body(sc, kv_own, kv_recv, kv_raw, cos, sin, gk, grad_q, normed, x,
                attn_part, pre_part, post_part, q_part, w_own, w_other, send, keep, part,
                part_send, w, acc):
     join_rows(w, w_own, w_other)
@@ -361,7 +368,7 @@
     gq = grad_q[...]
     qw, kw = gq.shape[1], kvg.shape[1]
     n_t = normed[...].T
-    d = PLAN["attn"][0]
+    d = PLAN["qkv"][0]
     split_grad(sc, n_t, gq, send, keep, acc, d, 0)
     split_grad(sc, n_t, kvg, send, keep, acc, d, qw)
     out = dot(gq, w[:, :qw], ((1,), (1,))) + dot(kvg, w[:, qw:], ((1,), (1,)))
@@ -382,7 +389,6 @@
     ends = jnp.concatenate([ends, jnp.zeros((half - kw, gain_cols), f32)], axis=0)
     gains = wide + jnp.concatenate([ends, ends], axis=0)
     split_sum(sc, gains, send, keep, acc, d, qw + kw)
-    split_grad(sc, grad_attn[...].T, heads[...], send, keep, acc, d, qw + kw + gain_cols)
 
 
 def finish_body(sc, own, recv, key, value, gains):
@@ -485,7 +491,6 @@
         cot_t = out_cotangent.T
         cot_narrow = cot_t.astype(bf16)
         cot_diag = off_to_diag(cot_narrow)
-        cot_off = diag_to_off_col(jnp.concatenate([cot_narrow, cot_diag], axis=0))
 
         segments = segment_ids[0]
         places = jnp.arange(rows, dtype=jnp.int32)
@@ -514,13 +519,15 @@
             raw_q, kv_mine, kv_theirs, mask, cos, sin, gq, gk, *wo, scalars=sc,
             scratch=[pltpu.VMEM((width, qw), bf16)],
         )
-        (cotangent,) = call(cot_body, [wide_f], cot_t, cot_diag, cot_off, scalars=sc)
         proj, mid, ffn_in, gate, up, hidden = call(
             mix_body,
             [wide_f, wide_f, wide_b, ((t, ff), f32), ((t, ff), f32), ((t, ff), bf16)],
             x, part, swap_col(send), gains, w_gate, w_up, *e1, *e2, scalars=sc,
             scratch=ffn_scratch[:2],
         )
+        (cot_send,) = call(cot_send_body, [((width, t), bf16)], cot_narrow, cot_diag, mid)
+        cot_off = diag_to_off_col(cot_send)
+        (cotangent,) = call(cot_body, [wide_f], cot_t, cot_diag, cot_off, scalars=sc)
         part, send = call(
             down_body, [wide_f, wide_b], hidden, down_own, *e1, *e2, scalars=sc,
             scratch=ffn_scratch[:1],
@@ -603,23 +610,25 @@
         )
         (gate_sum,) = grad_sum("gate", s_gate, k_gate, [(ff, f32)])
         (up_sum,) = grad_sum("up", s_up, k_up, [(ff, f32)])
-        grad_mid, grad_attn, pre_part, attn_part, kv_own, kv_send, grad_q, q_part = call(
+        grad_mid, pre_part, attn_part, kv_own, kv_send, grad_q, q_part, s_out, k_out = call(
             attn_grad_body,
-            [wide_f, wide_b, ((1, width), f32), ((1, width), f32),
-             ((t, hd), f32), ((t, hd), f32), ((t, qw), bf16), ((1, hd), f32)],
+            [wide_f, ((1, width), f32), ((1, width), f32), ((t, hd), f32), ((t, hd), f32),
+             ((t, qw), bf16), ((1, hd), f32)] + first_shapes("out", qw),
             part, swap_col(send), mid, proj, cotangent, gains, *wo, q, k, v, probs,
-            raw_q, cos, sin, gq, scalars=sc, scratch=[pltpu.VMEM((width, qw), bf16)],
-        )
-        n_attn = joint_width + gain_cols + qw
-        s_attn, k_attn, part, send = call(
-            joint_body, first_shapes("attn", n_attn) + [wide_f, wide_b],
+            raw_q, cos, sin, gq, heads, scalars=sc,
+            scratch=[pltpu.VMEM((width, qw), bf16), pltpu.VMEM((2, half_width, qw), f32)],
+        )
+        (out_sum,) = grad_sum("out", s_out, k_out, [(qw, f32)])
+        n_qkv = joint_width + gain_cols
+        s_qkv, k_qkv, part, send = call(
+            joint_body, first_shapes("qkv", n_qkv) + [wide_f, wide_b],
             kv_own, swap_col(kv_send), kv_mine, cos, sin, gk, grad_q, normed,
-            grad_attn, heads, x, attn_part, pre_part, post_part, q_part, *w_joint, scalars=sc,
+            x, attn_part, pre_part, post_part, q_part, *w_joint, scalars=sc,
             scratch=[pltpu.VMEM((width, joint_width), bf16),
-                     pltpu.VMEM((2, half_width, n_attn), f32)],
-        )
-        query_sum, kv_sum, out_sum = grad_sum(
-            "attn", s_attn, k_attn, [(qw, f32), (hd + gain_cols, bf16), (qw, f32)]
+                     pltpu.VMEM((2, half_width, n_qkv), f32)],
+        )
+        query_sum, kv_sum = grad_sum(
+            "qkv", s_qkv, k_qkv, [(qw, f32), (hd + gain_cols, bf16)]
         )
         in_own_t, in_send = call(
             input_body, out_pair,

time: 189 us -> 184 us (0.974)
  waiting for transfers between devices: 87 us -> 81.5 us
  Pallas kernels: 32.5 us -> 34.6 us
    ppermute x9 -> x10, waiting for transfers between devices: 32.1 us -> 39.3 us  [swap_row(): return lax.ppermute(v, 'row', [(0, 1), (1, 0)])]
    ppermute x3, starting transfers between devices: 10.8 us -> 4.34 us  [diag_to_off_col(): return lax.ppermute(v, ('row', 'col'), [(0, 1), (3, 2)])]
    ppermute x2, waiting for transfers between devices: 5.92 us -> 0.01 us  [off_to_diag(): return lax.ppermute(v, ('row', 'col'), [(1, 3), (2, 0)])]
    ppermute x24 -> x29, waiting for transfers between devices: 45.3 us -> 39.9 us  [swap_dp(): return lax.ppermute(v, 'dp', [(i, i ^ bit) for i in range(n_dp)])]
    ppermute x9 -> x10, starting transfers between devices: 9.49 us -> 13.4 us  [swap_row(): return lax.ppermute(v, 'row', [(0, 1), (1, 0)])]
    ppermute x24 -> x29, starting transfers between devices: 29.7 us -> 33.2 us  [swap_dp(): return lax.ppermute(v, 'dp', [(i, i ^ bit) for i in range(n_dp)])]
    pallas_call x31 -> x37, Pallas kernels: 32.5 us -> 34.6 us  [call(): pl.pallas_call(body, in_specs=in_specs, out_specs=[pl.BlockSpec(memory_sp...]
  transfers between devices with their start and end apart: 46 -> 52, of which waited for: 16 -> 20; matrix products, arithmetic and copies ran while one was open for 4% -> 4% of each run, Pallas kernels for 11% -> 14%
where the time goes in v2:
time: 184 us
  waiting for transfers between devices  81.5 us (44%)
  starting transfers between devices  56.8 us (31%)
  Pallas kernels  34.6 us (19%)
  other arithmetic  6.44 us (4%)
  local copies, waits for them, and re-layouts  2.98 us (2%)
    ppermute x29, waiting for transfers between devices, swap_dp(): return lax.ppermute(v, 'dp', [(i, i ^ bit) for i in range(n_dp)])  39.9 us
    ppermute x10, waiting for transfers between devices, swap_row(): return lax.ppermute(v, 'row', [(0, 1), (1, 0)])  39.3 us
    pallas_call x37, Pallas kernels, call(): pl.pallas_call(body, in_specs=in_specs, out_specs=[pl.BlockSpec(memory_sp...  34.6 us
    ppermute x29, starting transfers between devices, swap_dp(): return lax.ppermute(v, 'dp', [(i, i ^ bit) for i in range(n_dp)])  33.2 us
    ppermute x10, starting transfers between devices, swap_row(): return lax.ppermute(v, 'row', [(0, 1), (1, 0)])  13.4 us
    ppermute x3, starting transfers between devices, diag_to_off_col(): return lax.ppermute(v, ('row', 'col'), [(0, 1), (3, 2)])  4.34 us
  transfers between devices with their start and end apart: 52, of which 20 were waited for; matrix products, arithmetic and copies ran while one was open for 4% of the time, Pallas kernels for 14%

profile of v2, /device:TPU:0, one launch (start us, length us, event | category | flops | bytes accessed | tf_op | source)
XLA Modules:
  0.0 183.7 jit_solution(3533462518483054094)
XLA Ops:
  1.5 3.0 %collective-permute-start.3 = (f32[4,320]{1,0:T(4,128)S(1)}, f32[4,320]{1,0:T(4,128)S(1)}, u32[]{:S(2)}, u32[]{:S(2)}) collective-permute-start(f32[4,320]{1,0:T(4,128)S(1)} %select_select_fusion), channel_id=1, source_target_pairs={{0,2},{2,0},{1,3},{3,1},{4,6},{6,4},{5,7},{7,5},{8,10},{10,8},{9,1... | collective-permute-start | bytes 15368 | tf_op jit(solution)/shard_map/ppermute | solution.py:423
  9.9 3.4 %collective-permute-start.8 = (bf16[80,1536]{1,0:T(8,128)(2,1)S(1)}, bf16[80,1536]{1,0:T(8,128)(2,1)S(1)}, u32[]{:S(2)}, u32[]{:S(2)}) collective-permute-start(bf16[80,1536]{1,0:T(8,128)(2,1)S(1)} %pad_maximum_fusion.8), channel_id=1, source_target_pairs={{0,2},{2,0},{1,3},{3,1},{4,6},{6,4},{5,7},{7,5},{8,10},{10,8},{9,1... | collective-permute-start | bytes 737288 | tf_op jit(solution)/shard_map/ppermute | solution.py:423
  15.1 15.7 %collective-permute-done.8.refs_2_.refs_1_.refs_3_ = bf16[80,1536]{1,0:T(8,128)(2,1)S(1)} collective-permute-done((bf16[80,1536]{1,0:T(8,128)(2,1)S(1)}, bf16[80,1536]{1,0:T(8,128)(2,1)S(1)}, u32[]{:S(2)}, u32[]{:S(2)}) %collective-permute-start.8) | collective-permute-done | bytes 245792 | tf_op jit(solution)/shard_map/ppermute | solution.py:423
  30.7 1.5 collective-permute-start.9
  33.6 1.6 collective-permute-start.12
  36.9 1.8 collective-permute-start.6
  38.9 1.6 collective-permute-start.10
  40.4 2.0 %shard_map.271 = (f32[256,640]{1,0:T(8,128)S(1)}, bf16[256,640]{1,0:T(8,128)(2,1)S(1)}, f32[256,512]{1,0:T(8,128)S(1)}, f32[256,256]{1,0:T(8,128)S(1)}) custom-call(s32[8]{0:T(128)S(1)} %shift-right-arithmetic_and_fusion.sc, f32[320,256]{1,0:T(8,128)} %bitcast.x_local, f32[320,256]{1,0:T(8,128)S(1)} %collective-permute-done.x_own, ...), custom_call_target="tpu_custom_call" | custom-call | tf_op jit(solution)/shard_map/pallas_call | solution.py:67
  42.6 1.6 collective-permute-start.13
  44.7 1.7 collective-permute-done.6.w_other
  46.4 1.6 shard_map.272
  49.5 2.1 %collective-permute-done.10.refs_4_.refs_3_.refs_5_ = bf16[160,1536]{1,0:T(8,128)(2,1)S(1)} collective-permute-done((bf16[160,1536]{1,0:T(8,128)(2,1)S(1)}, bf16[160,1536]{1,0:T(8,128)(2,1)S(1)}, u32[]{:S(2)}, u32[]{:S(2)}) %collective-permute-start.10) | collective-permute-done | bytes 491552 | tf_op jit(solution)/shard_map/ppermute | solution.py:429
  51.5 4.8 %collective-permute-done.13.refs_7_.refs_6_.refs_8_ = bf16[160,1536]{1,0:T(8,128)(2,1)S(1)} collective-permute-done((bf16[160,1536]{1,0:T(8,128)(2,1)S(1)}, bf16[160,1536]{1,0:T(8,128)(2,1)S(1)}, u32[]{:S(2)}, u32[]{:S(2)}) %collective-permute-start.13) | collective-permute-done | bytes 491552 | tf_op jit(solution)/shard_map/ppermute | solution.py:429
  56.3 2.0 %shard_map.273 = (f32[256,640]{1,0:T(8,128)S(1)}, f32[256,640]{1,0:T(8,128)S(1)}, bf16[256,640]{1,0:T(8,128)(2,1)S(1)}, f32[256,1024]{1,0:T(8,128)S(1)}, f32[256...) custom-call(s32[8]{0:T(128)S(1)} %shift-right-arithmetic_and_fusion.sc, f32[256,640]{1,0:T(8,128)S(1)} %get-tuple-element.86.x, ...), custom_call_target="tpu_custom_call" | custom-call | tf_op jit(solution)/shard_map/pallas_call | solution.py:67
  58.3 1.7 collective-permute-start.16
  64.4 3.9 %shard_map.278 = (bf16[2,160,1024]{2,1,0:T(8,128)(2,1)S(1)}, f32[2,160,1024]{2,1,0:T(8,128)S(1)}, bf16[2,160,1024]{2,1,0:T(8,128)(2,1)S(1)}, f32[2,160,1024]{2,1...) custom-call(s32[8]{0:T(128)S(1)} %shift-right-arithmetic_and_fusion.sc, ...), custom_call_target="tpu_custom_call" | custom-call | tf_op jit(solution)/shard_map/pallas_call | solution.py:67
  68.5 1.5 collective-permute-done.17.recv
  70.0 2.8 %shard_map.279 = (f32[256,640]{1,0:T(8,128)S(1)}, f32[1,640]{1,0:T(1,128)S(1)}, f32[1,640]{1,0:T(1,128)S(1)}, f32[256,256]{1,0:T(8,128)S(1)}, f32[256,256]{1,0:T...) custom-call(s32[8]{0:T(128)S(1)} %shift-right-arithmetic_and_fusion., ...), custom_call_target="tpu_custom_call" | custom-call | tf_op jit(solution)/shard_map/pallas_call | solution.py:67
  74.0 1.5 collective-permute-start.40
  76.0 2.0 %shard_map.280 = (bf16[1,320,896]{2,1,0:T(8,128)(2,1)S(1)}, f32[1,320,896]{2,1,0:T(8,128)S(1)}, f32[256,640]{1,0:T(8,128)S(1)}, bf16[256,640]{1,0:T(8,128)(2,1)S(1)}) custom-call(s32[8]{0:T(128)S(1)} %shift-right-arithmetic_and_fusion.sc, f32[256,256]{1,0:T(8,128)S(1)} %get-tuple-element.109.kv_own, f32[256,256]{1,0:T(8,128)S(1)} %collective-permute-done.18.kv_recv, ...), custom_call_target="tpu_custom_call" | custom-call | tf_op jit(solution)/shard_map/pallas_call | solution.py:67
  80.1 10.5 %collective-permute-done.46.recv = bf16[1,320,1024]{2,1,0:T(8,128)(2,1)S(1)} collective-permute-done((bf16[1,320,1024]{2,1,0:T(8,128)(2,1)S(1)}, bf16[1,320,1024]{2,1,0:T(8,128)(2,1)S(1)}, u32[]{:S(2)}, u32[]{:S(2)}) %collective-permute-start.46) | collective-permute-done | bytes 655392 | tf_op jit(solution)/shard_map/ppermute | solution.py:423
  92.7 1.5 collective-permute-start.41
  94.3 8.6 %collective-permute-done.21.recv = bf16[1,320,896]{2,1,0:T(8,128)(2,1)S(1)} collective-permute-done((bf16[1,320,896]{2,1,0:T(8,128)(2,1)S(1)}, bf16[1,320,896]{2,1,0:T(8,128)(2,1)S(1)}, u32[]{:S(2)}, u32[]{:S(2)}) %collective-permute-start.21) | collective-permute-done | bytes 573472 | tf_op jit(solution)/shard_map/ppermute | solution.py:423
  105.0 1.5 collective-permute-start.35
  106.5 2.8 %collective-permute-done.28.recv = bf16[1,320,512]{2,1,0:T(8,128)(2,1)S(1)} collective-permute-done((bf16[1,320,512]{2,1,0:T(8,128)(2,1)S(1)}, bf16[1,320,512]{2,1,0:T(8,128)(2,1)S(1)}, u32[]{:S(2)}, u32[]{:S(2)}) %collective-permute-start.28) | collective-permute-done | bytes 327712 | tf_op jit(solution)/shard_map/ppermute | solution.py:423
  111.2 5.4 %collective-permute-done.29.recv = bf16[1,160,512]{2,1,0:T(8,128)(2,1)S(1)} collective-permute-done((bf16[1,160,512]{2,1,0:T(8,128)(2,1)S(1)}, bf16[1,160,512]{2,1,0:T(8,128)(2,1)S(1)}, u32[]{:S(2)}, u32[]{:S(2)}) %collective-permute-start.29) | collective-permute-done | bytes 163872 | tf_op jit(solution)/shard_map/ppermute | solution.py:429
  116.6 1.5 collective-permute-start.48
  120.0 1.6 collective-permute-start.23
  125.2 2.6 %collective-permute-start.49 = (bf16[1,80,1024]{2,1,0:T(8,128)(2,1)S(1)}, bf16[1,80,1024]{2,1,0:T(8,128)(2,1)S(1)}, u32[]{:S(2)}, u32[]{:S(2)}) collective-permute-start(bf16[1,80,1024]{2,1,0:T(8,128)(2,1)S(1)} %shard_map.305.keep_in), channel_id=1, source_target_pairs={{0,16},{4,20},{8,24},{12,28},{16,0},{20,4},{24,8},{28,12},{1,17},{... | collective-permute-start | bytes 491528 | tf_op jit(solution)/shard_map/ppermute | solution.py:429
  127.9 1.5 collective-permute-start.31
  129.4 1.6 collective-permute-start.24
  131.4 9.2 %collective-permute-done.31.recv = bf16[1,80,512]{2,1,0:T(8,128)(2,1)S(1)} collective-permute-done((bf16[1,80,512]{2,1,0:T(8,128)(2,1)S(1)}, bf16[1,80,512]{2,1,0:T(8,128)(2,1)S(1)}, u32[]{:S(2)}, u32[]{:S(2)}) %collective-permute-start.31) | collective-permute-done | bytes 81952 | tf_op jit(solution)/shard_map/ppermute | solution.py:429
  141.2 3.5 %collective-permute-start.43 = (bf16[1,80,1024]{2,1,0:T(8,128)(2,1)S(1)}, bf16[1,80,1024]{2,1,0:T(8,128)(2,1)S(1)}, u32[]{:S(2)}, u32[]{:S(2)}) collective-permute-start(bf16[1,80,1024]{2,1,0:T(8,128)(2,1)S(1)} %shard_map.300.keep_in), channel_id=1, source_target_pairs={{0,16},{4,20},{8,24},{12,28},{16,0},{20,4},{24,8},{28,12},{1,17},{... | collective-permute-start | bytes 491528 | tf_op jit(solution)/shard_map/ppermute | solution.py:429
  146.0 2.6 %collective-permute-start.20 = (bf16[640,256]{1,0:T(8,128)(2,1)S(1)}, bf16[640,256]{1,0:T(8,128)(2,1)S(1)}, u32[]{:S(2)}, u32[]{:S(2)}) collective-permute-start(bf16[640,256]{1,0:T(8,128)(2,1)S(1)} %pad_maximum_fusion.3), channel_id=1, source_target_pairs={{0,2},{3,1},{4,6},{7,5},{8,10},{11,9},{12,14},{15,13},{16,18},{19,... | collective-permute-start | bytes 983048 | tf_op jit(solution)/shard_map/ppermute | solution.py:460
  148.6 1.9 %collective-permute-start.25 = (bf16[1,80,896]{2,1,0:T(8,128)(2,1)S(1)}, bf16[1,80,896]{2,1,0:T(8,128)(2,1)S(1)}, u32[]{:S(2)}, u32[]{:S(2)}) collective-permute-start(bf16[1,80,896]{2,1,0:T(8,128)(2,1)S(1)} %shard_map.285), channel_id=1, source_target_pairs={{0,4},{4,0},{8,12},{12,8},{16,20},{20,16},{24,28},{28,24},{1,5},{5... | collective-permute-start | bytes 430088 | tf_op jit(solution)/shard_map/ppermute | solution.py:429
  150.6 4.2 %collective-permute-done.43.recv = bf16[1,80,1024]{2,1,0:T(8,128)(2,1)S(1)} collective-permute-done((bf16[1,80,1024]{2,1,0:T(8,128)(2,1)S(1)}, bf16[1,80,1024]{2,1,0:T(8,128)(2,1)S(1)}, u32[]{:S(2)}, u32[]{:S(2)}) %collective-permute-start.43) | collective-permute-done | bytes 163872 | tf_op jit(solution)/shard_map/ppermute | solution.py:429
  154.9 2.0 %collective-permute-done.37.recv = bf16[1,80,1024]{2,1,0:T(8,128)(2,1)S(1)} collective-permute-done((bf16[1,80,1024]{2,1,0:T(8,128)(2,1)S(1)}, bf16[1,80,1024]{2,1,0:T(8,128)(2,1)S(1)}, u32[]{:S(2)}, u32[]{:S(2)}) %collective-permute-start.37) | collective-permute-done | bytes 163872 | tf_op jit(solution)/shard_map/ppermute | solution.py:429
  157.7 1.5 collective-permute-start.51
  159.2 3.0 %collective-permute-done.44 = bf16[1,80,1024]{2,1,0:T(8,128)(2,1)S(1)} collective-permute-done((bf16[1,80,1024]{2,1,0:T(8,128)(2,1)S(1)}, bf16[1,80,1024]{2,1,0:T(8,128)(2,1)S(1)}, u32[]{:S(2)}, u32[]{:S(2)}) %collective-permute-start.44) | collective-permute-done | bytes 163872 | tf_op jit(solution)/shard_map/ppermute | solution.py:429
  162.3 3.1 %collective-permute-done.38 = bf16[1,80,1024]{2,1,0:T(8,128)(2,1)S(1)} collective-permute-done((bf16[1,80,1024]{2,1,0:T(8,128)(2,1)S(1)}, bf16[1,80,1024]{2,1,0:T(8,128)(2,1)S(1)}, u32[]{:S(2)}, u32[]{:S(2)}) %collective-permute-start.38) | collective-permute-done | bytes 163872 | tf_op jit(solution)/shard_map/ppermute | solution.py:429
  165.4 1.5 collective-permute-start.39
  168.3 3.6 %collective-permute-done.26.far = bf16[2,80,896]{2,1,0:T(8,128)(2,1)S(1)} collective-permute-done((bf16[2,80,896]{2,1,0:T(8,128)(2,1)S(1)}, bf16[2,80,896]{2,1,0:T(8,128)(2,1)S(1)}, u32[]{:S(2)}, u32[]{:S(2)}) %collective-permute-start.26) | collective-permute-done | bytes 286752 | tf_op jit(solution)/shard_map/ppermute | solution.py:429
  171.9 1.4 shard_map.286
  174.3 1.7 shard_map.307
  176.0 1.7 collective-permute-done.45.far
  177.6 1.7 shard_map.302
  179.3 1.7 shard_map.297
  181.0 1.5 shard_map.287
  (143 shorter events, 40.1 us)
Async XLA Ops:
  1.5 30.7 %collective-permute-start.3 = (f32[4,320]{1,0:T(4,128)S(1)}, f32[4,320]{1,0:T(4,128)S(1)}, u32[]{:S(2)}, u32[]{:S(2)}) collective-permute-start(f32[4,320]{1,0:T(4,128)S(1)} %select_select_fusion), channel_id=1, source_target_pairs={{0,2},{2,0},{1,3},{3,1},{4,6},{6,4},{5,7},{7,5},{8,10},{10,8},{9,1... | collective-permute-start | bytes 15368 | tf_op jit(solution)/shard_map/ppermute | solution.py:423
  6.6 33.8 %collective-permute-start.4 = (bf16[320,768]{1,0:T(8,128)(2,1)S(1)}, bf16[320,768]{1,0:T(8,128)(2,1)}, u32[]{:S(2)}, u32[]{:S(2)}) collective-permute-start(bf16[320,768]{1,0:T(8,128)(2,1)S(1)} %pad_maximum_fusion.w_own), channel_id=1, source_target_pairs={{0,2},{2,0},{1,3},{3,1},{4,6},{6,4},{5,7},{7,5},{8,10},{10,8},{9,1... | collective-permute-start | bytes 1474568 | tf_op jit(solution)/shard_map/ppermute | solution.py:423
  6.7 28.6 %collective-permute-start.1 = (f32[320,256]{1,0:T(8,128)}, f32[320,256]{1,0:T(8,128)}, u32[]{:S(2)}, u32[]{:S(2)}) collective-permute-start(f32[320,256]{1,0:T(8,128)} %bitcast.x_local), channel_id=1, source_target_pairs={{1,3},{2,0},{5,7},{6,4},{9,11},{10,8},{13,15},{14,12},{17,19},{18,... | collective-permute-start | bytes 983048 | tf_op jit(solution)/shard_map/ppermute | solution.py:454
  9.9 20.8 %collective-permute-start.8 = (bf16[80,1536]{1,0:T(8,128)(2,1)S(1)}, bf16[80,1536]{1,0:T(8,128)(2,1)S(1)}, u32[]{:S(2)}, u32[]{:S(2)}) collective-permute-start(bf16[80,1536]{1,0:T(8,128)(2,1)S(1)} %pad_maximum_fusion.8), channel_id=1, source_target_pairs={{0,2},{2,0},{1,3},{3,1},{4,6},{6,4},{5,7},{7,5},{8,10},{10,8},{9,1... | collective-permute-start | bytes 737288 | tf_op jit(solution)/shard_map/ppermute | solution.py:423
  14.1 19.5 %collective-permute-start.11 = (bf16[80,1536]{1,0:T(8,128)(2,1)}, bf16[80,1536]{1,0:T(8,128)(2,1)S(1)}, u32[]{:S(2)}, u32[]{:S(2)}) collective-permute-start(bf16[80,1536]{1,0:T(8,128)(2,1)} %pad_maximum_fusion.9), channel_id=1, source_target_pairs={{0,2},{2,0},{1,3},{3,1},{4,6},{6,4},{5,7},{7,5},{8,10},{10,8},{9,1... | collective-permute-start | bytes 737288 | tf_op jit(solution)/shard_map/ppermute | solution.py:423
  30.7 6.2 %collective-permute-start.9 = (bf16[80,1536]{1,0:T(8,128)(2,1)S(1)}, bf16[80,1536]{1,0:T(8,128)(2,1)S(1)}, u32[]{:S(2)}, u32[]{:S(2)}) collective-permute-start(bf16[80,1536]{1,0:T(8,128)(2,1)S(1)} %collective-permute-done.8.refs_2_.refs_1_.refs_3_), channel_id=1, source_target_pairs={{0,4},{4,0},{8,12},{12,8},{16,20},{20,16},{24,28},{28,24},{1,5},{5... | collective-permute-start | bytes 737288 | tf_op jit(solution)/shard_map/ppermute | solution.py:429
  32.3 6.6 %collective-permute-start = (f32[320,256]{1,0:T(8,128)}, f32[320,256]{1,0:T(8,128)S(1)}, u32[]{:S(2)}, u32[]{:S(2)}) collective-permute-start(f32[320,256]{1,0:T(8,128)} %bitcast.x_local), channel_id=1, source_target_pairs={{0,1},{3,2},{4,5},{7,6},{8,9},{11,10},{12,13},{15,14},{16,17},{19,... | collective-permute-start | bytes 983048 | tf_op jit(solution)/shard_map/ppermute | solution.py:457
  33.6 9.0 %collective-permute-start.12 = (bf16[80,1536]{1,0:T(8,128)(2,1)S(1)}, bf16[80,1536]{1,0:T(8,128)(2,1)S(1)}, u32[]{:S(2)}, u32[]{:S(2)}) collective-permute-start(bf16[80,1536]{1,0:T(8,128)(2,1)S(1)} %collective-permute-done.11.refs_5_.refs_4_.refs_6_), channel_id=1, source_target_pairs={{0,8},{4,12},{8,0},{12,4},{16,24},{20,28},{24,16},{28,20},{1,9},{5... | collective-permute-start | bytes 737288 | tf_op jit(solution)/shard_map/ppermute | solution.py:429
  35.2 5.2 %collective-permute-start.2 = (f32[320,256]{1,0:T(8,128)}, f32[320,256]{1,0:T(8,128)S(1)}, u32[]{:S(2)}, u32[]{:S(2)}) collective-permute-start(f32[320,256]{1,0:T(8,128)} %collective-permute-done.1.x_diag), channel_id=1, source_target_pairs={{0,1},{3,2},{4,5},{7,6},{8,9},{11,10},{12,13},{15,14},{16,17},{19,... | collective-permute-start | bytes 983048 | tf_op jit(solution)/shard_map/ppermute | solution.py:457
  36.9 9.5 %collective-permute-start.6 = (bf16[320,512]{1,0:T(8,128)(2,1)S(1)}, bf16[320,512]{1,0:T(8,128)(2,1)S(1)}, u32[]{:S(2)}, u32[]{:S(2)}) collective-permute-start(bf16[320,512]{1,0:T(8,128)(2,1)S(1)} %bitcast.19), channel_id=1, source_target_pairs={{0,2},{2,0},{1,3},{3,1},{4,6},{6,4},{5,7},{7,5},{8,10},{10,8},{9,1... | collective-permute-start | bytes 983048 | tf_op jit(solution)/shard_map/ppermute | solution.py:423
  38.9 12.7 %collective-permute-start.10 = (bf16[160,1536]{1,0:T(8,128)(2,1)S(1)}, bf16[160,1536]{1,0:T(8,128)(2,1)S(1)}, u32[]{:S(2)}, u32[]{:S(2)}) collective-permute-start(bf16[160,1536]{1,0:T(8,128)(2,1)S(1)} %pad_maximum_fusion.1), channel_id=1, source_target_pairs={{0,8},{4,12},{8,0},{12,4},{16,24},{20,28},{24,16},{28,20},{1,9},{5... | collective-permute-start | bytes 1474568 | tf_op jit(solution)/shard_map/ppermute | solution.py:429
  42.5 3.9 %collective-permute-start.5 = (f32[256,256]{1,0:T(8,128)S(1)}, f32[256,256]{1,0:T(8,128)S(1)}, u32[]{:S(2)}, u32[]{:S(2)}) collective-permute-start(f32[256,256]{1,0:T(8,128)S(1)} %get-tuple-element.88.kv_mine.kv_raw), channel_id=1, source_target_pairs={{0,1},{1,0},{2,3},{3,2},{4,5},{5,4},{6,7},{7,6},{8,9},{9,8},{10,11... | collective-permute-start | bytes 786440 | tf_op jit(solution)/shard_map/ppermute | solution.py:426
  42.6 13.7 %collective-permute-start.13 = (bf16[160,1536]{1,0:T(8,128)(2,1)S(1)}, bf16[160,1536]{1,0:T(8,128)(2,1)S(1)}, u32[]{:S(2)}, u32[]{:S(2)}) collective-permute-start(bf16[160,1536]{1,0:T(8,128)(2,1)S(1)} %pad_maximum_fusion.2), channel_id=1, source_target_pairs={{0,4},{4,0},{8,12},{12,8},{16,20},{20,16},{24,28},{28,24},{1,5},{5... | collective-permute-start | bytes 1474568 | tf_op jit(solution)/shard_map/ppermute | solution.py:429
  48.0 8.3 %collective-permute-start.7 = (bf16[256,640]{1,0:T(8,128)(2,1)S(1)}, bf16[256,640]{1,0:T(8,128)(2,1)S(1)}, u32[]{:S(2)}, u32[]{:S(2)}) collective-permute-start(bf16[256,640]{1,0:T(8,128)(2,1)S(1)} %get-tuple-element.90), channel_id=1, source_target_pairs={{0,1},{1,0},{2,3},{3,2},{4,5},{5,4},{6,7},{7,6},{8,9},{9,8},{10,11... | collective-permute-start | bytes 983048 | tf_op jit(solution)/shard_map/ppermute | solution.py:426
  48.2 10.1 %collective-permute-start.15 = (bf16[320,256]{1,0:T(8,128)(2,1)S(1)}, bf16[320,256]{1,0:T(8,128)(2,1)S(1)}, u32[]{:S(2)}, u32[]{:S(2)}) collective-permute-start(bf16[320,256]{1,0:T(8,128)(2,1)S(1)} %bitcast_convert_fusion.own), channel_id=1, source_target_pairs={{1,3},{2,0},{5,7},{6,4},{9,11},{10,8},{13,15},{14,12},{17,19},{18,... | collective-permute-start | bytes 491528 | tf_op jit(solution)/shard_map/ppermute | solution.py:454
  73.0 17.6 %collective-permute-start.46 = (bf16[1,320,1024]{2,1,0:T(8,128)(2,1)S(1)}, bf16[1,320,1024]{2,1,0:T(8,128)(2,1)S(1)}, u32[]{:S(2)}, u32[]{:S(2)}) collective-permute-start(bf16[1,320,1024]{2,1,0:T(8,128)(2,1)S(1)} %get-tuple-element.151), channel_id=1, source_target_pairs={{0,2},{2,0},{1,3},{3,1},{4,6},{6,4},{5,7},{7,5},{8,10},{10,8},{9,1... | collective-permute-start | bytes 1966088 | tf_op jit(solution)/shard_map/ppermute | solution.py:423
  74.0 18.0 %collective-permute-start.40 = (bf16[2,160,1024]{2,1,0:T(8,128)(2,1)S(1)}, bf16[2,160,1024]{2,1,0:T(8,128)(2,1)S(1)}, u32[]{:S(2)}, u32[]{:S(2)}) collective-permute-start(bf16[2,160,1024]{2,1,0:T(8,128)(2,1)S(1)} %get-tuple-element.145), channel_id=1, source_target_pairs={{0,4},{4,0},{8,12},{12,8},{16,20},{20,16},{24,28},{28,24},{1,5},{5... | collective-permute-start | bytes 1966088 | tf_op jit(solution)/shard_map/ppermute | solution.py:429
  75.5 28.7 %collective-permute-start.34 = (bf16[2,160,1024]{2,1,0:T(8,128)(2,1)S(1)}, bf16[2,160,1024]{2,1,0:T(8,128)(2,1)S(1)}, u32[]{:S(2)}, u32[]{:S(2)}) collective-permute-start(bf16[2,160,1024]{2,1,0:T(8,128)(2,1)S(1)} %get-tuple-element.139), channel_id=1, source_target_pairs={{0,8},{4,12},{8,0},{12,4},{16,24},{20,28},{24,16},{28,20},{1,9},{5... | collective-permute-start | bytes 1966088 | tf_op jit(solution)/shard_map/ppermute | solution.py:429
  78.0 24.9 %collective-permute-start.21 = (bf16[1,320,896]{2,1,0:T(8,128)(2,1)S(1)}, bf16[1,320,896]{2,1,0:T(8,128)(2,1)S(1)}, u32[]{:S(2)}, u32[]{:S(2)}) collective-permute-start(bf16[1,320,896]{2,1,0:T(8,128)(2,1)S(1)} %get-tuple-element.123), channel_id=1, source_target_pairs={{0,2},{2,0},{1,3},{3,1},{4,6},{6,4},{5,7},{7,5},{8,10},{10,8},{9,1... | collective-permute-start | bytes 1720328 | tf_op jit(solution)/shard_map/ppermute | solution.py:423
  79.1 30.2 %collective-permute-start.28 = (bf16[1,320,512]{2,1,0:T(8,128)(2,1)S(1)}, bf16[1,320,512]{2,1,0:T(8,128)(2,1)S(1)}, u32[]{:S(2)}, u32[]{:S(2)}) collective-permute-start(bf16[1,320,512]{2,1,0:T(8,128)(2,1)S(1)} %get-tuple-element.133), channel_id=1, source_target_pairs={{0,2},{2,0},{1,3},{3,1},{4,6},{6,4},{5,7},{7,5},{8,10},{10,8},{9,1... | collective-permute-start | bytes 983048 | tf_op jit(solution)/shard_map/ppermute | solution.py:423
  91.4 19.2 %collective-permute-start.47 = (bf16[1,160,1024]{2,1,0:T(8,128)(2,1)S(1)}, bf16[1,160,1024]{2,1,0:T(8,128)(2,1)S(1)}, u32[]{:S(2)}, u32[]{:S(2)}) collective-permute-start(bf16[1,160,1024]{2,1,0:T(8,128)(2,1)S(1)} %get-tuple-element.153), channel_id=1, source_target_pairs={{0,8},{4,12},{8,0},{12,4},{16,24},{20,28},{24,16},{28,20},{1,9},{5... | collective-permute-start | bytes 983048 | tf_op jit(solution)/shard_map/ppermute | solution.py:429
  92.7 27.2 %collective-permute-start.41 = (bf16[2,80,1024]{2,1,0:T(8,128)(2,1)S(1)}, bf16[2,80,1024]{2,1,0:T(8,128)(2,1)S(1)}, u32[]{:S(2)}, u32[]{:S(2)}) collective-permute-start(bf16[2,80,1024]{2,1,0:T(8,128)(2,1)S(1)} %get-tuple-element.147), channel_id=1, source_target_pairs={{0,8},{4,12},{8,0},{12,4},{16,24},{20,28},{24,16},{28,20},{1,9},{5... | collective-permute-start | bytes 983048 | tf_op jit(solution)/shard_map/ppermute | solution.py:429
  103.6 15.1 %collective-permute-start.22 = (bf16[1,160,896]{2,1,0:T(8,128)(2,1)S(1)}, bf16[1,160,896]{2,1,0:T(8,128)(2,1)S(1)}, u32[]{:S(2)}, u32[]{:S(2)}) collective-permute-start(bf16[1,160,896]{2,1,0:T(8,128)(2,1)S(1)} %get-tuple-element.125), channel_id=1, source_target_pairs={{0,8},{4,12},{8,0},{12,4},{16,24},{20,28},{24,16},{28,20},{1,9},{5... | collective-permute-start | bytes 860168 | tf_op jit(solution)/shard_map/ppermute | solution.py:429
  105.0 17.1 %collective-permute-start.35 = (bf16[2,80,1024]{2,1,0:T(8,128)(2,1)S(1)}, bf16[2,80,1024]{2,1,0:T(8,128)(2,1)S(1)}, u32[]{:S(2)}, u32[]{:S(2)}) collective-permute-start(bf16[2,80,1024]{2,1,0:T(8,128)(2,1)S(1)} %get-tuple-element.141), channel_id=1, source_target_pairs={{0,4},{4,0},{8,12},{12,8},{16,20},{20,16},{24,28},{28,24},{1,5},{5... | collective-permute-start | bytes 983048 | tf_op jit(solution)/shard_map/ppermute | solution.py:429
  110.0 6.7 %collective-permute-start.29 = (bf16[1,160,512]{2,1,0:T(8,128)(2,1)S(1)}, bf16[1,160,512]{2,1,0:T(8,128)(2,1)S(1)}, u32[]{:S(2)}, u32[]{:S(2)}) collective-permute-start(bf16[1,160,512]{2,1,0:T(8,128)(2,1)S(1)} %get-tuple-element.135), channel_id=1, source_target_pairs={{0,8},{4,12},{8,0},{12,4},{16,24},{20,28},{24,16},{28,20},{1,9},{5... | collective-permute-start | bytes 491528 | tf_op jit(solution)/shard_map/ppermute | solution.py:429
  110.6 18.8 %collective-permute-start.19 = (bf16[256,640]{1,0:T(8,128)(2,1)S(1)}, bf16[256,640]{1,0:T(8,128)(2,1)S(1)}, u32[]{:S(2)}, u32[]{:S(2)}) collective-permute-start(bf16[256,640]{1,0:T(8,128)(2,1)S(1)} %get-tuple-element.118), channel_id=1, source_target_pairs={{0,1},{1,0},{2,3},{3,2},{4,5},{5,4},{6,7},{7,6},{8,9},{9,8},{10,11... | collective-permute-start | bytes 983048 | tf_op jit(solution)/shard_map/ppermute | solution.py:426
  116.6 7.0 %collective-permute-start.48 = (bf16[1,80,1024]{2,1,0:T(8,128)(2,1)S(1)}, bf16[1,80,1024]{2,1,0:T(8,128)(2,1)S(1)}, u32[]{:S(2)}, u32[]{:S(2)}) collective-permute-start(bf16[1,80,1024]{2,1,0:T(8,128)(2,1)S(1)} %get-tuple-element.155), channel_id=1, source_target_pairs={{0,4},{4,0},{8,12},{12,8},{16,20},{20,16},{24,28},{28,24},{1,5},{5... | collective-permute-start | bytes 491528 | tf_op jit(solution)/shard_map/ppermute | solution.py:429
  118.7 6.5 %collective-permute-start.30 = (bf16[1,80,512]{2,1,0:T(8,128)(2,1)S(1)}, bf16[1,80,512]{2,1,0:T(8,128)(2,1)S(1)}, u32[]{:S(2)}, u32[]{:S(2)}) collective-permute-start(bf16[1,80,512]{2,1,0:T(8,128)(2,1)S(1)} %get-tuple-element.137), channel_id=1, source_target_pairs={{0,4},{4,0},{8,12},{12,8},{16,20},{20,16},{24,28},{28,24},{1,5},{5... | collective-permute-start | bytes 245768 | tf_op jit(solution)/shard_map/ppermute | solution.py:429
  120.0 7.9 %collective-permute-start.23 = (bf16[1,80,896]{2,1,0:T(8,128)(2,1)S(1)}, bf16[1,80,896]{2,1,0:T(8,128)(2,1)S(1)}, u32[]{:S(2)}, u32[]{:S(2)}) collective-permute-start(bf16[1,80,896]{2,1,0:T(8,128)(2,1)S(1)} %get-tuple-element.127), channel_id=1, source_target_pairs={{0,4},{4,0},{8,12},{12,8},{16,20},{20,16},{24,28},{28,24},{1,5},{5... | collective-permute-start | bytes 430088 | tf_op jit(solution)/shard_map/ppermute | solution.py:429
  122.2 19.0 %collective-permute-start.42 = (bf16[1,80,1024]{2,1,0:T(8,128)(2,1)S(1)}, bf16[1,80,1024]{2,1,0:T(8,128)(2,1)S(1)}, u32[]{:S(2)}, u32[]{:S(2)}) collective-permute-start(bf16[1,80,1024]{2,1,0:T(8,128)(2,1)S(1)} %get-tuple-element.149), channel_id=1, source_target_pairs={{0,2},{2,0},{1,3},{3,1},{4,6},{6,4},{5,7},{7,5},{8,10},{10,8},{9,1... | collective-permute-start | bytes 491528 | tf_op jit(solution)/shard_map/ppermute | solution.py:423
  123.7 21.0 %collective-permute-start.36 = (bf16[1,80,1024]{2,1,0:T(8,128)(2,1)S(1)}, bf16[1,80,1024]{2,1,0:T(8,128)(2,1)S(1)}, u32[]{:S(2)}, u32[]{:S(2)}) collective-permute-start(bf16[1,80,1024]{2,1,0:T(8,128)(2,1)S(1)} %get-tuple-element.143), channel_id=1, source_target_pairs={{0,2},{2,0},{1,3},{3,1},{4,6},{6,4},{5,7},{7,5},{8,10},{10,8},{9,1... | collective-permute-start | bytes 491528 | tf_op jit(solution)/shard_map/ppermute | solution.py:423
  125.2 19.6 %collective-permute-start.49 = (bf16[1,80,1024]{2,1,0:T(8,128)(2,1)S(1)}, bf16[1,80,1024]{2,1,0:T(8,128)(2,1)S(1)}, u32[]{:S(2)}, u32[]{:S(2)}) collective-permute-start(bf16[1,80,1024]{2,1,0:T(8,128)(2,1)S(1)} %shard_map.305.keep_in), channel_id=1, source_target_pairs={{0,16},{4,20},{8,24},{12,28},{16,0},{20,4},{24,8},{28,12},{1,17},{... | collective-permute-start | bytes 491528 | tf_op jit(solution)/shard_map/ppermute | solution.py:429
  127.9 12.7 %collective-permute-start.31 = (bf16[1,80,512]{2,1,0:T(8,128)(2,1)S(1)}, bf16[1,80,512]{2,1,0:T(8,128)(2,1)S(1)}, u32[]{:S(2)}, u32[]{:S(2)}) collective-permute-start(bf16[1,80,512]{2,1,0:T(8,128)(2,1)S(1)} %shard_map.290.keep_in), channel_id=1, source_target_pairs={{0,16},{4,20},{8,24},{12,28},{16,0},{20,4},{24,8},{28,12},{1,17},{... | collective-permute-start | bytes 245768 | tf_op jit(solution)/shard_map/ppermute | solution.py:429
  129.4 16.6 %collective-permute-start.24 = (bf16[1,80,896]{2,1,0:T(8,128)(2,1)S(1)}, bf16[1,80,896]{2,1,0:T(8,128)(2,1)S(1)}, u32[]{:S(2)}, u32[]{:S(2)}) collective-permute-start(bf16[1,80,896]{2,1,0:T(8,128)(2,1)S(1)} %shard_map.284.keep_in), channel_id=1, source_target_pairs={{0,16},{4,20},{8,24},{12,28},{16,0},{20,4},{24,8},{28,12},{1,17},{... | collective-permute-start | bytes 430088 | tf_op jit(solution)/shard_map/ppermute | solution.py:429
  140.6 8.0 %collective-permute-start.32 = (bf16[1,80,512]{2,1,0:T(8,128)(2,1)S(1)}, bf16[1,80,512]{2,1,0:T(8,128)(2,1)S(1)}, u32[]{:S(2)}, u32[]{:S(2)}) collective-permute-start(bf16[1,80,512]{2,1,0:T(8,128)(2,1)S(1)} %shard_map.291), channel_id=1, source_target_pairs={{0,8},{4,12},{8,0},{12,4},{16,24},{20,28},{24,16},{28,20},{1,9},{5... | collective-permute-start | bytes 245768 | tf_op jit(solution)/shard_map/ppermute | solution.py:429
  141.2 13.6 %collective-permute-start.43 = (bf16[1,80,1024]{2,1,0:T(8,128)(2,1)S(1)}, bf16[1,80,1024]{2,1,0:T(8,128)(2,1)S(1)}, u32[]{:S(2)}, u32[]{:S(2)}) collective-permute-start(bf16[1,80,1024]{2,1,0:T(8,128)(2,1)S(1)} %shard_map.300.keep_in), channel_id=1, source_target_pairs={{0,16},{4,20},{8,24},{12,28},{16,0},{20,4},{24,8},{28,12},{1,17},{... | collective-permute-start | bytes 491528 | tf_op jit(solution)/shard_map/ppermute | solution.py:429
  144.7 12.2 %collective-permute-start.37 = (bf16[1,80,1024]{2,1,0:T(8,128)(2,1)S(1)}, bf16[1,80,1024]{2,1,0:T(8,128)(2,1)S(1)}, u32[]{:S(2)}, u32[]{:S(2)}) collective-permute-start(bf16[1,80,1024]{2,1,0:T(8,128)(2,1)S(1)} %shard_map.295.keep_in), channel_id=1, source_target_pairs={{0,16},{4,20},{8,24},{12,28},{16,0},{20,4},{24,8},{28,12},{1,17},{... | collective-permute-start | bytes 491528 | tf_op jit(solution)/shard_map/ppermute | solution.py:429
  144.8 12.1 %collective-permute-start.50 = (bf16[1,80,1024]{2,1,0:T(8,128)(2,1)S(1)}, bf16[1,80,1024]{2,1,0:T(8,128)(2,1)S(1)}, u32[]{:S(2)}, u32[]{:S(2)}) collective-permute-start(bf16[1,80,1024]{2,1,0:T(8,128)(2,1)S(1)} %shard_map.306), channel_id=1, source_target_pairs={{0,8},{4,12},{8,0},{12,4},{16,24},{20,28},{24,16},{28,20},{1,9},{5... | collective-permute-start | bytes 491528 | tf_op jit(solution)/shard_map/ppermute | solution.py:429
  146.0 22.3 %collective-permute-start.20 = (bf16[640,256]{1,0:T(8,128)(2,1)S(1)}, bf16[640,256]{1,0:T(8,128)(2,1)S(1)}, u32[]{:S(2)}, u32[]{:S(2)}) collective-permute-start(bf16[640,256]{1,0:T(8,128)(2,1)S(1)} %pad_maximum_fusion.3), channel_id=1, source_target_pairs={{0,2},{3,1},{4,6},{7,5},{8,10},{11,9},{12,14},{15,13},{16,18},{19,... | collective-permute-start | bytes 983048 | tf_op jit(solution)/shard_map/ppermute | solution.py:460
  148.6 9.0 %collective-permute-start.25 = (bf16[1,80,896]{2,1,0:T(8,128)(2,1)S(1)}, bf16[1,80,896]{2,1,0:T(8,128)(2,1)S(1)}, u32[]{:S(2)}, u32[]{:S(2)}) collective-permute-start(bf16[1,80,896]{2,1,0:T(8,128)(2,1)S(1)} %shard_map.285), channel_id=1, source_target_pairs={{0,4},{4,0},{8,12},{12,8},{16,20},{20,16},{24,28},{28,24},{1,5},{5... | collective-permute-start | bytes 430088 | tf_op jit(solution)/shard_map/ppermute | solution.py:429
  154.8 10.6 %collective-permute-start.33 = (bf16[2,80,512]{2,1,0:T(8,128)(2,1)S(1)}, bf16[2,80,512]{2,1,0:T(8,128)(2,1)S(1)}, u32[]{:S(2)}, u32[]{:S(2)}) collective-permute-start(bf16[2,80,512]{2,1,0:T(8,128)(2,1)S(1)} %pad_maximum_fusion.10.near), channel_id=1, source_target_pairs={{0,4},{4,0},{8,12},{12,8},{16,20},{20,16},{24,28},{28,24},{1,5},{5... | collective-permute-start | bytes 491528 | tf_op jit(solution)/shard_map/ppermute | solution.py:429
  156.9 5.3 %collective-permute-start.44 = (bf16[1,80,1024]{2,1,0:T(8,128)(2,1)S(1)}, bf16[1,80,1024]{2,1,0:T(8,128)(2,1)S(1)}, u32[]{:S(2)}, u32[]{:S(2)}) collective-permute-start(bf16[1,80,1024]{2,1,0:T(8,128)(2,1)S(1)} %shard_map.301), channel_id=1, source_target_pairs={{0,8},{4,12},{8,0},{12,4},{16,24},{20,28},{24,16},{28,20},{1,9},{5... | collective-permute-start | bytes 491528 | tf_op jit(solution)/shard_map/ppermute | solution.py:429
  157.0 8.4 %collective-permute-start.38 = (bf16[1,80,1024]{2,1,0:T(8,128)(2,1)S(1)}, bf16[1,80,1024]{2,1,0:T(8,128)(2,1)S(1)}, u32[]{:S(2)}, u32[]{:S(2)}) collective-permute-start(bf16[1,80,1024]{2,1,0:T(8,128)(2,1)S(1)} %shard_map.296), channel_id=1, source_target_pairs={{0,4},{4,0},{8,12},{12,8},{16,20},{20,16},{24,28},{28,24},{1,5},{5... | collective-permute-start | bytes 491528 | tf_op jit(solution)/shard_map/ppermute | solution.py:429
  157.7 16.6 %collective-permute-start.51 = (bf16[2,80,1024]{2,1,0:T(8,128)(2,1)S(1)}, bf16[2,80,1024]{2,1,0:T(8,128)(2,1)S(1)}, u32[]{:S(2)}, u32[]{:S(2)}) collective-permute-start(bf16[2,80,1024]{2,1,0:T(8,128)(2,1)S(1)} %pad_maximum_fusion.6.near), channel_id=1, source_target_pairs={{0,4},{4,0},{8,12},{12,8},{16,20},{20,16},{24,28},{28,24},{1,5},{5... | collective-permute-start | bytes 983048 | tf_op jit(solution)/shard_map/ppermute | solution.py:429
  162.2 9.7 %collective-permute-start.26 = (bf16[2,80,896]{2,1,0:T(8,128)(2,1)S(1)}, bf16[2,80,896]{2,1,0:T(8,128)(2,1)S(1)}, u32[]{:S(2)}, u32[]{:S(2)}) collective-permute-start(bf16[2,80,896]{2,1,0:T(8,128)(2,1)S(1)} %pad_maximum_fusion.7.near), channel_id=1, source_target_pairs={{0,8},{4,12},{8,0},{12,4},{16,24},{20,28},{24,16},{28,20},{1,9},{5... | collective-permute-start | bytes 860168 | tf_op jit(solution)/shard_map/ppermute | solution.py:429
  165.3 12.3 %collective-permute-start.45 = (bf16[2,80,1024]{2,1,0:T(8,128)(2,1)S(1)}, bf16[2,80,1024]{2,1,0:T(8,128)(2,1)S(1)}, u32[]{:S(2)}, u32[]{:S(2)}) collective-permute-start(bf16[2,80,1024]{2,1,0:T(8,128)(2,1)S(1)} %pad_maximum_fusion.5.near), channel_id=1, source_target_pairs={{0,4},{4,0},{8,12},{12,8},{16,20},{20,16},{24,28},{28,24},{1,5},{5... | collective-permute-start | bytes 983048 | tf_op jit(solution)/shard_map/ppermute | solution.py:429
  165.4 14.0 %collective-permute-start.39 = (bf16[2,80,1024]{2,1,0:T(8,128)(2,1)S(1)}, bf16[2,80,1024]{2,1,0:T(8,128)(2,1)S(1)}, u32[]{:S(2)}, u32[]{:S(2)}) collective-permute-start(bf16[2,80,1024]{2,1,0:T(8,128)(2,1)S(1)} %pad_maximum_fusion.4.near), channel_id=1, source_target_pairs={{0,8},{4,12},{8,0},{12,4},{16,24},{20,28},{24,16},{28,20},{1,9},{5... | collective-permute-start | bytes 983048 | tf_op jit(solution)/shard_map/ppermute | solution.py:429
  173.4 7.7 %collective-permute-start.27 = (bf16[320,384]{1,0:T(8,128)(2,1)S(1)}, bf16[320,384]{1,0:T(8,128)(2,1)S(1)}, u32[]{:S(2)}, u32[]{:S(2)}) collective-permute-start(bf16[320,384]{1,0:T(8,128)(2,1)S(1)} %get-tuple-element.129.own), channel_id=1, source_target_pairs={{0,1},{1,0},{2,3},{3,2},{4,5},{5,4},{6,7},{7,6},{8,9},{9,8},{10,11... | collective-permute-start | bytes 737288 | tf_op jit(solution)/shard_map/ppermute | solution.py:426
  (13 other events, 89.8 us)

commit v3 on v2

--- a/solution.py
+++ b/solution.py
@@ -63,12 +63,13 @@
     if scalars is not None:
         in_specs = [pl.BlockSpec(memory_space=pltpu.SMEM)] + in_specs
         args = (scalars,) + args
-    place = jax.ShapeDtypeStruct if out_hbm else pltpu.VMEM
+    in_hbm = len(outs) if out_hbm is True else int(out_hbm)
+    place = [jax.ShapeDtypeStruct] * in_hbm + [pltpu.VMEM] * (len(outs) - in_hbm)
     return pl.pallas_call(
         body,
         in_specs=in_specs,
         out_specs=[pl.BlockSpec(memory_space=pltpu.VMEM) for _ in outs],
-        out_shape=[place(s, d) for s, d in outs],
+        out_shape=[at(s, d) for at, (s, d) in zip(place, outs)],
         scratch_shapes=list(scratch),
         compiler_params=pltpu.CompilerParams(vmem_limit_bytes=limit << 20),
     )(*args)
@@ -640,7 +641,7 @@
         key_sum, value_sum, gain_sum = call(
             finish_body,
             [((half_width, hd), f32), ((half_width, hd), f32), ((8, half_width), f32)],
-            kv_sum, swap_col(kv_sum), scalars=sc, out_hbm=True,
+            kv_sum, swap_col(kv_sum), scalars=sc, out_hbm=2,
         )
         return (
             block_output, input_grad, query_sum, key_sum, value_sum, out_sum.T,

time: 184 us -> 184 us (level)
  no operation moved by 1% of the time
where the time goes in v3:
time: 184 us
  waiting for transfers between devices  81.5 us (44%)
  starting transfers between devices  56.8 us (31%)
  Pallas kernels  34.6 us (19%)
  other arithmetic  6.44 us (4%)
  local copies, waits for them, and re-layouts  2.98 us (2%)
    ppermute x29, waiting for transfers between devices, swap_dp(): return lax.ppermute(v, 'dp', [(i, i ^ bit) for i in range(n_dp)])  39.9 us
    ppermute x10, waiting for transfers between devices, swap_row(): return lax.ppermute(v, 'row', [(0, 1), (1, 0)])  39.3 us
    pallas_call x37, Pallas kernels, call(): pl.pallas_call(body, in_specs=in_specs, out_specs=[pl.BlockSpec(memory_sp...  34.6 us
    ppermute x29, starting transfers between devices, swap_dp(): return lax.ppermute(v, 'dp', [(i, i ^ bit) for i in range(n_dp)])  33.2 us
    ppermute x10, starting transfers between devices, swap_row(): return lax.ppermute(v, 'row', [(0, 1), (1, 0)])  13.4 us
    ppermute x3, starting transfers between devices, diag_to_off_col(): return lax.ppermute(v, ('row', 'col'), [(0, 1), (3, 2)])  4.34 us
  transfers between devices with their start and end apart: 52, of which 20 were waited for; matrix products, arithmetic and copies ran while one was open for 4% of the time, Pallas kernels for 14%

profile of v3, /device:TPU:0, one launch (start us, length us, event | category | flops | bytes accessed | tf_op | source)
XLA Modules:
  0.0 183.7 jit_solution(3533462518483054094)
XLA Ops:
  1.5 3.0 %collective-permute-start.3 = (f32[4,320]{1,0:T(4,128)S(1)}, f32[4,320]{1,0:T(4,128)S(1)}, u32[]{:S(2)}, u32[]{:S(2)}) collective-permute-start(f32[4,320]{1,0:T(4,128)S(1)} %select_select_fusion), channel_id=1, source_target_pairs={{0,2},{2,0},{1,3},{3,1},{4,6},{6,4},{5,7},{7,5},{8,10},{10,8},{9,1... | collective-permute-start | bytes 15368 | tf_op jit(solution)/shard_map/ppermute | solution.py:424
  9.9 3.4 %collective-permute-start.8 = (bf16[80,1536]{1,0:T(8,128)(2,1)S(1)}, bf16[80,1536]{1,0:T(8,128)(2,1)S(1)}, u32[]{:S(2)}, u32[]{:S(2)}) collective-permute-start(bf16[80,1536]{1,0:T(8,128)(2,1)S(1)} %pad_maximum_fusion.8), channel_id=1, source_target_pairs={{0,2},{2,0},{1,3},{3,1},{4,6},{6,4},{5,7},{7,5},{8,10},{10,8},{9,1... | collective-permute-start | bytes 737288 | tf_op jit(solution)/shard_map/ppermute | solution.py:424
  15.1 15.7 %collective-permute-done.8.refs_2_.refs_1_.refs_3_ = bf16[80,1536]{1,0:T(8,128)(2,1)S(1)} collective-permute-done((bf16[80,1536]{1,0:T(8,128)(2,1)S(1)}, bf16[80,1536]{1,0:T(8,128)(2,1)S(1)}, u32[]{:S(2)}, u32[]{:S(2)}) %collective-permute-start.8) | collective-permute-done | bytes 245792 | tf_op jit(solution)/shard_map/ppermute | solution.py:424
  30.7 1.5 collective-permute-start.9
  33.6 1.6 collective-permute-start.12
  36.9 1.8 collective-permute-start.6
  38.9 1.6 collective-permute-start.10
  40.4 2.0 %shard_map.271 = (f32[256,640]{1,0:T(8,128)S(1)}, bf16[256,640]{1,0:T(8,128)(2,1)S(1)}, f32[256,512]{1,0:T(8,128)S(1)}, f32[256,256]{1,0:T(8,128)S(1)}) custom-call(s32[8]{0:T(128)S(1)} %shift-right-arithmetic_and_fusion.sc, f32[320,256]{1,0:T(8,128)} %bitcast.x_local, f32[320,256]{1,0:T(8,128)S(1)} %collective-permute-done.x_own, ...), custom_call_target="tpu_custom_call" | custom-call | tf_op jit(solution)/shard_map/pallas_call | solution.py:68
  42.6 1.6 collective-permute-start.13
  44.7 1.7 collective-permute-done.6.w_other
  46.4 1.6 shard_map.272
  49.5 2.1 %collective-permute-done.10.refs_4_.refs_3_.refs_5_ = bf16[160,1536]{1,0:T(8,128)(2,1)S(1)} collective-permute-done((bf16[160,1536]{1,0:T(8,128)(2,1)S(1)}, bf16[160,1536]{1,0:T(8,128)(2,1)S(1)}, u32[]{:S(2)}, u32[]{:S(2)}) %collective-permute-start.10) | collective-permute-done | bytes 491552 | tf_op jit(solution)/shard_map/ppermute | solution.py:430
  51.5 4.8 %collective-permute-done.13.refs_7_.refs_6_.refs_8_ = bf16[160,1536]{1,0:T(8,128)(2,1)S(1)} collective-permute-done((bf16[160,1536]{1,0:T(8,128)(2,1)S(1)}, bf16[160,1536]{1,0:T(8,128)(2,1)S(1)}, u32[]{:S(2)}, u32[]{:S(2)}) %collective-permute-start.13) | collective-permute-done | bytes 491552 | tf_op jit(solution)/shard_map/ppermute | solution.py:430
  56.3 2.0 %shard_map.273 = (f32[256,640]{1,0:T(8,128)S(1)}, f32[256,640]{1,0:T(8,128)S(1)}, bf16[256,640]{1,0:T(8,128)(2,1)S(1)}, f32[256,1024]{1,0:T(8,128)S(1)}, f32[256...) custom-call(s32[8]{0:T(128)S(1)} %shift-right-arithmetic_and_fusion.sc, f32[256,640]{1,0:T(8,128)S(1)} %get-tuple-element.86.x, ...), custom_call_target="tpu_custom_call" | custom-call | tf_op jit(solution)/shard_map/pallas_call | solution.py:68
  58.3 1.7 collective-permute-start.16
  64.4 3.9 %shard_map.278 = (bf16[2,160,1024]{2,1,0:T(8,128)(2,1)S(1)}, f32[2,160,1024]{2,1,0:T(8,128)S(1)}, bf16[2,160,1024]{2,1,0:T(8,128)(2,1)S(1)}, f32[2,160,1024]{2,1...) custom-call(s32[8]{0:T(128)S(1)} %shift-right-arithmetic_and_fusion.sc, ...), custom_call_target="tpu_custom_call" | custom-call | tf_op jit(solution)/shard_map/pallas_call | solution.py:68
  68.5 1.5 collective-permute-done.17.recv
  70.0 2.8 %shard_map.279 = (f32[256,640]{1,0:T(8,128)S(1)}, f32[1,640]{1,0:T(1,128)S(1)}, f32[1,640]{1,0:T(1,128)S(1)}, f32[256,256]{1,0:T(8,128)S(1)}, f32[256,256]{1,0:T...) custom-call(s32[8]{0:T(128)S(1)} %shift-right-arithmetic_and_fusion., ...), custom_call_target="tpu_custom_call" | custom-call | tf_op jit(solution)/shard_map/pallas_call | solution.py:68
  74.0 1.5 collective-permute-start.40
  76.0 2.0 %shard_map.280 = (bf16[1,320,896]{2,1,0:T(8,128)(2,1)S(1)}, f32[1,320,896]{2,1,0:T(8,128)S(1)}, f32[256,640]{1,0:T(8,128)S(1)}, bf16[256,640]{1,0:T(8,128)(2,1)S(1)}) custom-call(s32[8]{0:T(128)S(1)} %shift-right-arithmetic_and_fusion.sc, f32[256,256]{1,0:T(8,128)S(1)} %get-tuple-element.109.kv_own, f32[256,256]{1,0:T(8,128)S(1)} %collective-permute-done.18.kv_recv, ...), custom_call_target="tpu_custom_call" | custom-call | tf_op jit(solution)/shard_map/pallas_call | solution.py:68
  80.1 10.5 %collective-permute-done.46.recv = bf16[1,320,1024]{2,1,0:T(8,128)(2,1)S(1)} collective-permute-done((bf16[1,320,1024]{2,1,0:T(8,128)(2,1)S(1)}, bf16[1,320,1024]{2,1,0:T(8,128)(2,1)S(1)}, u32[]{:S(2)}, u32[]{:S(2)}) %collective-permute-start.46) | collective-permute-done | bytes 655392 | tf_op jit(solution)/shard_map/ppermute | solution.py:424
  92.7 1.5 collective-permute-start.41
  94.3 8.6 %collective-permute-done.21.recv = bf16[1,320,896]{2,1,0:T(8,128)(2,1)S(1)} collective-permute-done((bf16[1,320,896]{2,1,0:T(8,128)(2,1)S(1)}, bf16[1,320,896]{2,1,0:T(8,128)(2,1)S(1)}, u32[]{:S(2)}, u32[]{:S(2)}) %collective-permute-start.21) | collective-permute-done | bytes 573472 | tf_op jit(solution)/shard_map/ppermute | solution.py:424
  105.0 1.5 collective-permute-start.35
  106.5 2.8 %collective-permute-done.28.recv = bf16[1,320,512]{2,1,0:T(8,128)(2,1)S(1)} collective-permute-done((bf16[1,320,512]{2,1,0:T(8,128)(2,1)S(1)}, bf16[1,320,512]{2,1,0:T(8,128)(2,1)S(1)}, u32[]{:S(2)}, u32[]{:S(2)}) %collective-permute-start.28) | collective-permute-done | bytes 327712 | tf_op jit(solution)/shard_map/ppermute | solution.py:424
  111.2 5.4 %collective-permute-done.29.recv = bf16[1,160,512]{2,1,0:T(8,128)(2,1)S(1)} collective-permute-done((bf16[1,160,512]{2,1,0:T(8,128)(2,1)S(1)}, bf16[1,160,512]{2,1,0:T(8,128)(2,1)S(1)}, u32[]{:S(2)}, u32[]{:S(2)}) %collective-permute-start.29) | collective-permute-done | bytes 163872 | tf_op jit(solution)/shard_map/ppermute | solution.py:430
  116.6 1.5 collective-permute-start.48
  120.0 1.6 collective-permute-start.23
  125.2 2.6 %collective-permute-start.49 = (bf16[1,80,1024]{2,1,0:T(8,128)(2,1)S(1)}, bf16[1,80,1024]{2,1,0:T(8,128)(2,1)S(1)}, u32[]{:S(2)}, u32[]{:S(2)}) collective-permute-start(bf16[1,80,1024]{2,1,0:T(8,128)(2,1)S(1)} %shard_map.305.keep_in), channel_id=1, source_target_pairs={{0,16},{4,20},{8,24},{12,28},{16,0},{20,4},{24,8},{28,12},{1,17},{... | collective-permute-start | bytes 491528 | tf_op jit(solution)/shard_map/ppermute | solution.py:430
  127.9 1.5 collective-permute-start.31
  129.4 1.6 collective-permute-start.24
  131.4 9.2 %collective-permute-done.31.recv = bf16[1,80,512]{2,1,0:T(8,128)(2,1)S(1)} collective-permute-done((bf16[1,80,512]{2,1,0:T(8,128)(2,1)S(1)}, bf16[1,80,512]{2,1,0:T(8,128)(2,1)S(1)}, u32[]{:S(2)}, u32[]{:S(2)}) %collective-permute-start.31) | collective-permute-done | bytes 81952 | tf_op jit(solution)/shard_map/ppermute | solution.py:430
  141.2 3.5 %collective-permute-start.43 = (bf16[1,80,1024]{2,1,0:T(8,128)(2,1)S(1)}, bf16[1,80,1024]{2,1,0:T(8,128)(2,1)S(1)}, u32[]{:S(2)}, u32[]{:S(2)}) collective-permute-start(bf16[1,80,1024]{2,1,0:T(8,128)(2,1)S(1)} %shard_map.300.keep_in), channel_id=1, source_target_pairs={{0,16},{4,20},{8,24},{12,28},{16,0},{20,4},{24,8},{28,12},{1,17},{... | collective-permute-start | bytes 491528 | tf_op jit(solution)/shard_map/ppermute | solution.py:430
  146.0 2.6 %collective-permute-start.20 = (bf16[640,256]{1,0:T(8,128)(2,1)S(1)}, bf16[640,256]{1,0:T(8,128)(2,1)S(1)}, u32[]{:S(2)}, u32[]{:S(2)}) collective-permute-start(bf16[640,256]{1,0:T(8,128)(2,1)S(1)} %pad_maximum_fusion.3), channel_id=1, source_target_pairs={{0,2},{3,1},{4,6},{7,5},{8,10},{11,9},{12,14},{15,13},{16,18},{19,... | collective-permute-start | bytes 983048 | tf_op jit(solution)/shard_map/ppermute | solution.py:461
  148.6 1.9 %collective-permute-start.25 = (bf16[1,80,896]{2,1,0:T(8,128)(2,1)S(1)}, bf16[1,80,896]{2,1,0:T(8,128)(2,1)S(1)}, u32[]{:S(2)}, u32[]{:S(2)}) collective-permute-start(bf16[1,80,896]{2,1,0:T(8,128)(2,1)S(1)} %shard_map.285), channel_id=1, source_target_pairs={{0,4},{4,0},{8,12},{12,8},{16,20},{20,16},{24,28},{28,24},{1,5},{5... | collective-permute-start | bytes 430088 | tf_op jit(solution)/shard_map/ppermute | solution.py:430
  150.6 4.2 %collective-permute-done.43.recv = bf16[1,80,1024]{2,1,0:T(8,128)(2,1)S(1)} collective-permute-done((bf16[1,80,1024]{2,1,0:T(8,128)(2,1)S(1)}, bf16[1,80,1024]{2,1,0:T(8,128)(2,1)S(1)}, u32[]{:S(2)}, u32[]{:S(2)}) %collective-permute-start.43) | collective-permute-done | bytes 163872 | tf_op jit(solution)/shard_map/ppermute | solution.py:430
  154.9 2.0 %collective-permute-done.37.recv = bf16[1,80,1024]{2,1,0:T(8,128)(2,1)S(1)} collective-permute-done((bf16[1,80,1024]{2,1,0:T(8,128)(2,1)S(1)}, bf16[1,80,1024]{2,1,0:T(8,128)(2,1)S(1)}, u32[]{:S(2)}, u32[]{:S(2)}) %collective-permute-start.37) | collective-permute-done | bytes 163872 | tf_op jit(solution)/shard_map/ppermute | solution.py:430
  157.7 1.5 collective-permute-start.51
  159.2 3.0 %collective-permute-done.44 = bf16[1,80,1024]{2,1,0:T(8,128)(2,1)S(1)} collective-permute-done((bf16[1,80,1024]{2,1,0:T(8,128)(2,1)S(1)}, bf16[1,80,1024]{2,1,0:T(8,128)(2,1)S(1)}, u32[]{:S(2)}, u32[]{:S(2)}) %collective-permute-start.44) | collective-permute-done | bytes 163872 | tf_op jit(solution)/shard_map/ppermute | solution.py:430
  162.3 3.1 %collective-permute-done.38 = bf16[1,80,1024]{2,1,0:T(8,128)(2,1)S(1)} collective-permute-done((bf16[1,80,1024]{2,1,0:T(8,128)(2,1)S(1)}, bf16[1,80,1024]{2,1,0:T(8,128)(2,1)S(1)}, u32[]{:S(2)}, u32[]{:S(2)}) %collective-permute-start.38) | collective-permute-done | bytes 163872 | tf_op jit(solution)/shard_map/ppermute | solution.py:430
  165.4 1.5 collective-permute-start.39
  168.3 3.6 %collective-permute-done.26.far = bf16[2,80,896]{2,1,0:T(8,128)(2,1)S(1)} collective-permute-done((bf16[2,80,896]{2,1,0:T(8,128)(2,1)S(1)}, bf16[2,80,896]{2,1,0:T(8,128)(2,1)S(1)}, u32[]{:S(2)}, u32[]{:S(2)}) %collective-permute-start.26) | collective-permute-done | bytes 286752 | tf_op jit(solution)/shard_map/ppermute | solution.py:430
  171.9 1.4 shard_map.286
  174.3 1.7 shard_map.307
  176.0 1.7 collective-permute-done.45.far
  177.6 1.7 shard_map.302
  179.3 1.7 shard_map.297
  181.0 1.5 shard_map.287
  (143 shorter events, 40.1 us)
Async XLA Ops:
  1.5 30.7 %collective-permute-start.3 = (f32[4,320]{1,0:T(4,128)S(1)}, f32[4,320]{1,0:T(4,128)S(1)}, u32[]{:S(2)}, u32[]{:S(2)}) collective-permute-start(f32[4,320]{1,0:T(4,128)S(1)} %select_select_fusion), channel_id=1, source_target_pairs={{0,2},{2,0},{1,3},{3,1},{4,6},{6,4},{5,7},{7,5},{8,10},{10,8},{9,1... | collective-permute-start | bytes 15368 | tf_op jit(solution)/shard_map/ppermute | solution.py:424
  6.6 33.8 %collective-permute-start.4 = (bf16[320,768]{1,0:T(8,128)(2,1)S(1)}, bf16[320,768]{1,0:T(8,128)(2,1)}, u32[]{:S(2)}, u32[]{:S(2)}) collective-permute-start(bf16[320,768]{1,0:T(8,128)(2,1)S(1)} %pad_maximum_fusion.w_own), channel_id=1, source_target_pairs={{0,2},{2,0},{1,3},{3,1},{4,6},{6,4},{5,7},{7,5},{8,10},{10,8},{9,1... | collective-permute-start | bytes 1474568 | tf_op jit(solution)/shard_map/ppermute | solution.py:424
  6.7 28.6 %collective-permute-start.1 = (f32[320,256]{1,0:T(8,128)}, f32[320,256]{1,0:T(8,128)}, u32[]{:S(2)}, u32[]{:S(2)}) collective-permute-start(f32[320,256]{1,0:T(8,128)} %bitcast.x_local), channel_id=1, source_target_pairs={{1,3},{2,0},{5,7},{6,4},{9,11},{10,8},{13,15},{14,12},{17,19},{18,... | collective-permute-start | bytes 983048 | tf_op jit(solution)/shard_map/ppermute | solution.py:455
  9.9 20.8 %collective-permute-start.8 = (bf16[80,1536]{1,0:T(8,128)(2,1)S(1)}, bf16[80,1536]{1,0:T(8,128)(2,1)S(1)}, u32[]{:S(2)}, u32[]{:S(2)}) collective-permute-start(bf16[80,1536]{1,0:T(8,128)(2,1)S(1)} %pad_maximum_fusion.8), channel_id=1, source_target_pairs={{0,2},{2,0},{1,3},{3,1},{4,6},{6,4},{5,7},{7,5},{8,10},{10,8},{9,1... | collective-permute-start | bytes 737288 | tf_op jit(solution)/shard_map/ppermute | solution.py:424
  14.1 19.5 %collective-permute-start.11 = (bf16[80,1536]{1,0:T(8,128)(2,1)}, bf16[80,1536]{1,0:T(8,128)(2,1)S(1)}, u32[]{:S(2)}, u32[]{:S(2)}) collective-permute-start(bf16[80,1536]{1,0:T(8,128)(2,1)} %pad_maximum_fusion.9), channel_id=1, source_target_pairs={{0,2},{2,0},{1,3},{3,1},{4,6},{6,4},{5,7},{7,5},{8,10},{10,8},{9,1... | collective-permute-start | bytes 737288 | tf_op jit(solution)/shard_map/ppermute | solution.py:424
  30.7 6.2 %collective-permute-start.9 = (bf16[80,1536]{1,0:T(8,128)(2,1)S(1)}, bf16[80,1536]{1,0:T(8,128)(2,1)S(1)}, u32[]{:S(2)}, u32[]{:S(2)}) collective-permute-start(bf16[80,1536]{1,0:T(8,128)(2,1)S(1)} %collective-permute-done.8.refs_2_.refs_1_.refs_3_), channel_id=1, source_target_pairs={{0,4},{4,0},{8,12},{12,8},{16,20},{20,16},{24,28},{28,24},{1,5},{5... | collective-permute-start | bytes 737288 | tf_op jit(solution)/shard_map/ppermute | solution.py:430
  32.3 6.6 %collective-permute-start = (f32[320,256]{1,0:T(8,128)}, f32[320,256]{1,0:T(8,128)S(1)}, u32[]{:S(2)}, u32[]{:S(2)}) collective-permute-start(f32[320,256]{1,0:T(8,128)} %bitcast.x_local), channel_id=1, source_target_pairs={{0,1},{3,2},{4,5},{7,6},{8,9},{11,10},{12,13},{15,14},{16,17},{19,... | collective-permute-start | bytes 983048 | tf_op jit(solution)/shard_map/ppermute | solution.py:458
  33.6 9.0 %collective-permute-start.12 = (bf16[80,1536]{1,0:T(8,128)(2,1)S(1)}, bf16[80,1536]{1,0:T(8,128)(2,1)S(1)}, u32[]{:S(2)}, u32[]{:S(2)}) collective-permute-start(bf16[80,1536]{1,0:T(8,128)(2,1)S(1)} %collective-permute-done.11.refs_5_.refs_4_.refs_6_), channel_id=1, source_target_pairs={{0,8},{4,12},{8,0},{12,4},{16,24},{20,28},{24,16},{28,20},{1,9},{5... | collective-permute-start | bytes 737288 | tf_op jit(solution)/shard_map/ppermute | solution.py:430
  35.2 5.2 %collective-permute-start.2 = (f32[320,256]{1,0:T(8,128)}, f32[320,256]{1,0:T(8,128)S(1)}, u32[]{:S(2)}, u32[]{:S(2)}) collective-permute-start(f32[320,256]{1,0:T(8,128)} %collective-permute-done.1.x_diag), channel_id=1, source_target_pairs={{0,1},{3,2},{4,5},{7,6},{8,9},{11,10},{12,13},{15,14},{16,17},{19,... | collective-permute-start | bytes 983048 | tf_op jit(solution)/shard_map/ppermute | solution.py:458
  36.9 9.5 %collective-permute-start.6 = (bf16[320,512]{1,0:T(8,128)(2,1)S(1)}, bf16[320,512]{1,0:T(8,128)(2,1)S(1)}, u32[]{:S(2)}, u32[]{:S(2)}) collective-permute-start(bf16[320,512]{1,0:T(8,128)(2,1)S(1)} %bitcast.19), channel_id=1, source_target_pairs={{0,2},{2,0},{1,3},{3,1},{4,6},{6,4},{5,7},{7,5},{8,10},{10,8},{9,1... | collective-permute-start | bytes 983048 | tf_op jit(solution)/shard_map/ppermute | solution.py:424
  38.9 12.7 %collective-permute-start.10 = (bf16[160,1536]{1,0:T(8,128)(2,1)S(1)}, bf16[160,1536]{1,0:T(8,128)(2,1)S(1)}, u32[]{:S(2)}, u32[]{:S(2)}) collective-permute-start(bf16[160,1536]{1,0:T(8,128)(2,1)S(1)} %pad_maximum_fusion.1), channel_id=1, source_target_pairs={{0,8},{4,12},{8,0},{12,4},{16,24},{20,28},{24,16},{28,20},{1,9},{5... | collective-permute-start | bytes 1474568 | tf_op jit(solution)/shard_map/ppermute | solution.py:430
  42.5 3.9 %collective-permute-start.5 = (f32[256,256]{1,0:T(8,128)S(1)}, f32[256,256]{1,0:T(8,128)S(1)}, u32[]{:S(2)}, u32[]{:S(2)}) collective-permute-start(f32[256,256]{1,0:T(8,128)S(1)} %get-tuple-element.88.kv_mine.kv_raw), channel_id=1, source_target_pairs={{0,1},{1,0},{2,3},{3,2},{4,5},{5,4},{6,7},{7,6},{8,9},{9,8},{10,11... | collective-permute-start | bytes 786440 | tf_op jit(solution)/shard_map/ppermute | solution.py:427
  42.6 13.7 %collective-permute-start.13 = (bf16[160,1536]{1,0:T(8,128)(2,1)S(1)}, bf16[160,1536]{1,0:T(8,128)(2,1)S(1)}, u32[]{:S(2)}, u32[]{:S(2)}) collective-permute-start(bf16[160,1536]{1,0:T(8,128)(2,1)S(1)} %pad_maximum_fusion.2), channel_id=1, source_target_pairs={{0,4},{4,0},{8,12},{12,8},{16,20},{20,16},{24,28},{28,24},{1,5},{5... | collective-permute-start | bytes 1474568 | tf_op jit(solution)/shard_map/ppermute | solution.py:430
  48.0 8.3 %collective-permute-start.7 = (bf16[256,640]{1,0:T(8,128)(2,1)S(1)}, bf16[256,640]{1,0:T(8,128)(2,1)S(1)}, u32[]{:S(2)}, u32[]{:S(2)}) collective-permute-start(bf16[256,640]{1,0:T(8,128)(2,1)S(1)} %get-tuple-element.90), channel_id=1, source_target_pairs={{0,1},{1,0},{2,3},{3,2},{4,5},{5,4},{6,7},{7,6},{8,9},{9,8},{10,11... | collective-permute-start | bytes 983048 | tf_op jit(solution)/shard_map/ppermute | solution.py:427
  48.2 10.1 %collective-permute-start.15 = (bf16[320,256]{1,0:T(8,128)(2,1)S(1)}, bf16[320,256]{1,0:T(8,128)(2,1)S(1)}, u32[]{:S(2)}, u32[]{:S(2)}) collective-permute-start(bf16[320,256]{1,0:T(8,128)(2,1)S(1)} %bitcast_convert_fusion.own), channel_id=1, source_target_pairs={{1,3},{2,0},{5,7},{6,4},{9,11},{10,8},{13,15},{14,12},{17,19},{18,... | collective-permute-start | bytes 491528 | tf_op jit(solution)/shard_map/ppermute | solution.py:455
  73.0 17.6 %collective-permute-start.46 = (bf16[1,320,1024]{2,1,0:T(8,128)(2,1)S(1)}, bf16[1,320,1024]{2,1,0:T(8,128)(2,1)S(1)}, u32[]{:S(2)}, u32[]{:S(2)}) collective-permute-start(bf16[1,320,1024]{2,1,0:T(8,128)(2,1)S(1)} %get-tuple-element.151), channel_id=1, source_target_pairs={{0,2},{2,0},{1,3},{3,1},{4,6},{6,4},{5,7},{7,5},{8,10},{10,8},{9,1... | collective-permute-start | bytes 1966088 | tf_op jit(solution)/shard_map/ppermute | solution.py:424
  74.0 18.0 %collective-permute-start.40 = (bf16[2,160,1024]{2,1,0:T(8,128)(2,1)S(1)}, bf16[2,160,1024]{2,1,0:T(8,128)(2,1)S(1)}, u32[]{:S(2)}, u32[]{:S(2)}) collective-permute-start(bf16[2,160,1024]{2,1,0:T(8,128)(2,1)S(1)} %get-tuple-element.145), channel_id=1, source_target_pairs={{0,4},{4,0},{8,12},{12,8},{16,20},{20,16},{24,28},{28,24},{1,5},{5... | collective-permute-start | bytes 1966088 | tf_op jit(solution)/shard_map/ppermute | solution.py:430
  75.5 28.7 %collective-permute-start.34 = (bf16[2,160,1024]{2,1,0:T(8,128)(2,1)S(1)}, bf16[2,160,1024]{2,1,0:T(8,128)(2,1)S(1)}, u32[]{:S(2)}, u32[]{:S(2)}) collective-permute-start(bf16[2,160,1024]{2,1,0:T(8,128)(2,1)S(1)} %get-tuple-element.139), channel_id=1, source_target_pairs={{0,8},{4,12},{8,0},{12,4},{16,24},{20,28},{24,16},{28,20},{1,9},{5... | collective-permute-start | bytes 1966088 | tf_op jit(solution)/shard_map/ppermute | solution.py:430
  78.0 24.9 %collective-permute-start.21 = (bf16[1,320,896]{2,1,0:T(8,128)(2,1)S(1)}, bf16[1,320,896]{2,1,0:T(8,128)(2,1)S(1)}, u32[]{:S(2)}, u32[]{:S(2)}) collective-permute-start(bf16[1,320,896]{2,1,0:T(8,128)(2,1)S(1)} %get-tuple-element.123), channel_id=1, source_target_pairs={{0,2},{2,0},{1,3},{3,1},{4,6},{6,4},{5,7},{7,5},{8,10},{10,8},{9,1... | collective-permute-start | bytes 1720328 | tf_op jit(solution)/shard_map/ppermute | solution.py:424
  79.1 30.2 %collective-permute-start.28 = (bf16[1,320,512]{2,1,0:T(8,128)(2,1)S(1)}, bf16[1,320,512]{2,1,0:T(8,128)(2,1)S(1)}, u32[]{:S(2)}, u32[]{:S(2)}) collective-permute-start(bf16[1,320,512]{2,1,0:T(8,128)(2,1)S(1)} %get-tuple-element.133), channel_id=1, source_target_pairs={{0,2},{2,0},{1,3},{3,1},{4,6},{6,4},{5,7},{7,5},{8,10},{10,8},{9,1... | collective-permute-start | bytes 983048 | tf_op jit(solution)/shard_map/ppermute | solution.py:424
  91.4 19.2 %collective-permute-start.47 = (bf16[1,160,1024]{2,1,0:T(8,128)(2,1)S(1)}, bf16[1,160,1024]{2,1,0:T(8,128)(2,1)S(1)}, u32[]{:S(2)}, u32[]{:S(2)}) collective-permute-start(bf16[1,160,1024]{2,1,0:T(8,128)(2,1)S(1)} %get-tuple-element.153), channel_id=1, source_target_pairs={{0,8},{4,12},{8,0},{12,4},{16,24},{20,28},{24,16},{28,20},{1,9},{5... | collective-permute-start | bytes 983048 | tf_op jit(solution)/shard_map/ppermute | solution.py:430
  92.7 27.2 %collective-permute-start.41 = (bf16[2,80,1024]{2,1,0:T(8,128)(2,1)S(1)}, bf16[2,80,1024]{2,1,0:T(8,128)(2,1)S(1)}, u32[]{:S(2)}, u32[]{:S(2)}) collective-permute-start(bf16[2,80,1024]{2,1,0:T(8,128)(2,1)S(1)} %get-tuple-element.147), channel_id=1, source_target_pairs={{0,8},{4,12},{8,0},{12,4},{16,24},{20,28},{24,16},{28,20},{1,9},{5... | collective-permute-start | bytes 983048 | tf_op jit(solution)/shard_map/ppermute | solution.py:430
  103.6 15.1 %collective-permute-start.22 = (bf16[1,160,896]{2,1,0:T(8,128)(2,1)S(1)}, bf16[1,160,896]{2,1,0:T(8,128)(2,1)S(1)}, u32[]{:S(2)}, u32[]{:S(2)}) collective-permute-start(bf16[1,160,896]{2,1,0:T(8,128)(2,1)S(1)} %get-tuple-element.125), channel_id=1, source_target_pairs={{0,8},{4,12},{8,0},{12,4},{16,24},{20,28},{24,16},{28,20},{1,9},{5... | collective-permute-start | bytes 860168 | tf_op jit(solution)/shard_map/ppermute | solution.py:430
  105.0 17.1 %collective-permute-start.35 = (bf16[2,80,1024]{2,1,0:T(8,128)(2,1)S(1)}, bf16[2,80,1024]{2,1,0:T(8,128)(2,1)S(1)}, u32[]{:S(2)}, u32[]{:S(2)}) collective-permute-start(bf16[2,80,1024]{2,1,0:T(8,128)(2,1)S(1)} %get-tuple-element.141), channel_id=1, source_target_pairs={{0,4},{4,0},{8,12},{12,8},{16,20},{20,16},{24,28},{28,24},{1,5},{5... | collective-permute-start | bytes 983048 | tf_op jit(solution)/shard_map/ppermute | solution.py:430
  110.0 6.7 %collective-permute-start.29 = (bf16[1,160,512]{2,1,0:T(8,128)(2,1)S(1)}, bf16[1,160,512]{2,1,0:T(8,128)(2,1)S(1)}, u32[]{:S(2)}, u32[]{:S(2)}) collective-permute-start(bf16[1,160,512]{2,1,0:T(8,128)(2,1)S(1)} %get-tuple-element.135), channel_id=1, source_target_pairs={{0,8},{4,12},{8,0},{12,4},{16,24},{20,28},{24,16},{28,20},{1,9},{5... | collective-permute-start | bytes 491528 | tf_op jit(solution)/shard_map/ppermute | solution.py:430
  110.6 18.8 %collective-permute-start.19 = (bf16[256,640]{1,0:T(8,128)(2,1)S(1)}, bf16[256,640]{1,0:T(8,128)(2,1)S(1)}, u32[]{:S(2)}, u32[]{:S(2)}) collective-permute-start(bf16[256,640]{1,0:T(8,128)(2,1)S(1)} %get-tuple-element.118), channel_id=1, source_target_pairs={{0,1},{1,0},{2,3},{3,2},{4,5},{5,4},{6,7},{7,6},{8,9},{9,8},{10,11... | collective-permute-start | bytes 983048 | tf_op jit(solution)/shard_map/ppermute | solution.py:427
  116.6 7.0 %collective-permute-start.48 = (bf16[1,80,1024]{2,1,0:T(8,128)(2,1)S(1)}, bf16[1,80,1024]{2,1,0:T(8,128)(2,1)S(1)}, u32[]{:S(2)}, u32[]{:S(2)}) collective-permute-start(bf16[1,80,1024]{2,1,0:T(8,128)(2,1)S(1)} %get-tuple-element.155), channel_id=1, source_target_pairs={{0,4},{4,0},{8,12},{12,8},{16,20},{20,16},{24,28},{28,24},{1,5},{5... | collective-permute-start | bytes 491528 | tf_op jit(solution)/shard_map/ppermute | solution.py:430
  118.7 6.5 %collective-permute-start.30 = (bf16[1,80,512]{2,1,0:T(8,128)(2,1)S(1)}, bf16[1,80,512]{2,1,0:T(8,128)(2,1)S(1)}, u32[]{:S(2)}, u32[]{:S(2)}) collective-permute-start(bf16[1,80,512]{2,1,0:T(8,128)(2,1)S(1)} %get-tuple-element.137), channel_id=1, source_target_pairs={{0,4},{4,0},{8,12},{12,8},{16,20},{20,16},{24,28},{28,24},{1,5},{5... | collective-permute-start | bytes 245768 | tf_op jit(solution)/shard_map/ppermute | solution.py:430
  120.0 7.9 %collective-permute-start.23 = (bf16[1,80,896]{2,1,0:T(8,128)(2,1)S(1)}, bf16[1,80,896]{2,1,0:T(8,128)(2,1)S(1)}, u32[]{:S(2)}, u32[]{:S(2)}) collective-permute-start(bf16[1,80,896]{2,1,0:T(8,128)(2,1)S(1)} %get-tuple-element.127), channel_id=1, source_target_pairs={{0,4},{4,0},{8,12},{12,8},{16,20},{20,16},{24,28},{28,24},{1,5},{5... | collective-permute-start | bytes 430088 | tf_op jit(solution)/shard_map/ppermute | solution.py:430
  122.2 19.0 %collective-permute-start.42 = (bf16[1,80,1024]{2,1,0:T(8,128)(2,1)S(1)}, bf16[1,80,1024]{2,1,0:T(8,128)(2,1)S(1)}, u32[]{:S(2)}, u32[]{:S(2)}) collective-permute-start(bf16[1,80,1024]{2,1,0:T(8,128)(2,1)S(1)} %get-tuple-element.149), channel_id=1, source_target_pairs={{0,2},{2,0},{1,3},{3,1},{4,6},{6,4},{5,7},{7,5},{8,10},{10,8},{9,1... | collective-permute-start | bytes 491528 | tf_op jit(solution)/shard_map/ppermute | solution.py:424
  123.7 21.0 %collective-permute-start.36 = (bf16[1,80,1024]{2,1,0:T(8,128)(2,1)S(1)}, bf16[1,80,1024]{2,1,0:T(8,128)(2,1)S(1)}, u32[]{:S(2)}, u32[]{:S(2)}) collective-permute-start(bf16[1,80,1024]{2,1,0:T(8,128)(2,1)S(1)} %get-tuple-element.143), channel_id=1, source_target_pairs={{0,2},{2,0},{1,3},{3,1},{4,6},{6,4},{5,7},{7,5},{8,10},{10,8},{9,1... | collective-permute-start | bytes 491528 | tf_op jit(solution)/shard_map/ppermute | solution.py:424
  125.2 19.6 %collective-permute-start.49 = (bf16[1,80,1024]{2,1,0:T(8,128)(2,1)S(1)}, bf16[1,80,1024]{2,1,0:T(8,128)(2,1)S(1)}, u32[]{:S(2)}, u32[]{:S(2)}) collective-permute-start(bf16[1,80,1024]{2,1,0:T(8,128)(2,1)S(1)} %shard_map.305.keep_in), channel_id=1, source_target_pairs={{0,16},{4,20},{8,24},{12,28},{16,0},{20,4},{24,8},{28,12},{1,17},{... | collective-permute-start | bytes 491528 | tf_op jit(solution)/shard_map/ppermute | solution.py:430
  127.9 12.7 %collective-permute-start.31 = (bf16[1,80,512]{2,1,0:T(8,128)(2,1)S(1)}, bf16[1,80,512]{2,1,0:T(8,128)(2,1)S(1)}, u32[]{:S(2)}, u32[]{:S(2)}) collective-permute-start(bf16[1,80,512]{2,1,0:T(8,128)(2,1)S(1)} %shard_map.290.keep_in), channel_id=1, source_target_pairs={{0,16},{4,20},{8,24},{12,28},{16,0},{20,4},{24,8},{28,12},{1,17},{... | collective-permute-start | bytes 245768 | tf_op jit(solution)/shard_map/ppermute | solution.py:430
  129.4 16.6 %collective-permute-start.24 = (bf16[1,80,896]{2,1,0:T(8,128)(2,1)S(1)}, bf16[1,80,896]{2,1,0:T(8,128)(2,1)S(1)}, u32[]{:S(2)}, u32[]{:S(2)}) collective-permute-start(bf16[1,80,896]{2,1,0:T(8,128)(2,1)S(1)} %shard_map.284.keep_in), channel_id=1, source_target_pairs={{0,16},{4,20},{8,24},{12,28},{16,0},{20,4},{24,8},{28,12},{1,17},{... | collective-permute-start | bytes 430088 | tf_op jit(solution)/shard_map/ppermute | solution.py:430
  140.6 8.0 %collective-permute-start.32 = (bf16[1,80,512]{2,1,0:T(8,128)(2,1)S(1)}, bf16[1,80,512]{2,1,0:T(8,128)(2,1)S(1)}, u32[]{:S(2)}, u32[]{:S(2)}) collective-permute-start(bf16[1,80,512]{2,1,0:T(8,128)(2,1)S(1)} %shard_map.291), channel_id=1, source_target_pairs={{0,8},{4,12},{8,0},{12,4},{16,24},{20,28},{24,16},{28,20},{1,9},{5... | collective-permute-start | bytes 245768 | tf_op jit(solution)/shard_map/ppermute | solution.py:430
  141.2 13.6 %collective-permute-start.43 = (bf16[1,80,1024]{2,1,0:T(8,128)(2,1)S(1)}, bf16[1,80,1024]{2,1,0:T(8,128)(2,1)S(1)}, u32[]{:S(2)}, u32[]{:S(2)}) collective-permute-start(bf16[1,80,1024]{2,1,0:T(8,128)(2,1)S(1)} %shard_map.300.keep_in), channel_id=1, source_target_pairs={{0,16},{4,20},{8,24},{12,28},{16,0},{20,4},{24,8},{28,12},{1,17},{... | collective-permute-start | bytes 491528 | tf_op jit(solution)/shard_map/ppermute | solution.py:430
  144.7 12.2 %collective-permute-start.37 = (bf16[1,80,1024]{2,1,0:T(8,128)(2,1)S(1)}, bf16[1,80,1024]{2,1,0:T(8,128)(2,1)S(1)}, u32[]{:S(2)}, u32[]{:S(2)}) collective-permute-start(bf16[1,80,1024]{2,1,0:T(8,128)(2,1)S(1)} %shard_map.295.keep_in), channel_id=1, source_target_pairs={{0,16},{4,20},{8,24},{12,28},{16,0},{20,4},{24,8},{28,12},{1,17},{... | collective-permute-start | bytes 491528 | tf_op jit(solution)/shard_map/ppermute | solution.py:430
  144.8 12.1 %collective-permute-start.50 = (bf16[1,80,1024]{2,1,0:T(8,128)(2,1)S(1)}, bf16[1,80,1024]{2,1,0:T(8,128)(2,1)S(1)}, u32[]{:S(2)}, u32[]{:S(2)}) collective-permute-start(bf16[1,80,1024]{2,1,0:T(8,128)(2,1)S(1)} %shard_map.306), channel_id=1, source_target_pairs={{0,8},{4,12},{8,0},{12,4},{16,24},{20,28},{24,16},{28,20},{1,9},{5... | collective-permute-start | bytes 491528 | tf_op jit(solution)/shard_map/ppermute | solution.py:430
  146.0 22.3 %collective-permute-start.20 = (bf16[640,256]{1,0:T(8,128)(2,1)S(1)}, bf16[640,256]{1,0:T(8,128)(2,1)S(1)}, u32[]{:S(2)}, u32[]{:S(2)}) collective-permute-start(bf16[640,256]{1,0:T(8,128)(2,1)S(1)} %pad_maximum_fusion.3), channel_id=1, source_target_pairs={{0,2},{3,1},{4,6},{7,5},{8,10},{11,9},{12,14},{15,13},{16,18},{19,... | collective-permute-start | bytes 983048 | tf_op jit(solution)/shard_map/ppermute | solution.py:461
  148.6 9.0 %collective-permute-start.25 = (bf16[1,80,896]{2,1,0:T(8,128)(2,1)S(1)}, bf16[1,80,896]{2,1,0:T(8,128)(2,1)S(1)}, u32[]{:S(2)}, u32[]{:S(2)}) collective-permute-start(bf16[1,80,896]{2,1,0:T(8,128)(2,1)S(1)} %shard_map.285), channel_id=1, source_target_pairs={{0,4},{4,0},{8,12},{12,8},{16,20},{20,16},{24,28},{28,24},{1,5},{5... | collective-permute-start | bytes 430088 | tf_op jit(solution)/shard_map/ppermute | solution.py:430
  154.8 10.6 %collective-permute-start.33 = (bf16[2,80,512]{2,1,0:T(8,128)(2,1)S(1)}, bf16[2,80,512]{2,1,0:T(8,128)(2,1)S(1)}, u32[]{:S(2)}, u32[]{:S(2)}) collective-permute-start(bf16[2,80,512]{2,1,0:T(8,128)(2,1)S(1)} %pad_maximum_fusion.10.near), channel_id=1, source_target_pairs={{0,4},{4,0},{8,12},{12,8},{16,20},{20,16},{24,28},{28,24},{1,5},{5... | collective-permute-start | bytes 491528 | tf_op jit(solution)/shard_map/ppermute | solution.py:430
  156.9 5.3 %collective-permute-start.44 = (bf16[1,80,1024]{2,1,0:T(8,128)(2,1)S(1)}, bf16[1,80,1024]{2,1,0:T(8,128)(2,1)S(1)}, u32[]{:S(2)}, u32[]{:S(2)}) collective-permute-start(bf16[1,80,1024]{2,1,0:T(8,128)(2,1)S(1)} %shard_map.301), channel_id=1, source_target_pairs={{0,8},{4,12},{8,0},{12,4},{16,24},{20,28},{24,16},{28,20},{1,9},{5... | collective-permute-start | bytes 491528 | tf_op jit(solution)/shard_map/ppermute | solution.py:430
  157.0 8.4 %collective-permute-start.38 = (bf16[1,80,1024]{2,1,0:T(8,128)(2,1)S(1)}, bf16[1,80,1024]{2,1,0:T(8,128)(2,1)S(1)}, u32[]{:S(2)}, u32[]{:S(2)}) collective-permute-start(bf16[1,80,1024]{2,1,0:T(8,128)(2,1)S(1)} %shard_map.296), channel_id=1, source_target_pairs={{0,4},{4,0},{8,12},{12,8},{16,20},{20,16},{24,28},{28,24},{1,5},{5... | collective-permute-start | bytes 491528 | tf_op jit(solution)/shard_map/ppermute | solution.py:430
  157.7 16.6 %collective-permute-start.51 = (bf16[2,80,1024]{2,1,0:T(8,128)(2,1)S(1)}, bf16[2,80,1024]{2,1,0:T(8,128)(2,1)S(1)}, u32[]{:S(2)}, u32[]{:S(2)}) collective-permute-start(bf16[2,80,1024]{2,1,0:T(8,128)(2,1)S(1)} %pad_maximum_fusion.6.near), channel_id=1, source_target_pairs={{0,4},{4,0},{8,12},{12,8},{16,20},{20,16},{24,28},{28,24},{1,5},{5... | collective-permute-start | bytes 983048 | tf_op jit(solution)/shard_map/ppermute | solution.py:430
  162.2 9.7 %collective-permute-start.26 = (bf16[2,80,896]{2,1,0:T(8,128)(2,1)S(1)}, bf16[2,80,896]{2,1,0:T(8,128)(2,1)S(1)}, u32[]{:S(2)}, u32[]{:S(2)}) collective-permute-start(bf16[2,80,896]{2,1,0:T(8,128)(2,1)S(1)} %pad_maximum_fusion.7.near), channel_id=1, source_target_pairs={{0,8},{4,12},{8,0},{12,4},{16,24},{20,28},{24,16},{28,20},{1,9},{5... | collective-permute-start | bytes 860168 | tf_op jit(solution)/shard_map/ppermute | solution.py:430
  165.3 12.3 %collective-permute-start.45 = (bf16[2,80,1024]{2,1,0:T(8,128)(2,1)S(1)}, bf16[2,80,1024]{2,1,0:T(8,128)(2,1)S(1)}, u32[]{:S(2)}, u32[]{:S(2)}) collective-permute-start(bf16[2,80,1024]{2,1,0:T(8,128)(2,1)S(1)} %pad_maximum_fusion.5.near), channel_id=1, source_target_pairs={{0,4},{4,0},{8,12},{12,8},{16,20},{20,16},{24,28},{28,24},{1,5},{5... | collective-permute-start | bytes 983048 | tf_op jit(solution)/shard_map/ppermute | solution.py:430
  165.4 14.0 %collective-permute-start.39 = (bf16[2,80,1024]{2,1,0:T(8,128)(2,1)S(1)}, bf16[2,80,1024]{2,1,0:T(8,128)(2,1)S(1)}, u32[]{:S(2)}, u32[]{:S(2)}) collective-permute-start(bf16[2,80,1024]{2,1,0:T(8,128)(2,1)S(1)} %pad_maximum_fusion.4.near), channel_id=1, source_target_pairs={{0,8},{4,12},{8,0},{12,4},{16,24},{20,28},{24,16},{28,20},{1,9},{5... | collective-permute-start | bytes 983048 | tf_op jit(solution)/shard_map/ppermute | solution.py:430
  173.4 7.7 %collective-permute-start.27 = (bf16[320,384]{1,0:T(8,128)(2,1)S(1)}, bf16[320,384]{1,0:T(8,128)(2,1)S(1)}, u32[]{:S(2)}, u32[]{:S(2)}) collective-permute-start(bf16[320,384]{1,0:T(8,128)(2,1)S(1)} %get-tuple-element.129.own), channel_id=1, source_target_pairs={{0,1},{1,0},{2,3},{3,2},{4,5},{5,4},{6,7},{7,6},{8,9},{9,8},{10,11... | collective-permute-start | bytes 737288 | tf_op jit(solution)/shard_map/ppermute | solution.py:427
  (13 other events, 89.8 us)
